TPU v7x, 512 devices: a whole 4x4x16 slice. The times are simulated.
512 devices in a mesh: ctx: 128 (over z, x_hi, y), fsdp: 4 (over x_lo, core).
Axes of the slice: x: 4 (x_hi: 2, x_lo: 2; x = x_hi * 2 + x_lo), y: 4, z: 16, core: 2. Of those that a mesh axis runs over, the one named last changes fastest.
Arguments:
- normed: bfloat16 [2, 4, 16384, 1024], P(None, 'fsdp', 'ctx'), may hold values from -6 to 6
- out_grad: bfloat16 [2, 4, 16384, 1024], P(None, 'fsdp', 'ctx'), may hold values from -6 to 6
- ids: int32 [2, 4, 16384], P(None, 'fsdp', 'ctx'), may hold values from 0 to 4, as said below
- mask: int32 [2, 4, 16384], P(None, 'fsdp', 'ctx'), may hold values 0 or 1
- proj_half: bfloat16 [512, 1024], P('fsdp'), may hold values from -0.1875 to 0.1875
- conv_filter: float32 [7, 1024], replicated, may hold values from -2.5 to 2.5
- gate_bias: float32 [6, 1024], replicated, may hold values from -6 to 6
Outputs:
- in_grad: bfloat16 [2, 4, 16384, 1024], P(None, 'fsdp', 'ctx')
- proj_grad: float32 [128, 512, 1024], P('ctx', 'fsdp')
- filter_grad: float32 [128, 7, 1024], P('ctx', None, 'fsdp')
- bias_grad: float32 [128, 6, 1024], P('ctx', None, 'fsdp')
Inputs may be any that keep to these rules, and one draw needn't show every extreme that they name: Codes A=0, C=1, G=2, T=3, N=4. ids[1] is the reverse complement of ids[0] in its own coordinates: ids[1, b, p] = 3 - ids[0, b, 16383 - p] where that code is below 4, and 4 where it is 4. Every sequence holds at least one 4.
All inputs are finite; a program needn't handle non-finite values. No bound on the sum of `mask` on one device may be relied on, other than what follows from the above.
Results may differ from a plain program's by a relative error of at most 0.007.
Values may be sent and summed in bfloat16 or wider, within the bound.
No kernel may reach another device: no remote copies, remote signals or barrier semaphores. Data moves between devices by JAX's collectives and lax.ppermute only.
A program may use at most 64 MiB of HBM per device.

v0:
```python
import math

import jax
import jax.numpy as jnp
from jax import lax
from jax.sharding import PartitionSpec as P


def from_partner(value, axis, stride):
    mask = 2**stride
    pairs = [(source, source ^ mask) for source in range(lax.axis_size(axis))]
    return lax.ppermute(value, axis, pairs)


def shifted_2(block, axis, distance):
    devices = range(lax.axis_size(axis))
    route = [(i - distance, i) for i in devices if i - distance in devices]
    return lax.ppermute(block, axis, route)


def mirror_slab(slab_in):
    depth_count = lax.axis_size("ctx").bit_length() - 1
    bit_order = list(range(depth_count))
    arrived = slab_in
    for bit_number in bit_order:
        arrived = from_partner(arrived, "ctx", bit_number)
    return jnp.flip(arrived, axis=(0, 2, 3))


def project(rows_in, weight_full):
    return jnp.dot(rows_in, weight_full, preferred_element_type=jnp.float32)


def shards(normed, out_grad, ids, mask, proj_half, conv_filter, gate_bias):
    seq_local = normed.shape[1]
    row_count = normed.shape[2]
    feature_width = normed.shape[3]
    tap_count = conv_filter.shape[0]
    rim_rows = tap_count - 1
    half_rows = lax.all_gather(proj_half, "fsdp", axis=0, tiled=True)
    weight_full = jnp.concatenate([half_rows, jnp.flip(half_rows, axis=(0, 1))], axis=0)
    flat_in = normed.reshape(-1, feature_width)
    values = project(flat_in, weight_full).astype(jnp.bfloat16).reshape(normed.shape)
    mirrored = mirror_slab(values)
    before = shifted_2(values[:, :, row_count - rim_rows :, :], "ctx", 1)
    extended = jnp.concatenate([before, values], axis=2)
    conv_out = jnp.zeros(normed.shape, jnp.float32)
    for tap_index in range(tap_count):
        start_row = rim_rows - tap_index
        conv_out = conv_out + conv_filter[tap_index] * extended[
            :, :, start_row : start_row + row_count, :
        ].astype(jnp.float32)
    tokens = jnp.where(mask == 1, 5, ids)
    classes = lax.broadcasted_iota(jnp.int32, (1, 6), 1)
    one_hot = (tokens.reshape(-1, 1) == classes).astype(jnp.float32)
    bias_rows = jnp.dot(one_hot, gate_bias, precision=lax.Precision.HIGHEST).reshape(normed.shape)
    gate = jax.nn.sigmoid(mirrored.astype(jnp.float32) + bias_rows)
    cotangent = out_grad.astype(jnp.float32)
    conv_grad = cotangent * gate
    gate_pre = cotangent * conv_out * gate * (1.0 - gate)
    mirror_grad = gate_pre.astype(jnp.bfloat16)
    following = shifted_2(conv_grad[:, :, :rim_rows, :], "ctx", -1)
    grad_ext = jnp.concatenate([conv_grad, following], axis=2)
    returned = mirror_slab(mirror_grad)
    value_grad = returned.astype(jnp.float32)
    for tap_index in range(tap_count):
        value_grad = (
            value_grad
            + conv_filter[tap_index] * grad_ext[:, :, tap_index : tap_index + row_count, :]
        )
    value_grad = value_grad.astype(jnp.bfloat16)
    flat_grad = value_grad.reshape(-1, feature_width)
    in_grad = lax.dot_general(
        flat_grad, weight_full, (((1,), (1,)), ((), ())), preferred_element_type=jnp.float32
    )
    in_grad = in_grad.astype(jnp.bfloat16).reshape(normed.shape)
    half_width = feature_width // 2
    lower_in = flat_in[:, :half_width]
    upper_in = jnp.flip(flat_in[:, half_width:], axis=1)
    proj_term = lax.dot_general(
        lower_in, flat_grad, (((0,), (0,)), ((), ())), preferred_element_type=jnp.float32
    )
    proj_term = proj_term + lax.dot_general(
        upper_in,
        jnp.flip(flat_grad, axis=1),
        (((0,), (0,)), ((), ())),
        preferred_element_type=jnp.float32,
    )
    filter_terms = []
    for tap_index in range(tap_count):
        start_row = rim_rows - tap_index
        shifted = extended[:, :, start_row : start_row + row_count, :].astype(jnp.float32)
        filter_terms.append(jnp.sum(conv_grad * shifted, axis=(0, 1, 2)))
    filter_term = jnp.stack(filter_terms, axis=0)
    bias_term = lax.dot_general(
        one_hot,
        gate_pre.reshape(-1, feature_width),
        (((0,), (0,)), ((), ())),
        precision=lax.Precision.HIGHEST,
    )
    grad_scale = 1.0 / math.sqrt(2.0 * seq_local * lax.axis_size("fsdp") * row_count)
    proj_sum, filter_sum, bias_sum = (
        lax.psum_scatter(proj_term * grad_scale, "fsdp", scatter_dimension=0, tiled=True),
        lax.psum_scatter(filter_term * grad_scale, "fsdp", scatter_dimension=1, tiled=True),
        lax.psum_scatter(bias_term * grad_scale, "fsdp", scatter_dimension=1, tiled=True),
    )
    return (in_grad, proj_sum[None], filter_sum[None], bias_sum[None])


def solution(mesh):
    placed = (
        P(None, "fsdp", "ctx", None),
        P(None, "fsdp", "ctx", None),
        P(None, "fsdp", "ctx"),
        P(None, "fsdp", "ctx"),
        P("fsdp", None),
        P(),
        P(),
    )
    return jax.shard_map(
        shards,
        mesh=mesh,
        in_specs=placed,
        out_specs=(
            P(None, "fsdp", "ctx", None),
            P("ctx", "fsdp", None),
            P("ctx", None, "fsdp"),
            P("ctx", None, "fsdp"),
        ),
        check_vma=False,
    )
```

profile of v0, /device:TPU:1, one launch (start us, length us, event | category | flops | bytes accessed | tf_op | source)
XLA Modules:
  0.0 517.9 jit_solution(6132048127253158461)
XLA Ops:
  7.2 0.0 all-gather.2.cloned.1.call-start
  7.2 0.7 all-gather.2.cloned.1.call-update
  7.9 0.0 reduce-scatter.8.cloned.1.call-start
  8.0 36.2 %all-gather.2.cloned.1.call-done = bf16[512,1024]{1,0:T(8,128)(2,1)} async-done(((bf16[128,1024]{1,0:T(8,128)(2,1)}), bf16[512,1024]{1,0:T(8,128)(2,1)}) %all-gather.2.cloned.1.call-update) | async-done | bytes 1048592 | tf_op jit(solution)/shard_map/all_gather | solution.py:40
  44.2 14.0 %rev.19 = bf16[512,1024]{1,0:T(8,128)(2,1)S(1)} reverse(bf16[512,1024]{1,0:T(8,128)(2,1)} %all-gather.2.cloned.1.call-done), dimensions={0,1} | reverse | bytes 2097152 | tf_op jit(solution)/shard_map/jit(_flip)/rev | solution.py:41
  58.2 0.7 fusion.2
  58.9 0.2 copy-done.5
  59.1 3.1 collective-permute-start.1
  62.2 12.4 %collective-permute-done.1 = bf16[2,1,128,1024]{3,2,1,0:T(8,128)(2,1)S(1)} collective-permute-done((bf16[2,1,128,1024]{3,2,1,0:T(8,128)(2,1)S(1)}, bf16[2,1,128,1024]{3,2,1,0:T(8,128)(2,1)S(1)}, u32[]{:S(2)}, u32[]{:S(2)}) %collective-permute-start.1) | collective-permute-done | bytes 524320 | tf_op jit(solution)/shard_map/ppermute | solution.py:12
  74.7 4.6 collective-permute-start.2
  79.3 11.6 %collective-permute-done.2 = bf16[2,1,128,1024]{3,2,1,0:T(8,128)(2,1)S(1)} collective-permute-done((bf16[2,1,128,1024]{3,2,1,0:T(8,128)(2,1)S(1)}, bf16[2,1,128,1024]{3,2,1,0:T(8,128)(2,1)S(1)}, u32[]{:S(2)}, u32[]{:S(2)}) %collective-permute-start.2) | collective-permute-done | bytes 524320 | tf_op jit(solution)/shard_map/ppermute | solution.py:12
  90.9 4.3 collective-permute-start.3
  95.2 11.0 %collective-permute-done.3 = bf16[2,1,128,1024]{3,2,1,0:T(8,128)(2,1)S(1)} collective-permute-done((bf16[2,1,128,1024]{3,2,1,0:T(8,128)(2,1)S(1)}, bf16[2,1,128,1024]{3,2,1,0:T(8,128)(2,1)S(1)}, u32[]{:S(2)}, u32[]{:S(2)}) %collective-permute-start.3) | collective-permute-done | bytes 524320 | tf_op jit(solution)/shard_map/ppermute | solution.py:12
  106.2 3.2 collective-permute-start.4
  109.4 9.8 %collective-permute-done.4 = bf16[2,1,128,1024]{3,2,1,0:T(8,128)(2,1)S(1)} collective-permute-done((bf16[2,1,128,1024]{3,2,1,0:T(8,128)(2,1)S(1)}, bf16[2,1,128,1024]{3,2,1,0:T(8,128)(2,1)S(1)}, u32[]{:S(2)}, u32[]{:S(2)}) %collective-permute-start.4) | collective-permute-done | bytes 524320 | tf_op jit(solution)/shard_map/ppermute | solution.py:12
  119.2 4.2 collective-permute-start.5
  123.4 22.7 %collective-permute-done.5 = bf16[2,1,128,1024]{3,2,1,0:T(8,128)(2,1)S(1)} collective-permute-done((bf16[2,1,128,1024]{3,2,1,0:T(8,128)(2,1)S(1)}, bf16[2,1,128,1024]{3,2,1,0:T(8,128)(2,1)S(1)}, u32[]{:S(2)}, u32[]{:S(2)}) %collective-permute-start.5) | collective-permute-done | bytes 524320 | tf_op jit(solution)/shard_map/ppermute | solution.py:12
  146.1 7.4 %collective-permute-start.6 = (bf16[2,1,128,1024]{3,2,1,0:T(8,128)(2,1)S(1)}, bf16[2,1,128,1024]{3,2,1,0:T(8,128)(2,1)S(1)}, u32[]{:S(2)}, u32[]{:S(2)}) collective-permute-start(bf16[2,1,128,1024]{3,2,1,0:T(8,128)(2,1)S(1)} %collective-permute-done.5), channel_id=1, source_target_pairs={{0,128},{4,132},{8,136},{12,140},{16,144},{20,148},{24,152},{28,15... | collective-permute-start | bytes 1572872 | tf_op jit(solution)/shard_map/ppermute | solution.py:12
  153.5 56.4 %collective-permute-done.6 = bf16[2,1,128,1024]{3,2,1,0:T(8,128)(2,1)S(1)} collective-permute-done((bf16[2,1,128,1024]{3,2,1,0:T(8,128)(2,1)S(1)}, bf16[2,1,128,1024]{3,2,1,0:T(8,128)(2,1)S(1)}, u32[]{:S(2)}, u32[]{:S(2)}) %collective-permute-start.6) | collective-permute-done | bytes 524320 | tf_op jit(solution)/shard_map/ppermute | solution.py:12
  209.9 11.1 %collective-permute-start.7 = (bf16[2,1,128,1024]{3,2,1,0:T(8,128)(2,1)S(1)}, bf16[2,1,128,1024]{3,2,1,0:T(8,128)(2,1)S(1)}, u32[]{:S(2)}, u32[]{:S(2)}) collective-permute-start(bf16[2,1,128,1024]{3,2,1,0:T(8,128)(2,1)S(1)} %collective-permute-done.6), channel_id=1, source_target_pairs={{0,256},{4,260},{8,264},{12,268},{16,272},{20,276},{24,280},{28,28... | collective-permute-start | bytes 1572872 | tf_op jit(solution)/shard_map/ppermute | solution.py:12
  221.1 0.6 fusion.44
  221.7 3.1 collective-permute-start
  224.9 17.6 %collective-permute-done.7 = bf16[2,1,128,1024]{3,2,1,0:T(8,128)(2,1)S(1)} collective-permute-done((bf16[2,1,128,1024]{3,2,1,0:T(8,128)(2,1)S(1)}, bf16[2,1,128,1024]{3,2,1,0:T(8,128)(2,1)S(1)}, u32[]{:S(2)}, u32[]{:S(2)}) %collective-permute-start.7) | collective-permute-done | bytes 524320 | tf_op jit(solution)/shard_map/ppermute | solution.py:12
  242.5 1.8 rev.20
  244.3 2.4 fusion.49
  246.8 3.1 collective-permute-start.8
  249.9 11.6 %collective-permute-done.8 = bf16[2,1,128,1024]{3,2,1,0:T(8,128)(2,1)S(1)} collective-permute-done((bf16[2,1,128,1024]{3,2,1,0:T(8,128)(2,1)S(1)}, bf16[2,1,128,1024]{3,2,1,0:T(8,128)(2,1)S(1)}, u32[]{:S(2)}, u32[]{:S(2)}) %collective-permute-start.8) | collective-permute-done | bytes 524320 | tf_op jit(solution)/shard_map/ppermute | solution.py:12
  261.4 4.6 collective-permute-start.9
  266.1 10.7 %collective-permute-done.9 = bf16[2,1,128,1024]{3,2,1,0:T(8,128)(2,1)S(1)} collective-permute-done((bf16[2,1,128,1024]{3,2,1,0:T(8,128)(2,1)S(1)}, bf16[2,1,128,1024]{3,2,1,0:T(8,128)(2,1)S(1)}, u32[]{:S(2)}, u32[]{:S(2)}) %collective-permute-start.9) | collective-permute-done | bytes 524320 | tf_op jit(solution)/shard_map/ppermute | solution.py:12
  276.8 4.3 collective-permute-start.10
  281.1 10.2 %collective-permute-done.10 = bf16[2,1,128,1024]{3,2,1,0:T(8,128)(2,1)S(1)} collective-permute-done((bf16[2,1,128,1024]{3,2,1,0:T(8,128)(2,1)S(1)}, bf16[2,1,128,1024]{3,2,1,0:T(8,128)(2,1)S(1)}, u32[]{:S(2)}, u32[]{:S(2)}) %collective-permute-start.10) | collective-permute-done | bytes 524320 | tf_op jit(solution)/shard_map/ppermute | solution.py:12
  291.3 4.1 collective-permute-start.11
  295.4 9.2 %collective-permute-done.11 = bf16[2,1,128,1024]{3,2,1,0:T(8,128)(2,1)S(1)} collective-permute-done((bf16[2,1,128,1024]{3,2,1,0:T(8,128)(2,1)S(1)}, bf16[2,1,128,1024]{3,2,1,0:T(8,128)(2,1)S(1)}, u32[]{:S(2)}, u32[]{:S(2)}) %collective-permute-start.11) | collective-permute-done | bytes 524320 | tf_op jit(solution)/shard_map/ppermute | solution.py:12
  304.6 11.4 %collective-permute-start.12 = (bf16[2,1,128,1024]{3,2,1,0:T(8,128)(2,1)S(1)}, bf16[2,1,128,1024]{3,2,1,0:T(8,128)(2,1)}, u32[]{:S(2)}, u32[]{:S(2)}) collective-permute-start(bf16[2,1,128,1024]{3,2,1,0:T(8,128)(2,1)S(1)} %collective-permute-done.11), channel_id=1, source_target_pairs={{0,64},{4,68},{8,72},{12,76},{16,80},{20,84},{24,88},{28,92},{32,9... | collective-permute-start | bytes 1572872 | tf_op jit(solution)/shard_map/ppermute | solution.py:12
  316.0 22.8 %collective-permute-done.12 = bf16[2,1,128,1024]{3,2,1,0:T(8,128)(2,1)} collective-permute-done((bf16[2,1,128,1024]{3,2,1,0:T(8,128)(2,1)S(1)}, bf16[2,1,128,1024]{3,2,1,0:T(8,128)(2,1)}, u32[]{:S(2)}, u32[]{:S(2)}) %collective-permute-start.12) | collective-permute-done | bytes 524320 | tf_op jit(solution)/shard_map/ppermute | solution.py:12
  338.8 4.2 collective-permute-start.13
  343.0 0.7 slice.128
  343.8 3.5 rev.23
  347.3 55.4 %collective-permute-done.13 = bf16[2,1,128,1024]{3,2,1,0:T(8,128)(2,1)} collective-permute-done((bf16[2,1,128,1024]{3,2,1,0:T(8,128)(2,1)}, bf16[2,1,128,1024]{3,2,1,0:T(8,128)(2,1)}, u32[]{:S(2)}, u32[]{:S(2)}) %collective-permute-start.13) | collective-permute-done | bytes 524320 | tf_op jit(solution)/shard_map/ppermute | solution.py:12
  402.7 10.2 %collective-permute-start.14 = (bf16[2,1,128,1024]{3,2,1,0:T(8,128)(2,1)}, bf16[2,1,128,1024]{3,2,1,0:T(8,128)(2,1)}, u32[]{:S(2)}, u32[]{:S(2)}) collective-permute-start(bf16[2,1,128,1024]{3,2,1,0:T(8,128)(2,1)} %collective-permute-done.13), channel_id=1, source_target_pairs={{0,256},{4,260},{8,264},{12,268},{16,272},{20,276},{24,280},{28,28... | collective-permute-start | bytes 1572872 | tf_op jit(solution)/shard_map/ppermute | solution.py:12
  412.9 2.9 fusion.18
  415.8 1.0 copy-done.1
  416.8 1.4 collective-permute-start.15
  418.3 1.1 convolution_multiply_fusion
  419.4 0.0 reduce-scatter.8.cloned.1.call-update
  419.4 0.0 reduce-scatter.6.cloned.1.call-start
  419.5 0.8 stack.31
  420.3 0.6 broadcast_multiply_fusion
  420.9 0.0 reduce-scatter.6.cloned.1.call-update
  420.9 0.0 reduce-scatter.4.cloned.1.call-start
  420.9 9.6 %collective-permute-done.14 = bf16[2,1,128,1024]{3,2,1,0:T(8,128)(2,1)} collective-permute-done((bf16[2,1,128,1024]{3,2,1,0:T(8,128)(2,1)}, bf16[2,1,128,1024]{3,2,1,0:T(8,128)(2,1)}, u32[]{:S(2)}, u32[]{:S(2)}) %collective-permute-start.14) | collective-permute-done | bytes 524320 | tf_op jit(solution)/shard_map/ppermute | solution.py:12
  430.5 7.0 %rev.21 = bf16[2,1,128,1024]{3,2,1,0:T(8,128)(2,1)S(1)} reverse(bf16[2,1,128,1024]{3,2,1,0:T(8,128)(2,1)} %collective-permute-done.14), dimensions={0,2,3} | reverse | bytes 1048576 | tf_op jit(solution)/shard_map/jit(_flip)/rev | solution.py:27
  437.6 1.0 fusion.23
  438.6 0.5 fusion.42
  439.0 1.7 rev.22
  440.7 1.8 multiply_bitcast_fusion
  442.5 0.0 reduce-scatter.4.cloned.1.call-update
  442.6 0.0 reduce-scatter.8.cloned.1.call-done
  442.6 1.4 copy.18
  444.0 25.9 %reduce-scatter.6.cloned.1.call-done = f32[7,256]{1,0:T(8,128)} async-done(((f32[7,1024]{1,0:T(8,128)}), f32[7,256]{1,0:T(8,128)}) %reduce-scatter.6.cloned.1.call-update) | async-done | bytes 7184 | tf_op jit(solution)/shard_map/reduce_scatter | solution.py:104
  470.0 1.3 broadcast_in_dim.15
  471.3 1.5 fusion.3
  472.8 36.5 %reduce-scatter.4.cloned.1.call-done = f32[128,1024]{0,1:T(8,128)} async-done(((f32[512,1024]{0,1:T(8,128)}), f32[128,1024]{0,1:T(8,128)}) %reduce-scatter.4.cloned.1.call-update) | async-done | bytes 524304 | tf_op jit(solution)/shard_map/reduce_scatter | solution.py:103
  509.3 2.0 copy.17
  (34 shorter events, 0.1 us)
Async XLA Ops:
  7.2 213.9 %copy-start = (f32[6,1024]{1,0:T(8,128)S(1)}, f32[6,1024]{1,0:T(8,128)}, u32[]{:S(2)}) copy-start(f32[6,1024]{1,0:T(8,128)} %param.13) | copy-start | bytes 73732
  7.2 50.9 %copy-start.7 = (bf16[2,1,128,1024]{3,2,1,0:T(8,128)(2,1)S(1)}, bf16[2,1,128,1024]{3,2,1,0:T(8,128)(2,1)}, u32[]{:S(2)}) copy-start(bf16[2,1,128,1024]{3,2,1,0:T(8,128)(2,1)} %param.7) | copy-start | bytes 1572868
  7.2 37.0 %all-gather.2.cloned.1.call-start = ((), (), s32[]{:S(2)}) async-start(), calls=%async_computation.3 | async-start | bytes 1310720 | tf_op jit(solution)/shard_map/all_gather | solution.py:40
  7.9 434.7 %reduce-scatter.8.cloned.1.call-start = ((), (), s32[]{:S(2)}) async-start(), calls=%async_computation.6 | async-start | bytes 40960 | tf_op jit(solution)/shard_map/reduce_scatter | solution.py:105
  44.1 14.0 %copy-start.3 = (bf16[512,1024]{1,0:T(8,128)(2,1)S(1)}, bf16[512,1024]{1,0:T(8,128)(2,1)}, u32[]{:S(2)}) copy-start(bf16[512,1024]{1,0:T(8,128)(2,1)} %all-gather.2.cloned.1.call-done) | copy-start | bytes 3145732
  58.1 1.0 copy-start.5
  58.1 162.9 %copy-start.13 = (s32[2,1,128]{2,1,0:T(1,128)S(1)}, s32[2,1,128]{2,1,0:T(1,128)}, u32[]{:S(2)}) copy-start(s32[2,1,128]{2,1,0:T(1,128)} %param.9) | copy-start | bytes 3076
  58.2 162.9 %copy-start.14 = (s32[2,1,128]{2,1,0:T(1,128)S(1)}, s32[2,1,128]{2,1,0:T(1,128)}, u32[]{:S(2)}) copy-start(s32[2,1,128]{2,1,0:T(1,128)} %param.10) | copy-start | bytes 3076
  58.2 166.7 %copy-start.10 = (f32[7,1024]{1,0:T(8,128)S(1)}, f32[7,1024]{1,0:T(8,128)}, u32[]{:S(2)}) copy-start(f32[7,1024]{1,0:T(8,128)} %param.12) | copy-start | bytes 86020
  59.1 15.6 %collective-permute-start.1 = (bf16[2,1,128,1024]{3,2,1,0:T(8,128)(2,1)S(1)}, bf16[2,1,128,1024]{3,2,1,0:T(8,128)(2,1)S(1)}, u32[]{:S(2)}, u32[]{:S(2)}) collective-permute-start(bf16[2,1,128,1024]{3,2,1,0:T(8,128)(2,1)S(1)} %bitcast.46), channel_id=1, source_target_pairs={{0,4},{4,0},{8,12},{12,8},{16,20},{20,16},{24,28},{28,24},{32,36},... | collective-permute-start | bytes 1572872 | tf_op jit(solution)/shard_map/ppermute | solution.py:12
  74.7 16.2 %collective-permute-start.2 = (bf16[2,1,128,1024]{3,2,1,0:T(8,128)(2,1)S(1)}, bf16[2,1,128,1024]{3,2,1,0:T(8,128)(2,1)S(1)}, u32[]{:S(2)}, u32[]{:S(2)}) collective-permute-start(bf16[2,1,128,1024]{3,2,1,0:T(8,128)(2,1)S(1)} %collective-permute-done.1), channel_id=1, source_target_pairs={{0,8},{4,12},{8,0},{12,4},{16,24},{20,28},{24,16},{28,20},{32,40},... | collective-permute-start | bytes 1572872 | tf_op jit(solution)/shard_map/ppermute | solution.py:12
  90.9 15.3 %collective-permute-start.3 = (bf16[2,1,128,1024]{3,2,1,0:T(8,128)(2,1)S(1)}, bf16[2,1,128,1024]{3,2,1,0:T(8,128)(2,1)S(1)}, u32[]{:S(2)}, u32[]{:S(2)}) collective-permute-start(bf16[2,1,128,1024]{3,2,1,0:T(8,128)(2,1)S(1)} %collective-permute-done.2), channel_id=1, source_target_pairs={{0,16},{4,20},{8,24},{12,28},{16,0},{20,4},{24,8},{28,12},{32,48},... | collective-permute-start | bytes 1572872 | tf_op jit(solution)/shard_map/ppermute | solution.py:12
  106.2 13.0 %collective-permute-start.4 = (bf16[2,1,128,1024]{3,2,1,0:T(8,128)(2,1)S(1)}, bf16[2,1,128,1024]{3,2,1,0:T(8,128)(2,1)S(1)}, u32[]{:S(2)}, u32[]{:S(2)}) collective-permute-start(bf16[2,1,128,1024]{3,2,1,0:T(8,128)(2,1)S(1)} %collective-permute-done.3), channel_id=1, source_target_pairs={{0,32},{4,36},{8,40},{12,44},{16,48},{20,52},{24,56},{28,60},{32,0... | collective-permute-start | bytes 1572872 | tf_op jit(solution)/shard_map/ppermute | solution.py:12
  119.2 26.9 %collective-permute-start.5 = (bf16[2,1,128,1024]{3,2,1,0:T(8,128)(2,1)S(1)}, bf16[2,1,128,1024]{3,2,1,0:T(8,128)(2,1)S(1)}, u32[]{:S(2)}, u32[]{:S(2)}) collective-permute-start(bf16[2,1,128,1024]{3,2,1,0:T(8,128)(2,1)S(1)} %collective-permute-done.4), channel_id=1, source_target_pairs={{0,64},{4,68},{8,72},{12,76},{16,80},{20,84},{24,88},{28,92},{32,9... | collective-permute-start | bytes 1572872 | tf_op jit(solution)/shard_map/ppermute | solution.py:12
  146.1 63.8 %collective-permute-start.6 = (bf16[2,1,128,1024]{3,2,1,0:T(8,128)(2,1)S(1)}, bf16[2,1,128,1024]{3,2,1,0:T(8,128)(2,1)S(1)}, u32[]{:S(2)}, u32[]{:S(2)}) collective-permute-start(bf16[2,1,128,1024]{3,2,1,0:T(8,128)(2,1)S(1)} %collective-permute-done.5), channel_id=1, source_target_pairs={{0,128},{4,132},{8,136},{12,140},{16,144},{20,148},{24,152},{28,15... | collective-permute-start | bytes 1572872 | tf_op jit(solution)/shard_map/ppermute | solution.py:12
  209.9 32.6 %collective-permute-start.7 = (bf16[2,1,128,1024]{3,2,1,0:T(8,128)(2,1)S(1)}, bf16[2,1,128,1024]{3,2,1,0:T(8,128)(2,1)S(1)}, u32[]{:S(2)}, u32[]{:S(2)}) collective-permute-start(bf16[2,1,128,1024]{3,2,1,0:T(8,128)(2,1)S(1)} %collective-permute-done.6), channel_id=1, source_target_pairs={{0,256},{4,260},{8,264},{12,268},{16,272},{20,276},{24,280},{28,28... | collective-permute-start | bytes 1572872 | tf_op jit(solution)/shard_map/ppermute | solution.py:12
  221.1 25.7 %copy-start.11 = (s32[2,1,128]{2,1,0:T(1,128)}, s32[2,1,128]{2,1,0:T(1,128)S(1)}, u32[]{:S(2)}) copy-start(s32[2,1,128]{2,1,0:T(1,128)S(1)} %compare_select_fusion) | copy-start | bytes 3076
  221.7 22.6 %collective-permute-start = (bf16[2,1,6,1024]{3,2,1,0:T(8,128)(2,1)S(1)}, bf16[2,1,6,1024]{3,2,1,0:T(8,128)(2,1)S(1)}, u32[]{:S(2)}, u32[]{:S(2)}) collective-permute-start(bf16[2,1,6,1024]{3,2,1,0:T(8,128)(2,1)S(1)} %slice.105), channel_id=1, source_target_pairs={{0,4},{4,8},{8,12},{12,16},{16,20},{20,24},{24,28},{28,32},{32,36}... | collective-permute-start | bytes 73736 | tf_op jit(solution)/shard_map/ppermute | solution.py:18
  244.3 98.7 %copy-start.8 = (bf16[2,1,128,1024]{3,2,1,0:T(8,128)(2,1)S(1)}, bf16[2,1,128,1024]{3,2,1,0:T(8,128)(2,1)}, u32[]{:S(2)}) copy-start(bf16[2,1,128,1024]{3,2,1,0:T(8,128)(2,1)} %param.7) | copy-start | bytes 1572868
  246.8 14.7 %collective-permute-start.8 = (bf16[2,1,128,1024]{3,2,1,0:T(8,128)(2,1)S(1)}, bf16[2,1,128,1024]{3,2,1,0:T(8,128)(2,1)S(1)}, u32[]{:S(2)}, u32[]{:S(2)}) collective-permute-start(bf16[2,1,128,1024]{3,2,1,0:T(8,128)(2,1)S(1)} %get-tuple-element.16), channel_id=1, source_target_pairs={{0,4},{4,0},{8,12},{12,8},{16,20},{20,16},{24,28},{28,24},{32,36},... | collective-permute-start | bytes 1572872 | tf_op jit(solution)/shard_map/ppermute | solution.py:12
  261.4 15.3 %collective-permute-start.9 = (bf16[2,1,128,1024]{3,2,1,0:T(8,128)(2,1)S(1)}, bf16[2,1,128,1024]{3,2,1,0:T(8,128)(2,1)S(1)}, u32[]{:S(2)}, u32[]{:S(2)}) collective-permute-start(bf16[2,1,128,1024]{3,2,1,0:T(8,128)(2,1)S(1)} %collective-permute-done.8), channel_id=1, source_target_pairs={{0,8},{4,12},{8,0},{12,4},{16,24},{20,28},{24,16},{28,20},{32,40},... | collective-permute-start | bytes 1572872 | tf_op jit(solution)/shard_map/ppermute | solution.py:12
  276.8 14.5 %collective-permute-start.10 = (bf16[2,1,128,1024]{3,2,1,0:T(8,128)(2,1)S(1)}, bf16[2,1,128,1024]{3,2,1,0:T(8,128)(2,1)S(1)}, u32[]{:S(2)}, u32[]{:S(2)}) collective-permute-start(bf16[2,1,128,1024]{3,2,1,0:T(8,128)(2,1)S(1)} %collective-permute-done.9), channel_id=1, source_target_pairs={{0,16},{4,20},{8,24},{12,28},{16,0},{20,4},{24,8},{28,12},{32,48},... | collective-permute-start | bytes 1572872 | tf_op jit(solution)/shard_map/ppermute | solution.py:12
  291.3 13.4 %collective-permute-start.11 = (bf16[2,1,128,1024]{3,2,1,0:T(8,128)(2,1)S(1)}, bf16[2,1,128,1024]{3,2,1,0:T(8,128)(2,1)S(1)}, u32[]{:S(2)}, u32[]{:S(2)}) collective-permute-start(bf16[2,1,128,1024]{3,2,1,0:T(8,128)(2,1)S(1)} %collective-permute-done.10), channel_id=1, source_target_pairs={{0,32},{4,36},{8,40},{12,44},{16,48},{20,52},{24,56},{28,60},{32,0... | collective-permute-start | bytes 1572872 | tf_op jit(solution)/shard_map/ppermute | solution.py:12
  304.6 34.2 %collective-permute-start.12 = (bf16[2,1,128,1024]{3,2,1,0:T(8,128)(2,1)S(1)}, bf16[2,1,128,1024]{3,2,1,0:T(8,128)(2,1)}, u32[]{:S(2)}, u32[]{:S(2)}) collective-permute-start(bf16[2,1,128,1024]{3,2,1,0:T(8,128)(2,1)S(1)} %collective-permute-done.11), channel_id=1, source_target_pairs={{0,64},{4,68},{8,72},{12,76},{16,80},{20,84},{24,88},{28,92},{32,9... | collective-permute-start | bytes 1572872 | tf_op jit(solution)/shard_map/ppermute | solution.py:12
  338.8 63.9 %collective-permute-start.13 = (bf16[2,1,128,1024]{3,2,1,0:T(8,128)(2,1)}, bf16[2,1,128,1024]{3,2,1,0:T(8,128)(2,1)}, u32[]{:S(2)}, u32[]{:S(2)}) collective-permute-start(bf16[2,1,128,1024]{3,2,1,0:T(8,128)(2,1)} %collective-permute-done.12), channel_id=1, source_target_pairs={{0,128},{4,132},{8,136},{12,140},{16,144},{20,148},{24,152},{28,15... | collective-permute-start | bytes 1572872 | tf_op jit(solution)/shard_map/ppermute | solution.py:12
  347.3 71.0 %copy-start.12 = (s32[2,1,128]{2,1,0:T(1,128)S(1)}, s32[2,1,128]{2,1,0:T(1,128)}, u32[]{:S(2)}) copy-start(s32[2,1,128]{2,1,0:T(1,128)} %copy-done.11) | copy-start | bytes 3076
  402.7 27.8 %collective-permute-start.14 = (bf16[2,1,128,1024]{3,2,1,0:T(8,128)(2,1)}, bf16[2,1,128,1024]{3,2,1,0:T(8,128)(2,1)}, u32[]{:S(2)}, u32[]{:S(2)}) collective-permute-start(bf16[2,1,128,1024]{3,2,1,0:T(8,128)(2,1)} %collective-permute-done.13), channel_id=1, source_target_pairs={{0,256},{4,260},{8,264},{12,268},{16,272},{20,276},{24,280},{28,28... | collective-permute-start | bytes 1572872 | tf_op jit(solution)/shard_map/ppermute | solution.py:12
  415.8 1.0 copy-start.1
  416.8 20.7 %copy-start.2 = (f32[2,1,128,1024]{3,2,1,0:T(8,128)S(1)}, f32[2,1,128,1024]{3,2,1,0:T(8,128)}, u32[]{:S(2)}) copy-start(f32[2,1,128,1024]{3,2,1,0:T(8,128)} %copy-done.1) | copy-start | bytes 3145732
  416.8 20.7 %collective-permute-start.15 = (f32[2,1,6,1024]{3,2,1,0:T(8,128)S(1)}, f32[2,1,6,1024]{3,2,1,0:T(8,128)S(1)}, u32[]{:S(2)}, u32[]{:S(2)}) collective-permute-start(f32[2,1,6,1024]{3,2,1,0:T(8,128)S(1)} %slice.116), channel_id=1, source_target_pairs={{4,0},{8,4},{12,8},{16,12},{20,16},{24,20},{28,24},{32,28},{36,32}... | collective-permute-start | bytes 147464 | tf_op jit(solution)/shard_map/ppermute | solution.py:18
  419.4 19.2 %copy-start.9 = (bf16[2,1,128,1024]{3,2,1,0:T(8,128)(2,1)S(1)}, bf16[2,1,128,1024]{3,2,1,0:T(8,128)(2,1)}, u32[]{:S(2)}) copy-start(bf16[2,1,128,1024]{3,2,1,0:T(8,128)(2,1)} %param.7) | copy-start | bytes 1572868
  419.4 50.6 %reduce-scatter.6.cloned.1.call-start = ((), (), s32[]{:S(2)}) async-start(), calls=%async_computation.5 | async-start | bytes 40960 | tf_op jit(solution)/shard_map/reduce_scatter | solution.py:104
  420.9 88.4 %reduce-scatter.4.cloned.1.call-start = ((), (), s32[]{:S(2)}) async-start(), calls=%async_computation.4 | async-start | bytes 2621440 | tf_op jit(solution)/shard_map/reduce_scatter | solution.py:103
  442.5 28.7 %copy-start.4 = (bf16[512,1024]{1,0:T(8,128)(2,1)S(1)}, bf16[512,1024]{1,0:T(8,128)(2,1)}, u32[]{:S(2)}) copy-start(bf16[512,1024]{1,0:T(8,128)(2,1)} %all-gather.2.cloned.1.call-done) | copy-start | bytes 3145732
  442.5 28.7 %copy-start.6 = (bf16[512,1024]{1,0:T(8,128)(2,1)S(1)}, bf16[512,1024]{1,0:T(8,128)(2,1)}, u32[]{:S(2)}) copy-start(bf16[512,1024]{1,0:T(8,128)(2,1)} %copy-done.5) | copy-start | bytes 3145732
Sparse Core Ops, SparseCore 0:
  10.1 34.0 all-gather.1
  419.5 21.3 reduce-scatter.7
  444.3 25.5 reduce-scatter.5
  472.7 36.6 reduce-scatter.3
where the time goes:
time: 521 us; the launch traced here: 518 us
  waiting for transfers between devices  371 us (71%)
  starting transfers between devices  84.4 us (16%)
  local copies, waits for them, and re-layouts  35.6 us (7%)
  between operations  14.2 us (3%)
  other arithmetic  6.96 us (1%)
  matrix products  6.25 us (1%)
    ppermute x14, waiting for transfers between devices, from_partner(): return lax.ppermute(value, axis, pairs)  271 us
    ppermute x14, starting transfers between devices, from_partner(): return lax.ppermute(value, axis, pairs)  79.8 us
    reduce_scatter x1, waiting for transfers between devices, shards(): lax.psum_scatter(proj_term * grad_scale, 'fsdp', scatter_dimension=0, til...  36.5 us
    all_gather x1, waiting for transfers between devices, shards(): half_rows = lax.all_gather(proj_half, 'fsdp', axis=0, tiled=True)  36.2 us
    reduce_scatter x1, waiting for transfers between devices, shards(): lax.psum_scatter(filter_term * grad_scale, 'fsdp', scatter_dimension=1, t...  25.9 us
    rev x1, local copies, waits for them, and re-layouts, shards(): jnp.flip(half_rows, axis=(0, 1))  14 us
  transfers between devices with their start and end apart: 20, of which 17 were waited for; matrix products, arithmetic and copies ran while one was open for 5% of the time, Pallas kernels for 0%

commit v1 on v0

v1 whole, which is shorter than its diff:
```python
import functools
import math

import jax
import jax.numpy as jnp
from jax import lax
from jax.experimental import pallas as pl
from jax.experimental.pallas import tpu as pltpu
from jax.sharding import PartitionSpec as P

LANES = 128
HALO = 8
F32 = jnp.float32
BF16 = jnp.bfloat16
HIGHEST = lax.Precision.HIGHEST


def dot(a, b):
    return jnp.dot(a, b, preferred_element_type=F32)


def reversal(size, dtype=BF16):
    rows = lax.broadcasted_iota(jnp.int32, (size, size), 0)
    cols = lax.broadcasted_iota(jnp.int32, (size, size), 1)
    return (rows + cols == size - 1).astype(dtype)


def reverse_lanes(value, precision=None):
    count = value.shape[-1] // LANES
    swap = reversal(LANES, value.dtype)
    parts = []
    for block in reversed(range(count)):
        part = value[:, block * LANES : (block + 1) * LANES]
        parts.append(
            jnp.dot(part, swap, preferred_element_type=F32, precision=precision).astype(value.dtype)
        )
    return jnp.concatenate(parts, axis=1)


def reverse_rows(value):
    return dot(reversal(value.shape[0]), value).astype(value.dtype)


def reverse_both(value):
    return reverse_lanes(reverse_rows(value))


def call(kernel, out_shapes, *operands, scalars=0, scratch=(), flops=0, moved=0):
    specs = [pl.BlockSpec(memory_space=pltpu.SMEM)] * scalars
    specs += [pl.BlockSpec(memory_space=pltpu.VMEM)] * (len(operands) - scalars)
    return pl.pallas_call(
        kernel,
        out_shape=out_shapes,
        in_specs=specs,
        out_specs=[pl.BlockSpec(memory_space=pltpu.VMEM)] * len(out_shapes),
        scratch_shapes=list(scratch),
        cost_estimate=pl.CostEstimate(flops=flops, bytes_accessed=moved, transcendentals=0),
        compiler_params=pltpu.CompilerParams(vmem_limit_bytes=48 * 1024 * 1024),
    )(*operands)


def pack_kernel(grad_ref, tokens_ref, tail_ref, head_ref, slab_ref):
    rows = grad_ref.shape[0]
    head = head_ref[...].astype(F32)
    tail = tail_ref[...].astype(F32)
    tail_rev = jnp.dot(reversal(HALO, F32), tail, preferred_element_type=F32).astype(BF16)
    head_rev = jnp.dot(reversal(HALO, F32), head, preferred_element_type=F32).astype(BF16)
    near = head[HALO - 1 : HALO, :LANES].astype(BF16)
    own = tokens_ref[...].astype(F32).astype(BF16)
    both = jnp.concatenate([own, near, jnp.zeros((6, LANES), BF16)], axis=0)
    flipped = dot(both, reversal(LANES))
    token_row = jnp.concatenate(
        [flipped[0:1], flipped[1:2], jnp.zeros((1, slab_ref.shape[1] - 2 * LANES), F32)], axis=1
    )
    at_row = lax.broadcasted_iota(jnp.int32, (HALO, slab_ref.shape[1]), 0) == HALO - 1
    tail_out = jnp.where(at_row, token_row, reverse_lanes(tail_rev).astype(F32)).astype(BF16)
    slab_ref[0:HALO, :] = reverse_lanes(head_rev)
    slab_ref[HALO : HALO + rows, :] = reverse_both(grad_ref[...])
    slab_ref[HALO + rows :, :] = tail_out


def forward_kernel(place_ref, pair_ref, other_ref, normed_ref, tail_ref, weight_ref, values_ref):
    shard = pair_ref.shape[0] // 2
    half = 4 * shard
    x_lo = place_ref[0] // 2
    core = place_ref[0] % 2
    for source, at_core in ((pair_ref, core), (other_ref, 1 - core)):
        for step in range(2):
            block = source[step * shard : (step + 1) * shard, :]
            chip = x_lo if step == 0 else 1 - x_lo
            index = chip * 2 + at_core
            weight_ref[pl.ds(pl.multiple_of(index * shard, shard), shard), :] = block
            back = half + (3 - index) * shard
            weight_ref[pl.ds(pl.multiple_of(back, shard), shard), :] = reverse_both(block)
    weight = weight_ref[...]
    values_ref[HALO:, :] = dot(normed_ref[...], weight).astype(BF16).astype(F32)
    values_ref[0:HALO, :] = dot(tail_ref[...], weight).astype(BF16).astype(F32)


def mirror_forward_kernel(normed_ref, weight_ref, values_ref):
    values_ref[...] = dot(reverse_both(normed_ref[...]), weight_ref[...]).astype(BF16).astype(F32)


def one_hot(row, count):
    classes = lax.broadcasted_iota(jnp.int32, (HALO, count), 0)
    return (row.astype(jnp.int32) == classes).astype(F32)


def rows_of(hot, table):
    return lax.dot_general(
        hot, table, (((0,), (0,)), ((), ())), preferred_element_type=F32, precision=HIGHEST
    )


def gate_kernel(
    slab_ref, values0_ref, values1_ref, weight_ref, grad_ref, head_ref, tokens_ref,
    filter_ref, filter_rev_ref, bias_ref, bias_rev_ref,
    value_grad_ref, send_ref, terms_ref,
    wide0, wide1, pull0, pull1,
):
    rows = grad_ref.shape[0]
    taps = filter_ref.shape[0]
    width = grad_ref.shape[1]
    reach = rows + HALO
    token_row = slab_ref[reach:, :].astype(F32)[HALO - 1 : HALO, :]
    hot1_own = one_hot(token_row[:, :LANES], LANES)
    hot1_far = one_hot(token_row[:, LANES : 2 * LANES], LANES)
    hot0_own = one_hot(tokens_ref[...], LANES)
    hot0_far = one_hot(head_ref[...].astype(F32)[HALO - 1 : HALO, :LANES], LANES)
    edge = dot(slab_ref[reach:, :], weight_ref[...]).astype(BF16).astype(F32)
    values1_edge = edge
    wide = 2 * LANES

    for index in range(width // wide):
        cols = slice(index * wide, (index + 1) * wide)
        taps0 = filter_ref[:, cols]
        taps1 = filter_rev_ref[:, cols]
        wide0[...] = values0_ref[:, cols]
        wide1[0:rows, :] = values1_ref[:, cols]
        wide1[rows:, :] = values1_edge[:, cols]
        bias0 = rows_of(hot0_own, bias_ref[:, cols])
        bias0_far = rows_of(hot0_far, bias_ref[:, cols])
        bias1 = rows_of(hot1_own, bias_rev_ref[:, cols])
        bias1_far = rows_of(hot1_far, bias_rev_ref[:, cols])
        own0 = grad_ref[:, cols].astype(F32)
        own1 = slab_ref[HALO:reach, cols].astype(F32)
        gate0 = jax.nn.sigmoid(wide1[0:rows, :] + bias0)
        gate1 = jax.nn.sigmoid(wide0[HALO:, :] + bias1)
        conv_grad0 = own0 * gate0
        conv_grad1 = own1 * gate1
        pull0[0:rows, :] = conv_grad0
        pull1[HALO:, :] = conv_grad1
        pull0[rows:, :] = head_ref[:, cols].astype(F32) * jax.nn.sigmoid(wide1[rows:, :] + bias0_far[0:HALO])
        pull1[0:HALO, :] = slab_ref[0:HALO, cols].astype(F32) * jax.nn.sigmoid(
            wide0[0:HALO, :] + bias1_far[LANES - HALO :]
        )
        conv0 = jnp.zeros((rows, wide), F32)
        conv1 = jnp.zeros((rows, wide), F32)
        for tap in range(taps):
            shifted0 = wide0[HALO - tap : HALO - tap + rows, :]
            shifted1 = wide1[tap : tap + rows, :]
            conv0 = conv0 + taps0[tap : tap + 1] * shifted0
            conv1 = conv1 + taps1[tap : tap + 1] * shifted1
            terms_ref[tap : tap + 1, cols] = jnp.sum(conv_grad0 * shifted0, axis=0, keepdims=True)
            terms_ref[16 + tap : 17 + tap, cols] = jnp.sum(conv_grad1 * shifted1, axis=0, keepdims=True)
        pre0 = own0 * conv0 * gate0 * (1.0 - gate0)
        pre1 = own1 * conv1 * gate1 * (1.0 - gate1)
        terms_ref[8:16, cols] = jnp.dot(hot0_own, pre0, preferred_element_type=F32, precision=HIGHEST)
        terms_ref[24:32, cols] = jnp.dot(hot1_own, pre1, preferred_element_type=F32, precision=HIGHEST)
        total0 = pre1.astype(BF16).astype(F32)
        total1 = pre0.astype(BF16).astype(F32)
        for tap in range(taps):
            total0 = total0 + taps0[tap : tap + 1] * pull0[tap : tap + rows, :]
            total1 = total1 + taps1[tap : tap + 1] * pull1[HALO - tap : HALO - tap + rows, :]
        value_grad_ref[:, cols] = total0.astype(BF16)
        send_ref[0:rows, cols] = total1.astype(BF16)
    unused = jnp.zeros((1, width), F32)
    terms_ref[7:8, :] = unused
    terms_ref[23:24, :] = unused
    send_ref[rows:, :] = terms_ref[16:, :].astype(BF16)


def operands_kernel(normed_ref, value_grad_ref, left_ref, right_ref):
    rows = normed_ref.shape[1]
    half = normed_ref.shape[2] // 2
    for strand in range(2):
        value = normed_ref[strand]
        left_ref[strand * rows : (strand + 1) * rows, :] = value[:, :half]
        left_ref[(2 + strand) * rows : (3 + strand) * rows, :] = reverse_both(value)[:, :half]
    right_ref[0:rows, :] = value_grad_ref[...]
    right_ref[rows:, :] = reverse_both(value_grad_ref[...])


def project_kernel(
    place_ref, scale, left_ref, right_ref, back_ref, terms_ref, value_grad_ref,
    send_ref, keep_ref, sums_ref, final_ref,
):
    rows = right_ref.shape[0] // 2
    back = back_ref[0:rows, :]
    home = reverse_both(back)
    final_ref[0] = right_ref[0:rows, :]
    final_ref[1] = home
    right = jnp.concatenate([right_ref[0:rows, :], home, right_ref[rows:, :], back], axis=0)
    sums = (terms_ref[0:16, :] + reverse_lanes(back_ref[rows:, :]).astype(F32)) * scale
    sums_ref[...] = sums
    core = place_ref[0] % 2
    shard = left_ref.shape[1] // 4
    for chip in range(2):
        for mine in range(2):
            index = chip * 2 + (core if mine else 1 - core)
            left = left_ref[:, pl.ds(pl.multiple_of(index * shard, shard), shard)]
            part = lax.dot_general(left, right, (((0,), (0,)), ((), ())), preferred_element_type=F32) * scale
            if mine:
                keep_ref[chip * shard : (chip + 1) * shard, :] = part
            else:
                send_ref[chip * shard : (chip + 1) * shard, :] = part.astype(BF16)
    send_ref[2 * shard :, :] = sums.astype(BF16)


def input_grad_kernel(value_grad_ref, weight_ref, out_ref):
    weight = weight_ref[...]
    for strand in range(2):
        out_ref[strand] = lax.dot_general(
            value_grad_ref[strand], weight, (((1,), (1,)), ((), ())), preferred_element_type=F32
        ).astype(BF16)


def first_sum_kernel(place_ref, keep_ref, got_ref, sums_ref, send_ref, keep_out_ref, sums_out_ref):
    shard = keep_ref.shape[0] // 2
    x_lo = place_ref[0] // 2
    here = pl.ds(pl.multiple_of(x_lo * shard, shard), shard)
    there = pl.ds(pl.multiple_of((1 - x_lo) * shard, shard), shard)
    keep_out_ref[...] = keep_ref[here, :] + got_ref[here, :].astype(F32)
    send_ref[0:shard, :] = (keep_ref[there, :] + got_ref[there, :].astype(F32)).astype(BF16)
    sums = sums_ref[...] + got_ref[2 * shard :, :].astype(F32)
    sums_out_ref[...] = sums
    send_ref[shard:, :] = sums.astype(BF16)


def last_sum_kernel(place_ref, keep_ref, got_ref, sums_ref, proj_ref, filter_ref, bias_ref):
    shard = keep_ref.shape[0]
    part = filter_ref.shape[1]
    proj_ref[...] = keep_ref[...] + got_ref[0:shard, :].astype(F32)
    cols = pl.ds(pl.multiple_of(place_ref[0] * part, part), part)
    sums = sums_ref[:, cols] + got_ref[shard:, cols].astype(F32)
    filter_ref[...] = sums[0 : filter_ref.shape[0], :]
    bias_ref[...] = sums[8 : 8 + bias_ref.shape[0], :]


def mirrored(value):
    size = lax.axis_size("ctx")
    return lax.ppermute(value, "ctx", [(i, size - 1 - i) for i in range(size)])


def shifted(value, distance):
    devices = range(lax.axis_size("ctx"))
    return lax.ppermute(value, "ctx", [(i, i + distance) for i in devices if i + distance in devices])


def partner(value, bit):
    return lax.ppermute(value, "fsdp", [(i, i ^ bit) for i in range(lax.axis_size("fsdp"))])


def shape(dims, dtype):
    return jax.ShapeDtypeStruct(dims, dtype)


def after(value, *others):
    return lax.optimization_barrier((value, *others))[0]


def shards(normed, out_grad, ids, mask, proj_half, conv_filter, gate_bias):
    rows, width = normed.shape[2], normed.shape[3]
    taps = conv_filter.shape[0]
    shard = proj_half.shape[0]
    classes = gate_bias.shape[0]
    normed = normed[:, 0]
    out_grad = out_grad[:, 0]
    place = lax.axis_index("fsdp").astype(jnp.int32).reshape(1)
    tokens = jnp.where(mask == 1, 5, ids)[:, 0]

    normed_far = mirrored(normed[1])
    tails = shifted(normed[:, rows - HALO :, :], 1)
    token_rows = jnp.pad(tokens.astype(F32).astype(BF16), ((0, 0), (0, width - rows)))
    heads = jnp.concatenate([out_grad[:, : HALO - 1, :], token_rows[:, None, :]], axis=1)
    heads = shifted(heads, -1)
    near = partner(proj_half, 2)

    slab, = call(
        pack_kernel, (shape((rows + 2 * HALO, width), BF16),),
        out_grad[1], tokens[1:2], tails[1], heads[1],
        flops=2 * rows * width * 300, moved=4 * rows * width,
    )
    slab = mirrored(slab)
    pair = jnp.concatenate([proj_half, near], axis=0)
    other = partner(pair, 1)
    filter_rev = conv_filter[:, ::-1]
    bias = jnp.pad(gate_bias, ((0, HALO - classes), (0, 0)))
    bias_rev = bias[:, ::-1]

    weight, values0 = call(
        forward_kernel,
        (shape((width, width), BF16), shape((rows + HALO, width), F32)),
        place, pair, other, normed[0], tails[0], scalars=1,
        flops=2 * rows * width * width, moved=6 * width * width,
    )
    values1, = call(
        mirror_forward_kernel, (shape((rows, width), F32),), normed_far, weight,
        flops=2 * rows * width * width, moved=4 * width * width,
    )
    reach = rows + HALO
    wide = 2 * LANES
    value_grad, send, terms = call(
        gate_kernel,
        (shape((rows, width), BF16), shape((rows + 16, width), BF16), shape((32, width), F32)),
        slab, values0, values1, weight, out_grad[0], heads[0], tokens[0:1],
        conv_filter, filter_rev, bias, bias_rev,
        scratch=[pltpu.VMEM((reach, wide), F32)] * 4,
        flops=2 * rows * width * width, moved=4 * width * width,
    )
    back = mirrored(send)
    left, right = call(
        operands_kernel, (shape((4 * rows, width // 2), BF16), shape((2 * rows, width), BF16)),
        normed, value_grad, flops=rows * width * width, moved=8 * rows * width,
    )
    grad_scale = 1.0 / math.sqrt(2.0 * lax.axis_size("fsdp") * rows)
    send1, keep1, sums1, final = call(
        lambda place_ref, *refs: project_kernel(place_ref, grad_scale, *refs),
        (
            shape((2 * shard + 16, width), BF16),
            shape((2 * shard, width), F32),
            shape((16, width), F32),
            shape((2, rows, width), BF16),
        ),
        place, left, right, back, terms, value_grad, scalars=1,
        flops=4 * rows * width * width, moved=4 * width * width,
    )
    got1 = partner(send1, 1)
    in_grad, = call(
        input_grad_kernel, (shape((2, rows, width), BF16),), final, weight,
        flops=4 * rows * width * width, moved=4 * width * width,
    )
    send2, keep2, sums2 = call(
        first_sum_kernel,
        (shape((shard + 16, width), BF16), shape((shard, width), F32), shape((16, width), F32)),
        place, keep1, got1, sums1, scalars=1, moved=16 * shard * width,
    )
    got2 = partner(send2, 2)
    part = width // lax.axis_size("fsdp")
    proj_grad, filter_grad, bias_grad = call(
        last_sum_kernel,
        (shape((shard, width), F32), shape((taps, part), F32), shape((classes, part), F32)),
        place, keep2, got2, sums2, scalars=1, moved=12 * shard * width,
    )
    return in_grad[:, None], proj_grad[None], filter_grad[None], bias_grad[None]


def solution(mesh):
    placed = (
        P(None, "fsdp", "ctx", None),
        P(None, "fsdp", "ctx", None),
        P(None, "fsdp", "ctx"),
        P(None, "fsdp", "ctx"),
        P("fsdp", None),
        P(),
        P(),
    )
    return jax.shard_map(
        shards,
        mesh=mesh,
        in_specs=placed,
        out_specs=(
            P(None, "fsdp", "ctx", None),
            P("ctx", "fsdp", None),
            P("ctx", None, "fsdp"),
            P("ctx", None, "fsdp"),
        ),
        check_vma=False,
    )
```

time: 521 us -> 147 us (0.28)
  waiting for transfers between devices: 371 us -> 77.9 us
  starting transfers between devices: 84.4 us -> 47.1 us
  local copies, waits for them, and re-layouts: 35.6 us -> 6.07 us
  Pallas kernels: 0 us -> 13.7 us
  between operations: 14.2 us -> 0.86 us
  matrix products: 6.25 us -> 0 us
  other arithmetic: 6.96 us -> 0.73 us
    ppermute x16 -> x9, waiting for transfers between devices: 271 us -> 77.9 us  [the longest x3 68.6 us: mirrored(): return lax.ppermute(value, 'ctx', [(i, size - 1 - i) for i in range(size)])]
    reduce_scatter x3 -> x0, waiting for transfers between devices: 62.5 us -> none  [the longest x1 36.5 us: shards(): lax.psum_scatter(proj_term * grad_scale, 'fsdp', scatter_dimension=0, til...]
    ppermute x16 -> x9, starting transfers between devices: 84.3 us -> 47.1 us  [the longest x3 25.4 us: mirrored(): return lax.ppermute(value, 'ctx', [(i, size - 1 - i) for i in range(size)])]
    all_gather x1 -> x0, waiting for transfers between devices: 36.2 us -> none  [shards(): half_rows = lax.all_gather(proj_half, 'fsdp', axis=0, tiled=True)]
    rev x5 -> x2, local copies, waits for them, and re-layouts: 28 us -> 1.14 us  [the longest x1 0.58 us: shards(): bias_rev = bias[:, ::-1]]
    pallas_call x0 -> x9, Pallas kernels: none -> 13.7 us  [call(): pl.pallas_call(kernel, out_shape=out_shapes, in_specs=specs, out_specs=[p...]
    dot_general x6 -> x0, matrix products: 6.25 us -> none  [the longest x1 1.8 us: shards(): lax.dot_general(upper_in, jnp.flip(flat_grad, axis=1), (((0,), (0,)), (()...]
  transfers between devices with their start and end apart: 20 -> 9, of which waited for: 17 -> 5; matrix products, arithmetic and copies ran while one was open for 5% -> 3% of each run, Pallas kernels for 0% -> 4%
where the time goes in v1:
time: 147 us; the launch traced here: 146 us
  waiting for transfers between devices  77.9 us (53%)
  starting transfers between devices  47.1 us (32%)
  Pallas kernels  13.7 us (9%)
  local copies, waits for them, and re-layouts  6.07 us (4%)
    ppermute x3, waiting for transfers between devices, mirrored(): return lax.ppermute(value, 'ctx', [(i, size - 1 - i) for i in range(size)])  68.6 us
    ppermute x3, starting transfers between devices, mirrored(): return lax.ppermute(value, 'ctx', [(i, size - 1 - i) for i in range(size)])  25.4 us
    ppermute x4, starting transfers between devices, partner(): lax.ppermute(value, 'fsdp', [(i, i ^ bit) for i in range(lax.axis_size('f...  16.3 us
    pallas_call x9, Pallas kernels, call(): pl.pallas_call(kernel, out_shape=out_shapes, in_specs=specs, out_specs=[p...  13.7 us
    ppermute x4, waiting for transfers between devices, partner(): lax.ppermute(value, 'fsdp', [(i, i ^ bit) for i in range(lax.axis_size('f...  9.24 us
    ppermute x2, starting transfers between devices, shifted(): lax.ppermute(value, 'ctx', [(i, i + distance) for i in devices if i + dis...  5.43 us
  transfers between devices with their start and end apart: 9, of which 5 were waited for; matrix products, arithmetic and copies ran while one was open for 3% of the time, Pallas kernels for 4%

profile of v1, /device:TPU:1, one launch (start us, length us, event | category | flops | bytes accessed | tf_op | source)
XLA Modules:
  0.0 146.4 jit_solution(13730782973285050634)
XLA Ops:
  0.6 0.0 copy-start
  0.6 0.0 copy-start.2
  0.7 0.8 slice.61
  1.5 0.0 copy-start.1
  1.5 4.1 %collective-permute-start = (bf16[2,8,1024]{2,1,0:T(8,128)(2,1)S(1)}, bf16[2,8,1024]{2,1,0:T(8,128)(2,1)S(1)}, u32[]{:S(2)}, u32[]{:S(2)}) collective-permute-start(bf16[2,8,1024]{2,1,0:T(8,128)(2,1)S(1)} %slice.61), channel_id=1, source_target_pairs={{0,4},{4,8},{8,12},{12,16},{16,20},{20,24},{24,28},{28,32},{32,36}... | collective-permute-start | bytes 98312 | tf_op jit(solution)/shard_map/ppermute | solution.py:257
  5.6 0.7 convert_convert_fusion
  6.3 0.8 slice.63
  7.1 1.3 collective-permute-start.1
  8.4 3.1 %collective-permute-start.3 = (bf16[128,1024]{1,0:T(8,128)(2,1)}, bf16[128,1024]{1,0:T(8,128)(2,1)S(1)}, u32[]{:S(2)}, u32[]{:S(2)}) collective-permute-start(bf16[128,1024]{1,0:T(8,128)(2,1)} %param.11), channel_id=1, source_target_pairs={{0,2},{1,3},{2,0},{3,1},{4,6},{5,7},{6,4},{7,5},{8,10},{9,11},{10,... | collective-permute-start | bytes 786440 | tf_op jit(solution)/shard_map/ppermute | solution.py:261
  11.6 1.1 slice_bitcast_fusion
  12.6 1.0 constant_dynamic-update-slice_fusion.1
  13.6 0.0 collective-permute-done
  13.6 2.1 %collective-permute-done.3 = bf16[128,1024]{1,0:T(8,128)(2,1)S(1)} collective-permute-done((bf16[128,1024]{1,0:T(8,128)(2,1)}, bf16[128,1024]{1,0:T(8,128)(2,1)S(1)}, u32[]{:S(2)}, u32[]{:S(2)}) %collective-permute-start.3) | collective-permute-done | bytes 262176 | tf_op jit(solution)/shard_map/ppermute | solution.py:261
  15.8 7.6 %collective-permute-start.4 = (bf16[256,1024]{1,0:T(8,128)(2,1)S(1)}, bf16[256,1024]{1,0:T(8,128)(2,1)S(1)}, u32[]{:S(2)}, u32[]{:S(2)}) collective-permute-start(bf16[256,1024]{1,0:T(8,128)(2,1)S(1)} %constant_dynamic-update-slice_fusion.pair_ref), channel_id=1, source_target_pairs={{0,1},{1,0},{2,3},{3,2},{4,5},{5,4},{6,7},{7,6},{8,9},{9,8},{10,11... | collective-permute-start | bytes 1572872 | tf_op jit(solution)/shard_map/ppermute | solution.py:261
  23.4 0.0 collective-permute-done.1
  23.4 0.7 shard_map.102
  24.1 14.7 %collective-permute-start.2 = (bf16[144,1024]{1,0:T(8,128)(2,1)S(1)}, bf16[144,1024]{1,0:T(8,128)(2,1)S(1)}, u32[]{:S(2)}, u32[]{:S(2)}) collective-permute-start(bf16[144,1024]{1,0:T(8,128)(2,1)S(1)} %shard_map.102), channel_id=1, source_target_pairs={{0,508},{4,504},{8,500},{12,496},{16,492},{20,488},{24,484},{28,48... | collective-permute-start | bytes 884744 | tf_op jit(solution)/shard_map/ppermute | solution.py:252
  38.7 0.0 copy-done
  38.8 1.9 %collective-permute-start.5 = (bf16[128,1024]{1,0:T(8,128)(2,1)S(1)}, bf16[128,1024]{1,0:T(8,128)(2,1)S(1)}, u32[]{:S(2)}, u32[]{:S(2)}) collective-permute-start(bf16[128,1024]{1,0:T(8,128)(2,1)S(1)} %get-tuple-element.50), channel_id=1, source_target_pairs={{0,508},{4,504},{8,500},{12,496},{16,492},{20,488},{24,484},{28,48... | collective-permute-start | bytes 786440 | tf_op jit(solution)/shard_map/ppermute | solution.py:252
  40.7 0.0 copy-done.2
  40.7 0.6 rev.7.bias_rev_ref
  41.3 0.0 copy-done.1
  41.3 0.6 rev.6.filter_rev_ref
  41.9 0.0 collective-permute-done.4.other_ref
  41.9 1.9 %shard_map.103 = (bf16[1024,1024]{1,0:T(8,128)(2,1)S(1)}, f32[136,1024]{1,0:T(8,128)S(1)}) custom-call(s32[1]{0:T(128)} %bitcast.place_ref, bf16[256,1024]{1,0:T(8,128)(2,1)S(1)} %constant_dynamic-update-slice_fusion.pair_ref, bf16[256,1024]{1,0:T(8,128)(2,1)S(1)} %collective-permute-done.4.other_ref, bf16[128,1024]{1,0:T(8,128)(2,1)S(1)} %get-tuple-element.51.normed_ref, ...), custom_call_target="tpu_custom_call" | custom-call | flops 268435456 | bytes 6291456 | tf_op jit(solution)/shard_map/pallas_call | solution.py:51
  43.8 62.7 %collective-permute-done.5.normed_ref = bf16[128,1024]{1,0:T(8,128)(2,1)S(1)} collective-permute-done((bf16[128,1024]{1,0:T(8,128)(2,1)S(1)}, bf16[128,1024]{1,0:T(8,128)(2,1)S(1)}, u32[]{:S(2)}, u32[]{:S(2)}) %collective-permute-start.5) | collective-permute-done | bytes 262176 | tf_op jit(solution)/shard_map/ppermute | solution.py:252
  106.5 0.7 shard_map.104.values1_ref
  107.2 0.0 collective-permute-done.2.slab_ref
  107.2 5.3 %shard_map.105 = (bf16[128,1024]{1,0:T(8,128)(2,1)S(1)}, bf16[144,1024]{1,0:T(8,128)(2,1)S(1)}, f32[32,1024]{1,0:T(8,128)S(1)}) custom-call(bf16[144,1024]{1,0:T(8,128)(2,1)S(1)} %collective-permute-done.2.slab_ref, f32[136,1024]{1,0:T(8,128)S(1)} %get-tuple-element.21.values0_ref, f32[128,1024]{1,0:T(8,128)S(1)} %shard_map.104.values1_ref, ...), custom_call_target="tpu_custom_call" | custom-call | flops 268435456 | bytes 4194304 | tf_op jit(solution)/shard_map/pallas_call | solution.py:51
  112.6 8.8 %collective-permute-start.6 = (bf16[144,1024]{1,0:T(8,128)(2,1)S(1)}, bf16[144,1024]{1,0:T(8,128)(2,1)S(1)}, u32[]{:S(2)}, u32[]{:S(2)}) collective-permute-start(bf16[144,1024]{1,0:T(8,128)(2,1)S(1)} %get-tuple-element.26), channel_id=1, source_target_pairs={{0,508},{4,504},{8,500},{12,496},{16,492},{20,488},{24,484},{28,48... | collective-permute-start | bytes 884744 | tf_op jit(solution)/shard_map/ppermute | solution.py:252
  121.4 0.8 shard_map.106
  122.2 6.0 %collective-permute-done.6.refs_2_ = bf16[144,1024]{1,0:T(8,128)(2,1)S(1)} collective-permute-done((bf16[144,1024]{1,0:T(8,128)(2,1)S(1)}, bf16[144,1024]{1,0:T(8,128)(2,1)S(1)}, u32[]{:S(2)}, u32[]{:S(2)}) %collective-permute-start.6) | collective-permute-done | bytes 294944 | tf_op jit(solution)/shard_map/ppermute | solution.py:252
  128.2 1.1 shard_map.107
  129.2 3.4 %collective-permute-start.7 = (bf16[272,1024]{1,0:T(8,128)(2,1)S(1)}, bf16[272,1024]{1,0:T(8,128)(2,1)S(1)}, u32[]{:S(2)}, u32[]{:S(2)}) collective-permute-start(bf16[272,1024]{1,0:T(8,128)(2,1)S(1)} %get-tuple-element.30), channel_id=1, source_target_pairs={{0,1},{1,0},{2,3},{3,2},{4,5},{5,4},{6,7},{7,6},{8,9},{9,8},{10,11... | collective-permute-start | bytes 1671176 | tf_op jit(solution)/shard_map/ppermute | solution.py:261
  132.6 1.6 %collective-permute-done.7.got_ref = bf16[272,1024]{1,0:T(8,128)(2,1)S(1)} collective-permute-done((bf16[272,1024]{1,0:T(8,128)(2,1)S(1)}, bf16[272,1024]{1,0:T(8,128)(2,1)S(1)}, u32[]{:S(2)}, u32[]{:S(2)}) %collective-permute-start.7) | collective-permute-done | bytes 557088 | tf_op jit(solution)/shard_map/ppermute | solution.py:261
  134.2 0.1 shard_map.109
  134.3 2.2 %collective-permute-start.8 = (bf16[144,1024]{1,0:T(8,128)(2,1)S(1)}, bf16[144,1024]{1,0:T(8,128)(2,1)S(1)}, u32[]{:S(2)}, u32[]{:S(2)}) collective-permute-start(bf16[144,1024]{1,0:T(8,128)(2,1)S(1)} %get-tuple-element.33), channel_id=1, source_target_pairs={{0,2},{1,3},{2,0},{3,1},{4,6},{5,7},{6,4},{7,5},{8,10},{9,11},{10,... | collective-permute-start | bytes 884744 | tf_op jit(solution)/shard_map/ppermute | solution.py:261
  136.5 2.3 %shard_map.108 = bf16[2,128,1024]{2,1,0:T(8,128)(2,1)} custom-call(bf16[2,128,1024]{2,1,0:T(8,128)(2,1)S(1)} %get-tuple-element.28.value_grad_ref, bf16[1024,1024]{1,0:T(8,128)(2,1)S(1)} %get-tuple-element.22.weight_ref), custom_call_target="tpu_custom_call" | custom-call | flops 536870912 | bytes 4194304 | tf_op jit(solution)/shard_map/pallas_call | solution.py:51
  138.8 5.6 %collective-permute-done.8.got_ref = bf16[144,1024]{1,0:T(8,128)(2,1)S(1)} collective-permute-done((bf16[144,1024]{1,0:T(8,128)(2,1)S(1)}, bf16[144,1024]{1,0:T(8,128)(2,1)S(1)}, u32[]{:S(2)}, u32[]{:S(2)}) %collective-permute-start.8) | collective-permute-done | bytes 294944 | tf_op jit(solution)/shard_map/ppermute | solution.py:261
  144.4 0.8 shard_map.110
  145.2 0.6 copy.18
  145.8 0.6 copy.19
  (10 shorter events, 0.1 us)
Async XLA Ops:
  0.6 38.1 %copy-start = (bf16[2,1,128,1024]{3,2,1,0:T(8,128)(2,1)S(1)}, bf16[2,1,128,1024]{3,2,1,0:T(8,128)(2,1)}, u32[]{:S(2)}) copy-start(bf16[2,1,128,1024]{3,2,1,0:T(8,128)(2,1)} %param.7) | copy-start | bytes 1572868
  0.6 40.1 %copy-start.2 = (f32[6,1024]{1,0:T(8,128)S(1)}, f32[6,1024]{1,0:T(8,128)}, u32[]{:S(2)}) copy-start(f32[6,1024]{1,0:T(8,128)} %param.13) | copy-start | bytes 73732
  1.5 39.9 %copy-start.1 = (f32[7,1024]{1,0:T(8,128)S(1)}, f32[7,1024]{1,0:T(8,128)}, u32[]{:S(2)}) copy-start(f32[7,1024]{1,0:T(8,128)} %filter_ref.1) | copy-start | bytes 86020
  1.5 12.2 %collective-permute-start = (bf16[2,8,1024]{2,1,0:T(8,128)(2,1)S(1)}, bf16[2,8,1024]{2,1,0:T(8,128)(2,1)S(1)}, u32[]{:S(2)}, u32[]{:S(2)}) collective-permute-start(bf16[2,8,1024]{2,1,0:T(8,128)(2,1)S(1)} %slice.61), channel_id=1, source_target_pairs={{0,4},{4,8},{8,12},{12,16},{16,20},{20,24},{24,28},{28,32},{32,36}... | collective-permute-start | bytes 98312 | tf_op jit(solution)/shard_map/ppermute | solution.py:257
  7.1 16.2 %collective-permute-start.1 = (bf16[2,8,1024]{2,1,0:T(8,128)(2,1)S(1)}, bf16[2,8,1024]{2,1,0:T(8,128)(2,1)S(1)}, u32[]{:S(2)}, u32[]{:S(2)}) collective-permute-start(bf16[2,8,1024]{2,1,0:T(8,128)(2,1)S(1)} %pad_maximum_fusion), channel_id=1, source_target_pairs={{4,0},{8,4},{12,8},{16,12},{20,16},{24,20},{28,24},{32,28},{36,32}... | collective-permute-start | bytes 98312 | tf_op jit(solution)/shard_map/ppermute | solution.py:257
  8.4 7.3 %collective-permute-start.3 = (bf16[128,1024]{1,0:T(8,128)(2,1)}, bf16[128,1024]{1,0:T(8,128)(2,1)S(1)}, u32[]{:S(2)}, u32[]{:S(2)}) collective-permute-start(bf16[128,1024]{1,0:T(8,128)(2,1)} %param.11), channel_id=1, source_target_pairs={{0,2},{1,3},{2,0},{3,1},{4,6},{5,7},{6,4},{7,5},{8,10},{9,11},{10,... | collective-permute-start | bytes 786440 | tf_op jit(solution)/shard_map/ppermute | solution.py:261
  15.8 26.1 %collective-permute-start.4 = (bf16[256,1024]{1,0:T(8,128)(2,1)S(1)}, bf16[256,1024]{1,0:T(8,128)(2,1)S(1)}, u32[]{:S(2)}, u32[]{:S(2)}) collective-permute-start(bf16[256,1024]{1,0:T(8,128)(2,1)S(1)} %constant_dynamic-update-slice_fusion.pair_ref), channel_id=1, source_target_pairs={{0,1},{1,0},{2,3},{3,2},{4,5},{5,4},{6,7},{7,6},{8,9},{9,8},{10,11... | collective-permute-start | bytes 1572872 | tf_op jit(solution)/shard_map/ppermute | solution.py:261
  24.1 83.2 %collective-permute-start.2 = (bf16[144,1024]{1,0:T(8,128)(2,1)S(1)}, bf16[144,1024]{1,0:T(8,128)(2,1)S(1)}, u32[]{:S(2)}, u32[]{:S(2)}) collective-permute-start(bf16[144,1024]{1,0:T(8,128)(2,1)S(1)} %shard_map.102), channel_id=1, source_target_pairs={{0,508},{4,504},{8,500},{12,496},{16,492},{20,488},{24,484},{28,48... | collective-permute-start | bytes 884744 | tf_op jit(solution)/shard_map/ppermute | solution.py:252
  38.8 67.7 %collective-permute-start.5 = (bf16[128,1024]{1,0:T(8,128)(2,1)S(1)}, bf16[128,1024]{1,0:T(8,128)(2,1)S(1)}, u32[]{:S(2)}, u32[]{:S(2)}) collective-permute-start(bf16[128,1024]{1,0:T(8,128)(2,1)S(1)} %get-tuple-element.50), channel_id=1, source_target_pairs={{0,508},{4,504},{8,500},{12,496},{16,492},{20,488},{24,484},{28,48... | collective-permute-start | bytes 786440 | tf_op jit(solution)/shard_map/ppermute | solution.py:252
  112.6 15.6 %collective-permute-start.6 = (bf16[144,1024]{1,0:T(8,128)(2,1)S(1)}, bf16[144,1024]{1,0:T(8,128)(2,1)S(1)}, u32[]{:S(2)}, u32[]{:S(2)}) collective-permute-start(bf16[144,1024]{1,0:T(8,128)(2,1)S(1)} %get-tuple-element.26), channel_id=1, source_target_pairs={{0,508},{4,504},{8,500},{12,496},{16,492},{20,488},{24,484},{28,48... | collective-permute-start | bytes 884744 | tf_op jit(solution)/shard_map/ppermute | solution.py:252
  129.2 4.9 %collective-permute-start.7 = (bf16[272,1024]{1,0:T(8,128)(2,1)S(1)}, bf16[272,1024]{1,0:T(8,128)(2,1)S(1)}, u32[]{:S(2)}, u32[]{:S(2)}) collective-permute-start(bf16[272,1024]{1,0:T(8,128)(2,1)S(1)} %get-tuple-element.30), channel_id=1, source_target_pairs={{0,1},{1,0},{2,3},{3,2},{4,5},{5,4},{6,7},{7,6},{8,9},{9,8},{10,11... | collective-permute-start | bytes 1671176 | tf_op jit(solution)/shard_map/ppermute | solution.py:261
  134.3 10.1 %collective-permute-start.8 = (bf16[144,1024]{1,0:T(8,128)(2,1)S(1)}, bf16[144,1024]{1,0:T(8,128)(2,1)S(1)}, u32[]{:S(2)}, u32[]{:S(2)}) collective-permute-start(bf16[144,1024]{1,0:T(8,128)(2,1)S(1)} %get-tuple-element.33), channel_id=1, source_target_pairs={{0,2},{1,3},{2,0},{3,1},{4,6},{5,7},{6,4},{7,5},{8,10},{9,11},{10,... | collective-permute-start | bytes 884744 | tf_op jit(solution)/shard_map/ppermute | solution.py:261

commit v2 on v1

v2 whole, which is shorter than its diff:
```python
import math

import jax
import jax.numpy as jnp
from jax import lax
from jax.experimental import pallas as pl
from jax.experimental.pallas import tpu as pltpu
from jax.sharding import PartitionSpec as P


LANES = 128
HALO = 8
F32 = jnp.float32
BF16 = jnp.bfloat16
HIGHEST = lax.Precision.HIGHEST


def dot(a, b):
    return jnp.dot(a, b, preferred_element_type=F32)


def reversal(size, dtype=BF16):
    rows = lax.broadcasted_iota(jnp.int32, (size, size), 0)
    cols = lax.broadcasted_iota(jnp.int32, (size, size), 1)
    return (rows + cols == size - 1).astype(dtype)


def reverse_lanes(value, precision=None):
    count = value.shape[-1] // LANES
    swap = reversal(LANES, value.dtype)
    parts = []
    for block in reversed(range(count)):
        part = value[:, block * LANES : (block + 1) * LANES]
        parts.append(
            jnp.dot(part, swap, preferred_element_type=F32, precision=precision).astype(value.dtype)
        )
    return jnp.concatenate(parts, axis=1)


def reverse_rows(value):
    return dot(reversal(value.shape[0]), value).astype(value.dtype)


def reverse_both(value):
    return reverse_lanes(reverse_rows(value))


def call(kernel, out_shapes, *operands, scalars=0, scratch=(), flops=0, moved=0):
    specs = [pl.BlockSpec(memory_space=pltpu.SMEM)] * scalars
    specs += [pl.BlockSpec(memory_space=pltpu.VMEM)] * (len(operands) - scalars)
    return pl.pallas_call(
        kernel,
        out_shape=out_shapes,
        in_specs=specs,
        out_specs=[pl.BlockSpec(memory_space=pltpu.VMEM)] * len(out_shapes),
        scratch_shapes=list(scratch),
        cost_estimate=pl.CostEstimate(flops=flops, bytes_accessed=moved, transcendentals=0),
        compiler_params=pltpu.CompilerParams(vmem_limit_bytes=48 * 1024 * 1024),
    )(*operands)


def token_row(ids_ref, mask_ref, strand):
    return jnp.where(mask_ref[strand] == 1, 5, ids_ref[strand]).astype(F32)


def halo_kernel(normed_ref, grad_ref, ids_ref, mask_ref, tails_ref, heads_ref):
    rows = normed_ref.shape[1]
    tails_ref[...] = normed_ref[:, rows - HALO :, :]
    width = grad_ref.shape[2]
    at_row = lax.broadcasted_iota(jnp.int32, (HALO, width), 0) == HALO - 1
    for strand in range(2):
        tokens = token_row(ids_ref, mask_ref, strand)
        tokens = jnp.concatenate([tokens, jnp.zeros((1, width - LANES), F32)], axis=1)
        heads_ref[strand] = jnp.where(at_row, tokens, grad_ref[strand, 0:HALO, :].astype(F32)).astype(BF16)


def pack_kernel(grad_ref, ids_ref, mask_ref, tails_ref, heads_ref, slab_ref):
    rows, width = grad_ref.shape[1], grad_ref.shape[2]
    head = heads_ref[1].astype(F32)
    swap = reversal(HALO, F32)
    tail_rev = jnp.dot(swap, tails_ref[1].astype(F32), preferred_element_type=F32).astype(BF16)
    head_rev = jnp.dot(swap, head, preferred_element_type=F32).astype(BF16)
    own = token_row(ids_ref, mask_ref, 1)
    both = jnp.concatenate([own, head[HALO - 1 : HALO, :LANES], jnp.zeros((6, LANES), F32)], axis=0)
    flipped = dot(both.astype(BF16), reversal(LANES))
    tokens = jnp.concatenate([flipped[0:1], flipped[1:2], jnp.zeros((1, width - 2 * LANES), F32)], axis=1)
    at_row = lax.broadcasted_iota(jnp.int32, (HALO, width), 0) == HALO - 1
    slab_ref[0:HALO, :] = reverse_lanes(head_rev)
    slab_ref[HALO : HALO + rows, :] = reverse_both(grad_ref[1])
    slab_ref[HALO + rows :, :] = jnp.where(at_row, tokens, reverse_lanes(tail_rev).astype(F32)).astype(BF16)


def forward_kernel(place_ref, own_ref, near_ref, other_ref, normed_ref, tails_ref, weight_ref, values_ref):
    shard = own_ref.shape[0]
    half = 4 * shard
    x_lo = place_ref[0] // 2
    core = place_ref[0] % 2
    pieces = (
        (own_ref[...], x_lo, core),
        (near_ref[...], 1 - x_lo, core),
        (other_ref[0:shard, :], x_lo, 1 - core),
        (other_ref[shard:, :], 1 - x_lo, 1 - core),
    )
    for block, chip, at_core in pieces:
        index = chip * 2 + at_core
        weight_ref[pl.ds(pl.multiple_of(index * shard, shard), shard), :] = block
        back = half + (3 - index) * shard
        weight_ref[pl.ds(pl.multiple_of(back, shard), shard), :] = reverse_both(block)
    weight = weight_ref[...]
    values_ref[HALO:, :] = dot(normed_ref[0], weight).astype(BF16).astype(F32)
    values_ref[0:HALO, :] = dot(tails_ref[0], weight).astype(BF16).astype(F32)


def one_hot(row, count):
    classes = lax.broadcasted_iota(jnp.int32, (HALO, count), 0)
    return (row.astype(jnp.int32) == classes).astype(F32)


def rows_of(hot, table):
    return lax.dot_general(
        hot, table, (((0,), (0,)), ((), ())), preferred_element_type=F32, precision=HIGHEST
    )


def near_strand_kernel(
    far_ref, weight_ref, values0_ref, grad_ref, ids_ref, mask_ref, filter_ref, bias_ref,
    values1_ref, conv_grad_ref, mirror_ref, terms_ref,
):
    rows, width = grad_ref.shape[1], grad_ref.shape[2]
    taps = filter_ref.shape[0]
    values1_ref[...] = dot(reverse_both(far_ref[...]), weight_ref[...]).astype(BF16).astype(F32)
    hot = one_hot(token_row(ids_ref, mask_ref, 0), LANES)
    wide = 2 * LANES
    for index in range(width // wide):
        cols = slice(index * wide, (index + 1) * wide)
        weights = filter_ref[:, cols]
        own = grad_ref[0, :, cols].astype(F32)
        gate = jax.nn.sigmoid(values1_ref[:, cols] + rows_of(hot, bias_ref[:, cols]))
        conv_grad = own * gate
        conv_grad_ref[:, cols] = conv_grad
        conv = jnp.zeros((rows, wide), F32)
        for tap in range(taps):
            shifted = values0_ref[HALO - tap : HALO - tap + rows, cols]
            conv = conv + weights[tap : tap + 1] * shifted
            terms_ref[tap : tap + 1, cols] = jnp.sum(conv_grad * shifted, axis=0, keepdims=True)
        pre = own * conv * gate * (1.0 - gate)
        mirror_ref[:, cols] = pre.astype(BF16)
        terms_ref[8:16, cols] = jnp.dot(hot, pre, preferred_element_type=F32, precision=HIGHEST)
    terms_ref[7:8, :] = jnp.zeros((1, width), F32)


def far_strand_kernel(
    slab_ref, weight_ref, values0_ref, values1_ref, mirror_ref, heads_ref,
    filter_rev_ref, bias_ref, bias_rev_ref,
    send_ref, mirror_out_ref, edge_ref,
    wide1, pull1, sums,
):
    rows, width = mirror_ref.shape
    taps = filter_rev_ref.shape[0]
    reach = rows + HALO
    tokens = slab_ref[reach:, :].astype(F32)[HALO - 1 : HALO, :]
    hot_own = one_hot(tokens[:, :LANES], LANES)
    hot_far = one_hot(tokens[:, LANES : 2 * LANES], LANES)
    hot_edge = one_hot(heads_ref[0].astype(F32)[HALO - 1 : HALO, :LANES], LANES)
    edge = dot(slab_ref[reach:, :], weight_ref[...]).astype(BF16).astype(F32)
    edge_gate = jax.nn.sigmoid(edge + rows_of(hot_edge, bias_ref[...])[0:HALO])
    edge_ref[...] = heads_ref[0].astype(F32) * edge_gate
    sums[...] = jnp.zeros_like(sums)
    wide = 2 * LANES
    for index in range(width // wide):
        cols = slice(index * wide, (index + 1) * wide)
        weights = filter_rev_ref[:, cols]
        wide1[0:rows, :] = values1_ref[:, cols]
        wide1[rows:, :] = edge[:, cols]
        own = slab_ref[HALO:reach, cols].astype(F32)
        gate = jax.nn.sigmoid(values0_ref[HALO:, cols] + rows_of(hot_own, bias_rev_ref[:, cols]))
        far_gate = jax.nn.sigmoid(
            values0_ref[0:HALO, cols] + rows_of(hot_far, bias_rev_ref[:, cols])[LANES - HALO :]
        )
        conv_grad = own * gate
        pull1[HALO:, :] = conv_grad
        pull1[0:HALO, :] = slab_ref[0:HALO, cols].astype(F32) * far_gate
        conv = jnp.zeros((rows, wide), F32)
        for tap in range(taps):
            shifted = wide1[tap : tap + rows, :]
            conv = conv + weights[tap : tap + 1] * shifted
            sums[tap : tap + 1, cols] = jnp.sum(conv_grad * shifted, axis=0, keepdims=True)
        pre = own * conv * gate * (1.0 - gate)
        mirror_out_ref[:, cols] = pre.astype(BF16)
        sums[8:16, cols] = jnp.dot(hot_own, pre, preferred_element_type=F32, precision=HIGHEST)
        total = mirror_ref[:, cols].astype(F32)
        for tap in range(taps):
            total = total + weights[tap : tap + 1] * pull1[HALO - tap : HALO - tap + rows, :]
        send_ref[0:rows, cols] = total.astype(BF16)
    send_ref[rows:, :] = sums[...].astype(BF16)


def operands_kernel(
    normed_ref, conv_grad_ref, edge_ref, mirror_ref, filter_ref, left_ref, right_ref, pull0,
):
    rows, width = conv_grad_ref.shape
    half = width // 2
    pull0[0:rows, :] = conv_grad_ref[...]
    pull0[rows:, :] = edge_ref[...]
    for strand in range(2):
        value = normed_ref[strand]
        left_ref[strand * rows : (strand + 1) * rows, :] = value[:, :half]
        left_ref[(2 + strand) * rows : (3 + strand) * rows, :] = reverse_both(value)[:, :half]
    wide = 2 * LANES
    for index in range(width // wide):
        cols = slice(index * wide, (index + 1) * wide)
        total = mirror_ref[:, cols].astype(F32)
        for tap in range(filter_ref.shape[0]):
            total = total + filter_ref[tap : tap + 1, cols] * pull0[tap : tap + rows, cols]
        right_ref[0:rows, cols] = total.astype(BF16)
    right_ref[rows:, :] = reverse_both(right_ref[0:rows, :])


def project_kernel(
    place_ref, scale, left_ref, right_ref, back_ref, terms_ref,
    send_ref, keep_ref, sums_ref, final_ref,
):
    rows = right_ref.shape[0] // 2
    back = back_ref[0:rows, :]
    home = reverse_both(back)
    final_ref[0] = right_ref[0:rows, :]
    final_ref[1] = home
    right = jnp.concatenate([right_ref[0:rows, :], home, right_ref[rows:, :], back], axis=0)
    sums = (terms_ref[...] + reverse_lanes(back_ref[rows:, :]).astype(F32)) * scale
    sums_ref[...] = sums
    core = place_ref[0] % 2
    shard = left_ref.shape[1] // 4
    for chip in range(2):
        for mine in range(2):
            index = chip * 2 + (core if mine else 1 - core)
            left = left_ref[:, pl.ds(pl.multiple_of(index * shard, shard), shard)]
            part = lax.dot_general(left, right, (((0,), (0,)), ((), ())), preferred_element_type=F32) * scale
            if mine:
                keep_ref[chip * shard : (chip + 1) * shard, :] = part
            else:
                send_ref[chip * shard : (chip + 1) * shard, :] = part.astype(BF16)
    send_ref[2 * shard :, :] = sums.astype(BF16)


def input_grad_kernel(value_grad_ref, weight_ref, out_ref):
    weight = weight_ref[...]
    for strand in range(2):
        out_ref[strand] = lax.dot_general(
            value_grad_ref[strand], weight, (((1,), (1,)), ((), ())), preferred_element_type=F32
        ).astype(BF16)


def first_sum_kernel(place_ref, keep_ref, got_ref, sums_ref, send_ref, keep_out_ref, sums_out_ref):
    shard = keep_ref.shape[0] // 2
    x_lo = place_ref[0] // 2
    here = pl.ds(pl.multiple_of(x_lo * shard, shard), shard)
    there = pl.ds(pl.multiple_of((1 - x_lo) * shard, shard), shard)
    keep_out_ref[...] = keep_ref[here, :] + got_ref[here, :].astype(F32)
    send_ref[0:shard, :] = (keep_ref[there, :] + got_ref[there, :].astype(F32)).astype(BF16)
    sums = sums_ref[...] + got_ref[2 * shard :, :].astype(F32)
    sums_out_ref[...] = sums
    send_ref[shard:, :] = sums.astype(BF16)


def last_sum_kernel(place_ref, keep_ref, got_ref, sums_ref, proj_ref, filter_ref, bias_ref):
    shard = keep_ref.shape[0]
    part = filter_ref.shape[2]
    proj_ref[...] = keep_ref[...] + got_ref[0:shard, :].astype(F32)
    cols = pl.ds(pl.multiple_of(place_ref[0] * part, part), part)
    sums = sums_ref[:, cols] + got_ref[shard:, cols].astype(F32)
    for tap in range(filter_ref.shape[0]):
        filter_ref[tap] = sums[tap : tap + 1, :]
    for token in range(bias_ref.shape[0]):
        bias_ref[token] = sums[8 + token : 9 + token, :]


def mirrored(value):
    size = lax.axis_size("ctx")
    return lax.ppermute(value, "ctx", [(i, size - 1 - i) for i in range(size)])


def shifted(value, distance):
    devices = range(lax.axis_size("ctx"))
    return lax.ppermute(value, "ctx", [(i, i + distance) for i in devices if i + distance in devices])


def partner(value, bit):
    return lax.ppermute(value, "fsdp", [(i, i ^ bit) for i in range(lax.axis_size("fsdp"))])


def shape(dims, dtype):
    return jax.ShapeDtypeStruct(dims, dtype)


def step(normed, out_grad, ids, mask, proj_half, conv_filter, gate_bias):
    rows, width = normed.shape[2], normed.shape[3]
    taps = conv_filter.shape[0]
    shard = proj_half.shape[0]
    classes = gate_bias.shape[0]
    normed, out_grad = normed[:, 0], out_grad[:, 0]
    place = lax.axis_index("fsdp").astype(jnp.int32).reshape(1)

    normed_far = mirrored(normed[1])
    tails, heads = call(
        halo_kernel, (shape((2, HALO, width), BF16), shape((2, HALO, width), BF16)),
        normed, out_grad, ids, mask,
        moved=16 * HALO * width,
    )
    heads = shifted(heads, -1)
    tails = shifted(tails, 1)
    near = partner(proj_half, 2)
    slab, = call(
        pack_kernel, (shape((rows + 2 * HALO, width), BF16),),
        out_grad, ids, mask, tails, heads,
        flops=600 * rows * width, moved=4 * rows * width,
    )
    slab = mirrored(slab)
    other = partner(jnp.concatenate([proj_half, near], axis=0), 1)
    filter_rev = conv_filter[:, ::-1]
    bias = jnp.pad(gate_bias, ((0, HALO - classes), (0, 0)))
    bias_rev = bias[:, ::-1]

    weight, values0 = call(
        forward_kernel,
        (shape((width, width), BF16), shape((rows + HALO, width), F32)),
        place, proj_half, near, other, normed, tails, scalars=1,
        flops=2 * rows * width * width, moved=6 * width * width,
    )
    values1, conv_grad, mirror0, terms = call(
        near_strand_kernel,
        (
            shape((rows, width), F32),
            shape((rows, width), F32),
            shape((rows, width), BF16),
            shape((16, width), F32),
        ),
        normed_far, weight, values0, out_grad, ids, mask, conv_filter, bias,
        flops=2 * rows * width * width, moved=8 * width * width,
    )
    wide = 2 * LANES
    send, mirror1, edge = call(
        far_strand_kernel,
        (shape((rows + 16, width), BF16), shape((rows, width), BF16), shape((HALO, width), F32)),
        slab, weight, values0, values1, mirror0, heads, filter_rev, bias, bias_rev,
        scratch=[pltpu.VMEM((rows + HALO, wide), F32)] * 2 + [pltpu.VMEM((16, width), F32)],
        flops=2 * rows * width * width, moved=8 * width * width,
    )
    back = mirrored(send)
    left, right = call(
        operands_kernel, (shape((4 * rows, width // 2), BF16), shape((2 * rows, width), BF16)),
        normed, conv_grad, edge, mirror1, conv_filter,
        scratch=[pltpu.VMEM((rows + HALO, width), F32)],
        flops=rows * width * width, moved=16 * rows * width,
    )
    grad_scale = 1.0 / math.sqrt(2.0 * lax.axis_size("fsdp") * rows)
    send1, keep1, sums1, final = call(
        lambda place_ref, *refs: project_kernel(place_ref, grad_scale, *refs),
        (
            shape((2 * shard + 16, width), BF16),
            shape((2 * shard, width), F32),
            shape((16, width), F32),
            shape((2, rows, width), BF16),
        ),
        place, left, right, back, terms, scalars=1,
        flops=4 * rows * width * width, moved=4 * width * width,
    )
    got1 = partner(send1, 1)
    send2, keep2, sums2 = call(
        first_sum_kernel,
        (shape((shard + 16, width), BF16), shape((shard, width), F32), shape((16, width), F32)),
        place, keep1, got1, sums1, scalars=1, moved=16 * shard * width,
    )
    got2 = partner(send2, 2)
    in_grad, = call(
        input_grad_kernel, (shape((2, rows, width), BF16),), final, weight,
        flops=4 * rows * width * width, moved=4 * width * width,
    )
    part = width // lax.axis_size("fsdp")
    proj_grad, filter_grad, bias_grad = call(
        last_sum_kernel,
        (shape((shard, width), F32), shape((taps, 1, part), F32), shape((classes, 1, part), F32)),
        place, keep2, got2, sums2, scalars=1, moved=12 * shard * width,
    )
    return (
        in_grad[:, None],
        proj_grad[None],
        jnp.transpose(filter_grad, (1, 0, 2)),
        jnp.transpose(bias_grad, (1, 0, 2)),
    )


def solution(mesh):
    placed = (
        P(None, "fsdp", "ctx", None),
        P(None, "fsdp", "ctx", None),
        P(None, "fsdp", "ctx"),
        P(None, "fsdp", "ctx"),
        P("fsdp", None),
        P(),
        P(),
    )
    return jax.shard_map(
        step,
        mesh=mesh,
        in_specs=placed,
        out_specs=(
            P(None, "fsdp", "ctx", None),
            P("ctx", "fsdp", None),
            P("ctx", None, "fsdp"),
            P("ctx", None, "fsdp"),
        ),
        check_vma=False,
    )
```

time: 147 us -> 153 us (1.041)
  the two profiles are of different devices: /device:TPU:1 before, /device:TPU:4 now
where the time goes in v2:
time: 153 us
  waiting for transfers between devices  83.2 us (54%)
  starting transfers between devices  47.8 us (31%)
  Pallas kernels  14.6 us (10%)
  local copies, waits for them, and re-layouts  4.64 us (3%)
  other arithmetic  1.78 us (1%)
    ppermute x3, waiting for transfers between devices, mirrored(): return lax.ppermute(value, 'ctx', [(i, size - 1 - i) for i in range(size)])  67.1 us
    ppermute x3, starting transfers between devices, mirrored(): return lax.ppermute(value, 'ctx', [(i, size - 1 - i) for i in range(size)])  28.1 us
    pallas_call x10, Pallas kernels, call(): pl.pallas_call(kernel, out_shape=out_shapes, in_specs=specs, out_specs=[p...  14.6 us
    ppermute x4, waiting for transfers between devices, partner(): lax.ppermute(value, 'fsdp', [(i, i ^ bit) for i in range(lax.axis_size('f...  14.5 us
    ppermute x4, starting transfers between devices, partner(): lax.ppermute(value, 'fsdp', [(i, i ^ bit) for i in range(lax.axis_size('f...  10.2 us
    ppermute x2, starting transfers between devices, shifted(): lax.ppermute(value, 'ctx', [(i, i + distance) for i in devices if i + dis...  9.59 us
    unnamed x22, local copies, waits for them, and re-layouts  3.47 us
  transfers between devices with their start and end apart: 9, of which 6 were waited for; matrix products, arithmetic and copies ran while one was open for 1% of the time, Pallas kernels for 6%

profile of v2, /device:TPU:4, one launch (start us, length us, event | category | flops | bytes accessed | tf_op | source)
XLA Modules:
  0.0 152.9 jit_solution(2618438222460917827)
XLA Ops:
  0.6 0.0 copy-start.1
  0.6 0.0 copy-start.3
  0.7 3.2 %collective-permute-start.1 = (bf16[128,1024]{1,0:T(8,128)(2,1)}, bf16[128,1024]{1,0:T(8,128)(2,1)S(1)}, u32[]{:S(2)}, u32[]{:S(2)}) collective-permute-start(bf16[128,1024]{1,0:T(8,128)(2,1)} %own_ref.1), channel_id=1, source_target_pairs={{0,2},{1,3},{2,0},{3,1},{4,6},{5,7},{6,4},{7,5},{8,10},{9,11},{10,... | collective-permute-start | bytes 786440 | tf_op jit(solution)/shard_map/ppermute | solution.py:288
  3.9 7.0 %collective-permute-done.1.near_ref = bf16[128,1024]{1,0:T(8,128)(2,1)S(1)} collective-permute-done((bf16[128,1024]{1,0:T(8,128)(2,1)}, bf16[128,1024]{1,0:T(8,128)(2,1)S(1)}, u32[]{:S(2)}, u32[]{:S(2)}) %collective-permute-start.1) | collective-permute-done | bytes 262176 | tf_op jit(solution)/shard_map/ppermute | solution.py:288
  10.9 1.8 %pad_maximum_fusion = bf16[256,1024]{1,0:T(8,128)(2,1)} fusion(bf16[128,1024]{1,0:T(8,128)(2,1)S(1)} %collective-permute-done.1.near_ref, bf16[128,1024]{1,0:T(8,128)(2,1)} %own_ref.1), kind=kLoop, calls=%fused_computation | loop fusion | flops 1048576 | bytes 1048576 | tf_op jit(solution)/shard_map/concatenate | solution.py:318
  12.7 1.9 %collective-permute-start.2 = (bf16[256,1024]{1,0:T(8,128)(2,1)}, bf16[256,1024]{1,0:T(8,128)(2,1)S(1)}, u32[]{:S(2)}, u32[]{:S(2)}) collective-permute-start(bf16[256,1024]{1,0:T(8,128)(2,1)} %pad_maximum_fusion), channel_id=1, source_target_pairs={{0,1},{1,0},{2,3},{3,2},{4,5},{5,4},{6,7},{7,6},{8,9},{9,8},{10,11... | collective-permute-start | bytes 1572872 | tf_op jit(solution)/shard_map/ppermute | solution.py:288
  14.6 0.0 copy-start
  14.6 1.0 copy-done
  15.7 0.0 copy-start.2
  15.7 1.0 copy-done.2
  16.7 0.0 copy-start.6
  16.7 0.7 copy-done.6
  17.4 0.0 copy-start.8
  17.4 0.7 copy-done.8
  18.1 0.0 copy-start.10
  18.1 0.0 copy-start.5
  18.1 0.0 copy-start.4
  18.1 0.0 copy-start.7
  18.1 0.0 copy-start.9
  18.1 3.6 %collective-permute-start.3 = (bf16[2,8,1024]{2,1,0:T(8,128)(2,1)S(1)}, bf16[2,8,1024]{2,1,0:T(8,128)(2,1)S(1)}, u32[]{:S(2)}, u32[]{:S(2)}) collective-permute-start(bf16[2,8,1024]{2,1,0:T(8,128)(2,1)S(1)} %get-tuple-element.27), channel_id=1, source_target_pairs={{0,4},{4,8},{8,12},{12,16},{16,20},{20,24},{24,28},{28,32},{32,36}... | collective-permute-start | bytes 98312 | tf_op jit(solution)/shard_map/ppermute | solution.py:284
  21.7 6.0 %collective-permute-start.4 = (bf16[2,8,1024]{2,1,0:T(8,128)(2,1)S(1)}, bf16[2,8,1024]{2,1,0:T(8,128)(2,1)S(1)}, u32[]{:S(2)}, u32[]{:S(2)}) collective-permute-start(bf16[2,8,1024]{2,1,0:T(8,128)(2,1)S(1)} %get-tuple-element.31), channel_id=1, source_target_pairs={{4,0},{8,4},{12,8},{16,12},{20,16},{24,20},{28,24},{32,28},{36,32}... | collective-permute-start | bytes 98312 | tf_op jit(solution)/shard_map/ppermute | solution.py:284
  27.7 0.0 collective-permute-done.3.tails_ref
  27.7 1.6 %collective-permute-done.4.heads_ref = bf16[2,8,1024]{2,1,0:T(8,128)(2,1)S(1)} collective-permute-done((bf16[2,8,1024]{2,1,0:T(8,128)(2,1)S(1)}, bf16[2,8,1024]{2,1,0:T(8,128)(2,1)S(1)}, u32[]{:S(2)}, u32[]{:S(2)}) %collective-permute-start.4) | collective-permute-done | bytes 32800 | tf_op jit(solution)/shard_map/ppermute | solution.py:284
  29.3 0.0 copy-done.3
  29.3 0.6 shard_map.105
  29.9 16.8 %collective-permute-start.5 = (bf16[144,1024]{1,0:T(8,128)(2,1)S(1)}, bf16[144,1024]{1,0:T(8,128)(2,1)S(1)}, u32[]{:S(2)}, u32[]{:S(2)}) collective-permute-start(bf16[144,1024]{1,0:T(8,128)(2,1)S(1)} %shard_map.105), channel_id=1, source_target_pairs={{0,508},{4,504},{8,500},{12,496},{16,492},{20,488},{24,484},{28,48... | collective-permute-start | bytes 884744 | tf_op jit(solution)/shard_map/ppermute | solution.py:279
  46.7 0.0 copy-done.1
  46.8 1.9 %collective-permute-start = (bf16[128,1024]{1,0:T(8,128)(2,1)S(1)}, bf16[128,1024]{1,0:T(8,128)(2,1)S(1)}, u32[]{:S(2)}, u32[]{:S(2)}) collective-permute-start(bf16[128,1024]{1,0:T(8,128)(2,1)S(1)} %slice_bitcast_fusion), channel_id=1, source_target_pairs={{0,508},{4,504},{8,500},{12,496},{16,492},{20,488},{24,484},{28,48... | collective-permute-start | bytes 786440 | tf_op jit(solution)/shard_map/ppermute | solution.py:279
  48.7 0.0 copy-done.10
  48.7 0.6 rev.7.bias_rev_ref
  49.3 0.0 copy-done.5
  49.3 0.6 rev.6.filter_rev_ref
  49.9 0.0 collective-permute-done.2.other_ref
  49.9 0.0 copy-done.4
  49.9 1.9 %shard_map.103 = (bf16[1024,1024]{1,0:T(8,128)(2,1)S(1)}, f32[136,1024]{1,0:T(8,128)S(1)}) custom-call(s32[1]{0:T(128)} %bitcast.place_ref, bf16[128,1024]{1,0:T(8,128)(2,1)S(1)} %copy-done.4, bf16[128,1024]{1,0:T(8,128)(2,1)S(1)} %collective-permute-done.1.near_ref, bf16[256,1024]{1,0:T(8,128)(2,1)S(1)} %collective-permute-done.2.other_ref, ...), custom_call_target="tpu_custom_call" | custom-call | flops 268435456 | bytes 6291456 | tf_op jit(solution)/shard_map/pallas_call | solution.py:51
  51.8 61.5 %collective-permute-done.far_ref = bf16[128,1024]{1,0:T(8,128)(2,1)S(1)} collective-permute-done((bf16[128,1024]{1,0:T(8,128)(2,1)S(1)}, bf16[128,1024]{1,0:T(8,128)(2,1)S(1)}, u32[]{:S(2)}, u32[]{:S(2)}) %collective-permute-start) | collective-permute-done | bytes 262176 | tf_op jit(solution)/shard_map/ppermute | solution.py:279
  113.3 0.0 copy-done.7
  113.3 0.0 copy-done.9
  113.3 3.3 %shard_map.104 = (f32[128,1024]{1,0:T(8,128)S(1)}, f32[128,1024]{1,0:T(8,128)S(1)}, bf16[128,1024]{1,0:T(8,128)(2,1)S(1)}, f32[16,1024]{1,0:T(8,128)S(1)}) custom-call(bf16[128,1024]{1,0:T(8,128)(2,1)S(1)} %collective-permute-done.far_ref, bf16[1024,1024]{1,0:T(8,128)(2,1)S(1)} %get-tuple-element.28.weight_ref, ...), custom_call_target="tpu_custom_call" | custom-call | flops 268435456 | bytes 8388608 | tf_op jit(solution)/shard_map/pallas_call | solution.py:51
  116.6 0.0 collective-permute-done.5.slab_ref
  116.6 3.3 %shard_map.106 = (bf16[144,1024]{1,0:T(8,128)(2,1)S(1)}, bf16[128,1024]{1,0:T(8,128)(2,1)S(1)}, f32[8,1024]{1,0:T(8,128)S(1)}) custom-call(bf16[144,1024]{1,0:T(8,128)(2,1)S(1)} %collective-permute-done.5.slab_ref, bf16[1024,1024]{1,0:T(8,128)(2,1)S(1)} %get-tuple-element.28.weight_ref, f32[136,1024]{1,0:T(8,128)S(1)} %get-tuple-element.29.values0_ref, ...), custom_call_target="tpu_custom_call" | custom-call | flops 268435456 | bytes 8388608 | tf_op jit(solution)/shard_map/pallas_call | solution.py:51
  120.0 9.4 %collective-permute-start.6 = (bf16[144,1024]{1,0:T(8,128)(2,1)S(1)}, bf16[144,1024]{1,0:T(8,128)(2,1)S(1)}, u32[]{:S(2)}, u32[]{:S(2)}) collective-permute-start(bf16[144,1024]{1,0:T(8,128)(2,1)S(1)} %get-tuple-element.38), channel_id=1, source_target_pairs={{0,508},{4,504},{8,500},{12,496},{16,492},{20,488},{24,484},{28,48... | collective-permute-start | bytes 884744 | tf_op jit(solution)/shard_map/ppermute | solution.py:279
  129.3 1.2 shard_map.107
  130.5 5.6 %collective-permute-done.6.refs_2_ = bf16[144,1024]{1,0:T(8,128)(2,1)S(1)} collective-permute-done((bf16[144,1024]{1,0:T(8,128)(2,1)S(1)}, bf16[144,1024]{1,0:T(8,128)(2,1)S(1)}, u32[]{:S(2)}, u32[]{:S(2)}) %collective-permute-start.6) | collective-permute-done | bytes 294944 | tf_op jit(solution)/shard_map/ppermute | solution.py:279
  136.1 1.1 shard_map.108
  137.1 1.9 %collective-permute-start.7 = (bf16[272,1024]{1,0:T(8,128)(2,1)S(1)}, bf16[272,1024]{1,0:T(8,128)(2,1)S(1)}, u32[]{:S(2)}, u32[]{:S(2)}) collective-permute-start(bf16[272,1024]{1,0:T(8,128)(2,1)S(1)} %get-tuple-element.42), channel_id=1, source_target_pairs={{0,1},{1,0},{2,3},{3,2},{4,5},{5,4},{6,7},{7,6},{8,9},{9,8},{10,11... | collective-permute-start | bytes 1671176 | tf_op jit(solution)/shard_map/ppermute | solution.py:288
  139.1 1.9 %collective-permute-done.7.got_ref = bf16[272,1024]{1,0:T(8,128)(2,1)S(1)} collective-permute-done((bf16[272,1024]{1,0:T(8,128)(2,1)S(1)}, bf16[272,1024]{1,0:T(8,128)(2,1)S(1)}, u32[]{:S(2)}, u32[]{:S(2)}) %collective-permute-start.7) | collective-permute-done | bytes 557088 | tf_op jit(solution)/shard_map/ppermute | solution.py:288
  141.0 0.1 shard_map.110
  141.1 3.1 %collective-permute-start.8 = (bf16[144,1024]{1,0:T(8,128)(2,1)S(1)}, bf16[144,1024]{1,0:T(8,128)(2,1)S(1)}, u32[]{:S(2)}, u32[]{:S(2)}) collective-permute-start(bf16[144,1024]{1,0:T(8,128)(2,1)S(1)} %get-tuple-element.45), channel_id=1, source_target_pairs={{0,2},{1,3},{2,0},{3,1},{4,6},{5,7},{6,4},{7,5},{8,10},{9,11},{10,... | collective-permute-start | bytes 884744 | tf_op jit(solution)/shard_map/ppermute | solution.py:288
  144.2 2.3 %shard_map.109 = bf16[2,128,1024]{2,1,0:T(8,128)(2,1)} custom-call(bf16[2,128,1024]{2,1,0:T(8,128)(2,1)S(1)} %get-tuple-element.40.value_grad_ref, bf16[1024,1024]{1,0:T(8,128)(2,1)S(1)} %get-tuple-element.28.weight_ref), custom_call_target="tpu_custom_call" | custom-call | flops 536870912 | bytes 4194304 | tf_op jit(solution)/shard_map/pallas_call | solution.py:51
  146.5 5.6 %collective-permute-done.8.got_ref = bf16[144,1024]{1,0:T(8,128)(2,1)S(1)} collective-permute-done((bf16[144,1024]{1,0:T(8,128)(2,1)S(1)}, bf16[144,1024]{1,0:T(8,128)(2,1)S(1)}, u32[]{:S(2)}, u32[]{:S(2)}) %collective-permute-start.8) | collective-permute-done | bytes 294944 | tf_op jit(solution)/shard_map/ppermute | solution.py:288
  152.0 0.8 shard_map.111
  (3 shorter events, 0.0 us)
Async XLA Ops:
  0.6 46.1 %copy-start.1 = (bf16[2,1,128,1024]{3,2,1,0:T(8,128)(2,1)S(1)}, bf16[2,1,128,1024]{3,2,1,0:T(8,128)(2,1)}, u32[]{:S(2)}) copy-start(bf16[2,1,128,1024]{3,2,1,0:T(8,128)(2,1)} %param.7) | copy-start | bytes 1572868
  0.6 28.7 %copy-start.3 = (bf16[2,1,128,1024]{3,2,1,0:T(8,128)(2,1)S(1)}, bf16[2,1,128,1024]{3,2,1,0:T(8,128)(2,1)}, u32[]{:S(2)}) copy-start(bf16[2,1,128,1024]{3,2,1,0:T(8,128)(2,1)} %param.8) | copy-start | bytes 1572868
  0.7 10.3 %collective-permute-start.1 = (bf16[128,1024]{1,0:T(8,128)(2,1)}, bf16[128,1024]{1,0:T(8,128)(2,1)S(1)}, u32[]{:S(2)}, u32[]{:S(2)}) collective-permute-start(bf16[128,1024]{1,0:T(8,128)(2,1)} %own_ref.1), channel_id=1, source_target_pairs={{0,2},{1,3},{2,0},{3,1},{4,6},{5,7},{6,4},{7,5},{8,10},{9,11},{10,... | collective-permute-start | bytes 786440 | tf_op jit(solution)/shard_map/ppermute | solution.py:288
  12.7 37.1 %collective-permute-start.2 = (bf16[256,1024]{1,0:T(8,128)(2,1)}, bf16[256,1024]{1,0:T(8,128)(2,1)S(1)}, u32[]{:S(2)}, u32[]{:S(2)}) collective-permute-start(bf16[256,1024]{1,0:T(8,128)(2,1)} %pad_maximum_fusion), channel_id=1, source_target_pairs={{0,1},{1,0},{2,3},{3,2},{4,5},{5,4},{6,7},{7,6},{8,9},{9,8},{10,11... | collective-permute-start | bytes 1572872 | tf_op jit(solution)/shard_map/ppermute | solution.py:288
  14.6 1.0 copy-start
  15.7 1.0 copy-start.2
  16.7 0.7 copy-start.6
  17.4 0.7 copy-start.8
  18.1 30.6 %copy-start.10 = (f32[6,1024]{1,0:T(8,128)S(1)}, f32[6,1024]{1,0:T(8,128)}, u32[]{:S(2)}) copy-start(f32[6,1024]{1,0:T(8,128)} %param.13) | copy-start | bytes 73732
  18.1 31.2 %copy-start.5 = (f32[7,1024]{1,0:T(8,128)S(1)}, f32[7,1024]{1,0:T(8,128)}, u32[]{:S(2)}) copy-start(f32[7,1024]{1,0:T(8,128)} %filter_ref.3) | copy-start | bytes 86020
  18.1 31.8 %copy-start.4 = (bf16[128,1024]{1,0:T(8,128)(2,1)S(1)}, bf16[128,1024]{1,0:T(8,128)(2,1)}, u32[]{:S(2)}) copy-start(bf16[128,1024]{1,0:T(8,128)(2,1)} %own_ref.1) | copy-start | bytes 786436
  18.1 95.3 %copy-start.7 = (s32[2,1,128]{2,1,0:T(1,128)S(1)}, s32[2,1,128]{2,1,0:T(1,128)}, u32[]{:S(2)}) copy-start(s32[2,1,128]{2,1,0:T(1,128)} %ids_ref.5) | copy-start | bytes 3076
  18.1 95.3 %copy-start.9 = (s32[2,1,128]{2,1,0:T(1,128)S(1)}, s32[2,1,128]{2,1,0:T(1,128)}, u32[]{:S(2)}) copy-start(s32[2,1,128]{2,1,0:T(1,128)} %mask_ref.5) | copy-start | bytes 3076
  18.1 9.6 %collective-permute-start.3 = (bf16[2,8,1024]{2,1,0:T(8,128)(2,1)S(1)}, bf16[2,8,1024]{2,1,0:T(8,128)(2,1)S(1)}, u32[]{:S(2)}, u32[]{:S(2)}) collective-permute-start(bf16[2,8,1024]{2,1,0:T(8,128)(2,1)S(1)} %get-tuple-element.27), channel_id=1, source_target_pairs={{0,4},{4,8},{8,12},{12,16},{16,20},{20,24},{24,28},{28,32},{32,36}... | collective-permute-start | bytes 98312 | tf_op jit(solution)/shard_map/ppermute | solution.py:284
  21.7 7.6 %collective-permute-start.4 = (bf16[2,8,1024]{2,1,0:T(8,128)(2,1)S(1)}, bf16[2,8,1024]{2,1,0:T(8,128)(2,1)S(1)}, u32[]{:S(2)}, u32[]{:S(2)}) collective-permute-start(bf16[2,8,1024]{2,1,0:T(8,128)(2,1)S(1)} %get-tuple-element.31), channel_id=1, source_target_pairs={{4,0},{8,4},{12,8},{16,12},{20,16},{24,20},{28,24},{32,28},{36,32}... | collective-permute-start | bytes 98312 | tf_op jit(solution)/shard_map/ppermute | solution.py:284
  29.9 86.7 %collective-permute-start.5 = (bf16[144,1024]{1,0:T(8,128)(2,1)S(1)}, bf16[144,1024]{1,0:T(8,128)(2,1)S(1)}, u32[]{:S(2)}, u32[]{:S(2)}) collective-permute-start(bf16[144,1024]{1,0:T(8,128)(2,1)S(1)} %shard_map.105), channel_id=1, source_target_pairs={{0,508},{4,504},{8,500},{12,496},{16,492},{20,488},{24,484},{28,48... | collective-permute-start | bytes 884744 | tf_op jit(solution)/shard_map/ppermute | solution.py:279
  46.8 66.6 %collective-permute-start = (bf16[128,1024]{1,0:T(8,128)(2,1)S(1)}, bf16[128,1024]{1,0:T(8,128)(2,1)S(1)}, u32[]{:S(2)}, u32[]{:S(2)}) collective-permute-start(bf16[128,1024]{1,0:T(8,128)(2,1)S(1)} %slice_bitcast_fusion), channel_id=1, source_target_pairs={{0,508},{4,504},{8,500},{12,496},{16,492},{20,488},{24,484},{28,48... | collective-permute-start | bytes 786440 | tf_op jit(solution)/shard_map/ppermute | solution.py:279
  120.0 16.1 %collective-permute-start.6 = (bf16[144,1024]{1,0:T(8,128)(2,1)S(1)}, bf16[144,1024]{1,0:T(8,128)(2,1)S(1)}, u32[]{:S(2)}, u32[]{:S(2)}) collective-permute-start(bf16[144,1024]{1,0:T(8,128)(2,1)S(1)} %get-tuple-element.38), channel_id=1, source_target_pairs={{0,508},{4,504},{8,500},{12,496},{16,492},{20,488},{24,484},{28,48... | collective-permute-start | bytes 884744 | tf_op jit(solution)/shard_map/ppermute | solution.py:279
  137.1 3.9 %collective-permute-start.7 = (bf16[272,1024]{1,0:T(8,128)(2,1)S(1)}, bf16[272,1024]{1,0:T(8,128)(2,1)S(1)}, u32[]{:S(2)}, u32[]{:S(2)}) collective-permute-start(bf16[272,1024]{1,0:T(8,128)(2,1)S(1)} %get-tuple-element.42), channel_id=1, source_target_pairs={{0,1},{1,0},{2,3},{3,2},{4,5},{5,4},{6,7},{7,6},{8,9},{9,8},{10,11... | collective-permute-start | bytes 1671176 | tf_op jit(solution)/shard_map/ppermute | solution.py:288
  141.1 10.9 %collective-permute-start.8 = (bf16[144,1024]{1,0:T(8,128)(2,1)S(1)}, bf16[144,1024]{1,0:T(8,128)(2,1)S(1)}, u32[]{:S(2)}, u32[]{:S(2)}) collective-permute-start(bf16[144,1024]{1,0:T(8,128)(2,1)S(1)} %get-tuple-element.45), channel_id=1, source_target_pairs={{0,2},{1,3},{2,0},{3,1},{4,6},{5,7},{6,4},{7,5},{8,10},{9,11},{10,... | collective-permute-start | bytes 884744 | tf_op jit(solution)/shard_map/ppermute | solution.py:288

commit v3 on v2

--- a/solution.py
+++ b/solution.py
@@ -74,8 +74,15 @@
         heads_ref[strand] = jnp.where(at_row, tokens, grad_ref[strand, 0:HALO, :].astype(F32)).astype(BF16)
 
 
-def pack_kernel(grad_ref, ids_ref, mask_ref, tails_ref, heads_ref, slab_ref):
-    rows, width = grad_ref.shape[1], grad_ref.shape[2]
+def flip_kernel(grad_ref, out_ref, block, arrived):
+    copy = pltpu.make_async_copy(grad_ref.at[1], block, arrived)
+    copy.start()
+    copy.wait()
+    out_ref[...] = reverse_both(block[...])
+
+
+def edge_kernel(ids_ref, mask_ref, tails_ref, heads_ref, slab_ref):
+    width = slab_ref.shape[1]
     head = heads_ref[1].astype(F32)
     swap = reversal(HALO, F32)
     tail_rev = jnp.dot(swap, tails_ref[1].astype(F32), preferred_element_type=F32).astype(BF16)
@@ -86,8 +93,7 @@
     tokens = jnp.concatenate([flipped[0:1], flipped[1:2], jnp.zeros((1, width - 2 * LANES), F32)], axis=1)
     at_row = lax.broadcasted_iota(jnp.int32, (HALO, width), 0) == HALO - 1
     slab_ref[0:HALO, :] = reverse_lanes(head_rev)
-    slab_ref[HALO : HALO + rows, :] = reverse_both(grad_ref[1])
-    slab_ref[HALO + rows :, :] = jnp.where(at_row, tokens, reverse_lanes(tail_rev).astype(F32)).astype(BF16)
+    slab_ref[HALO:, :] = jnp.where(at_row, tokens, reverse_lanes(tail_rev).astype(F32)).astype(BF16)
 
 
 def forward_kernel(place_ref, own_ref, near_ref, other_ref, normed_ref, tails_ref, weight_ref, values_ref):
@@ -150,19 +156,18 @@
 
 
 def far_strand_kernel(
-    slab_ref, weight_ref, values0_ref, values1_ref, mirror_ref, heads_ref,
+    slab_ref, halo_ref, weight_ref, values0_ref, values1_ref, mirror_ref, heads_ref,
     filter_rev_ref, bias_ref, bias_rev_ref,
     send_ref, mirror_out_ref, edge_ref,
     wide1, pull1, sums,
 ):
     rows, width = mirror_ref.shape
     taps = filter_rev_ref.shape[0]
-    reach = rows + HALO
-    tokens = slab_ref[reach:, :].astype(F32)[HALO - 1 : HALO, :]
+    tokens = halo_ref[HALO:, :].astype(F32)[HALO - 1 : HALO, :]
     hot_own = one_hot(tokens[:, :LANES], LANES)
     hot_far = one_hot(tokens[:, LANES : 2 * LANES], LANES)
     hot_edge = one_hot(heads_ref[0].astype(F32)[HALO - 1 : HALO, :LANES], LANES)
-    edge = dot(slab_ref[reach:, :], weight_ref[...]).astype(BF16).astype(F32)
+    edge = dot(halo_ref[HALO:, :], weight_ref[...]).astype(BF16).astype(F32)
     edge_gate = jax.nn.sigmoid(edge + rows_of(hot_edge, bias_ref[...])[0:HALO])
     edge_ref[...] = heads_ref[0].astype(F32) * edge_gate
     sums[...] = jnp.zeros_like(sums)
@@ -172,14 +177,14 @@
         weights = filter_rev_ref[:, cols]
         wide1[0:rows, :] = values1_ref[:, cols]
         wide1[rows:, :] = edge[:, cols]
-        own = slab_ref[HALO:reach, cols].astype(F32)
+        own = slab_ref[:, cols].astype(F32)
         gate = jax.nn.sigmoid(values0_ref[HALO:, cols] + rows_of(hot_own, bias_rev_ref[:, cols]))
         far_gate = jax.nn.sigmoid(
             values0_ref[0:HALO, cols] + rows_of(hot_far, bias_rev_ref[:, cols])[LANES - HALO :]
         )
         conv_grad = own * gate
         pull1[HALO:, :] = conv_grad
-        pull1[0:HALO, :] = slab_ref[0:HALO, cols].astype(F32) * far_gate
+        pull1[0:HALO, :] = halo_ref[0:HALO, cols].astype(F32) * far_gate
         conv = jnp.zeros((rows, wide), F32)
         for tap in range(taps):
             shifted = wide1[tap : tap + rows, :]
@@ -292,6 +297,19 @@
     return jax.ShapeDtypeStruct(dims, dtype)
 
 
+def flipped_strand(out_grad):
+    rows, width = out_grad.shape[1:]
+    return pl.pallas_call(
+        flip_kernel,
+        out_shape=shape((rows, width), BF16),
+        in_specs=[pl.BlockSpec(memory_space=pl.ANY)],
+        out_specs=pl.BlockSpec(memory_space=pltpu.VMEM),
+        scratch_shapes=[pltpu.VMEM((rows, width), BF16), pltpu.SemaphoreType.DMA],
+        cost_estimate=pl.CostEstimate(flops=600 * rows * width, bytes_accessed=4 * rows * width, transcendentals=0),
+        compiler_params=pltpu.CompilerParams(vmem_limit_bytes=48 * 1024 * 1024),
+    )(out_grad)
+
+
 def step(normed, out_grad, ids, mask, proj_half, conv_filter, gate_bias):
     rows, width = normed.shape[2], normed.shape[3]
     taps = conv_filter.shape[0]
@@ -301,6 +319,7 @@
     place = lax.axis_index("fsdp").astype(jnp.int32).reshape(1)
 
     normed_far = mirrored(normed[1])
+    slab = mirrored(flipped_strand(out_grad))
     tails, heads = call(
         halo_kernel, (shape((2, HALO, width), BF16), shape((2, HALO, width), BF16)),
         normed, out_grad, ids, mask,
@@ -309,12 +328,11 @@
     heads = shifted(heads, -1)
     tails = shifted(tails, 1)
     near = partner(proj_half, 2)
-    slab, = call(
-        pack_kernel, (shape((rows + 2 * HALO, width), BF16),),
-        out_grad, ids, mask, tails, heads,
-        flops=600 * rows * width, moved=4 * rows * width,
-    )
-    slab = mirrored(slab)
+    halo, = call(
+        edge_kernel, (shape((2 * HALO, width), BF16),), ids, mask, tails, heads,
+        flops=600 * HALO * width, moved=8 * HALO * width,
+    )
+    halo = mirrored(halo)
     other = partner(jnp.concatenate([proj_half, near], axis=0), 1)
     filter_rev = conv_filter[:, ::-1]
     bias = jnp.pad(gate_bias, ((0, HALO - classes), (0, 0)))
@@ -341,7 +359,7 @@
     send, mirror1, edge = call(
         far_strand_kernel,
         (shape((rows + 16, width), BF16), shape((rows, width), BF16), shape((HALO, width), F32)),
-        slab, weight, values0, values1, mirror0, heads, filter_rev, bias, bias_rev,
+        slab, halo, weight, values0, values1, mirror0, heads, filter_rev, bias, bias_rev,
         scratch=[pltpu.VMEM((rows + HALO, wide), F32)] * 2 + [pltpu.VMEM((16, width), F32)],
         flops=2 * rows * width * width, moved=8 * width * width,
     )

time: 153 us -> 139 us (0.908)
  the two profiles are of different devices: /device:TPU:4 before, /device:TPU:254 now
where the time goes in v3:
time: 139 us; the launch traced here: 138 us
  waiting for transfers between devices  81 us (58%)
  starting transfers between devices  36.7 us (26%)
  Pallas kernels  14.8 us (11%)
  local copies, waits for them, and re-layouts  3.19 us (2%)
  other arithmetic  1.78 us (1%)
    ppermute x2, waiting for transfers between devices, shifted(): lax.ppermute(value, 'ctx', [(i, i + distance) for i in devices if i + dis...  36 us
    ppermute x4, waiting for transfers between devices, mirrored(): return lax.ppermute(value, 'ctx', [(i, size - 1 - i) for i in range(size)])  29 us
    ppermute x4, starting transfers between devices, mirrored(): return lax.ppermute(value, 'ctx', [(i, size - 1 - i) for i in range(size)])  20.5 us
    ppermute x4, waiting for transfers between devices, partner(): lax.ppermute(value, 'fsdp', [(i, i ^ bit) for i in range(lax.axis_size('f...  16.1 us
    pallas_call x10, Pallas kernels, call(): pl.pallas_call(kernel, out_shape=out_shapes, in_specs=specs, out_specs=[p...  14.4 us
    ppermute x4, starting transfers between devices, partner(): lax.ppermute(value, 'fsdp', [(i, i ^ bit) for i in range(lax.axis_size('f...  8.75 us
    ppermute x2, starting transfers between devices, shifted(): lax.ppermute(value, 'ctx', [(i, i + distance) for i in devices if i + dis...  7.46 us
  transfers between devices with their start and end apart: 10, of which 7 were waited for; matrix products, arithmetic and copies ran while one was open for 2% of the time, Pallas kernels for 7%

profile of v3, /device:TPU:254, one launch (start us, length us, event | category | flops | bytes accessed | tf_op | source)
XLA Modules:
  0.0 138.4 jit_solution(13388351239479435541)
XLA Ops:
  0.6 0.0 copy-start.3
  0.6 0.0 copy-start
  0.7 0.0 copy-start.6
  0.7 0.0 copy-start.5
  0.7 0.0 copy-start.7
  0.7 0.0 copy-start.4
  0.7 2.9 %collective-permute-start.1 = (bf16[128,1024]{1,0:T(8,128)(2,1)}, bf16[128,1024]{1,0:T(8,128)(2,1)S(1)}, u32[]{:S(2)}, u32[]{:S(2)}) collective-permute-start(bf16[128,1024]{1,0:T(8,128)(2,1)} %own_ref.1), channel_id=1, source_target_pairs={{0,2},{1,3},{2,0},{3,1},{4,6},{5,7},{6,4},{7,5},{8,10},{9,11},{10,... | collective-permute-start | bytes 786440 | tf_op jit(solution)/shard_map/ppermute | solution.py:293
  3.6 7.4 %collective-permute-done.1.near_ref = bf16[128,1024]{1,0:T(8,128)(2,1)S(1)} collective-permute-done((bf16[128,1024]{1,0:T(8,128)(2,1)}, bf16[128,1024]{1,0:T(8,128)(2,1)S(1)}, u32[]{:S(2)}, u32[]{:S(2)}) %collective-permute-start.1) | collective-permute-done | bytes 262176 | tf_op jit(solution)/shard_map/ppermute | solution.py:293
  11.0 1.8 %pad_maximum_fusion = bf16[256,1024]{1,0:T(8,128)(2,1)} fusion(bf16[128,1024]{1,0:T(8,128)(2,1)S(1)} %collective-permute-done.1.near_ref, bf16[128,1024]{1,0:T(8,128)(2,1)} %own_ref.1), kind=kLoop, calls=%fused_computation | loop fusion | flops 1048576 | bytes 1048576 | tf_op jit(solution)/shard_map/concatenate | solution.py:336
  12.8 0.0 copy-start.2
  12.8 2.0 %collective-permute-start.2 = (bf16[256,1024]{1,0:T(8,128)(2,1)}, bf16[256,1024]{1,0:T(8,128)(2,1)S(1)}, u32[]{:S(2)}, u32[]{:S(2)}) collective-permute-start(bf16[256,1024]{1,0:T(8,128)(2,1)} %pad_maximum_fusion), channel_id=1, source_target_pairs={{0,1},{1,0},{2,3},{3,2},{4,5},{5,4},{6,7},{7,6},{8,9},{9,8},{10,11... | collective-permute-start | bytes 1572872 | tf_op jit(solution)/shard_map/ppermute | solution.py:293
  14.8 1.0 slice_bitcast_fusion
  15.8 5.5 %collective-permute-start = (bf16[128,1024]{1,0:T(8,128)(2,1)S(1)}, bf16[128,1024]{1,0:T(8,128)(2,1)S(1)}, u32[]{:S(2)}, u32[]{:S(2)}) collective-permute-start(bf16[128,1024]{1,0:T(8,128)(2,1)S(1)} %slice_bitcast_fusion), channel_id=1, source_target_pairs={{0,508},{4,504},{8,500},{12,496},{16,492},{20,488},{24,484},{28,48... | collective-permute-start | bytes 786440 | tf_op jit(solution)/shard_map/ppermute | solution.py:284
  21.3 0.0 copy-start.1
  21.3 1.0 copy-done.1
  22.4 0.4 shard_map.105
  22.8 6.0 %collective-permute-start.4 = (bf16[128,1024]{1,0:T(8,128)(2,1)S(1)}, bf16[128,1024]{1,0:T(8,128)(2,1)S(1)}, u32[]{:S(2)}, u32[]{:S(2)}) collective-permute-start(bf16[128,1024]{1,0:T(8,128)(2,1)S(1)} %shard_map.105), channel_id=1, source_target_pairs={{0,508},{4,504},{8,500},{12,496},{16,492},{20,488},{24,484},{28,48... | collective-permute-start | bytes 786440 | tf_op jit(solution)/shard_map/ppermute | solution.py:284
  28.9 0.0 copy-done
  28.9 0.0 copy-done.6
  28.9 0.0 copy-done.5
  28.9 5.5 %collective-permute-start.3 = (bf16[2,8,1024]{2,1,0:T(8,128)(2,1)S(1)}, bf16[2,8,1024]{2,1,0:T(8,128)(2,1)S(1)}, u32[]{:S(2)}, u32[]{:S(2)}) collective-permute-start(bf16[2,8,1024]{2,1,0:T(8,128)(2,1)S(1)} %get-tuple-element.27), channel_id=1, source_target_pairs={{0,4},{4,8},{8,12},{12,16},{16,20},{20,24},{24,28},{28,32},{32,36}... | collective-permute-start | bytes 98312 | tf_op jit(solution)/shard_map/ppermute | solution.py:289
  34.4 1.9 %collective-permute-start.5 = (bf16[2,8,1024]{2,1,0:T(8,128)(2,1)S(1)}, bf16[2,8,1024]{2,1,0:T(8,128)(2,1)S(1)}, u32[]{:S(2)}, u32[]{:S(2)}) collective-permute-start(bf16[2,8,1024]{2,1,0:T(8,128)(2,1)S(1)} %get-tuple-element.31), channel_id=1, source_target_pairs={{4,0},{8,4},{12,8},{16,12},{20,16},{24,20},{28,24},{32,28},{36,32}... | collective-permute-start | bytes 98312 | tf_op jit(solution)/shard_map/ppermute | solution.py:289
  36.4 0.0 copy-done.7
  36.4 0.6 rev.7.bias_rev_ref
  37.0 0.0 copy-done.4
  37.0 0.6 rev.6.filter_rev_ref
  37.6 31.4 %collective-permute-done.3.tails_ref = bf16[2,8,1024]{2,1,0:T(8,128)(2,1)S(1)} collective-permute-done((bf16[2,8,1024]{2,1,0:T(8,128)(2,1)S(1)}, bf16[2,8,1024]{2,1,0:T(8,128)(2,1)S(1)}, u32[]{:S(2)}, u32[]{:S(2)}) %collective-permute-start.3) | collective-permute-done | bytes 32800 | tf_op jit(solution)/shard_map/ppermute | solution.py:289
  69.0 4.6 %collective-permute-done.5.heads_ref = bf16[2,8,1024]{2,1,0:T(8,128)(2,1)S(1)} collective-permute-done((bf16[2,8,1024]{2,1,0:T(8,128)(2,1)S(1)}, bf16[2,8,1024]{2,1,0:T(8,128)(2,1)S(1)}, u32[]{:S(2)}, u32[]{:S(2)}) %collective-permute-start.5) | collective-permute-done | bytes 32800 | tf_op jit(solution)/shard_map/ppermute | solution.py:289
  73.5 0.4 shard_map.106
  73.9 5.5 %collective-permute-start.6 = (bf16[16,1024]{1,0:T(8,128)(2,1)S(1)}, bf16[16,1024]{1,0:T(8,128)(2,1)S(1)}, u32[]{:S(2)}, u32[]{:S(2)}) collective-permute-start(bf16[16,1024]{1,0:T(8,128)(2,1)S(1)} %shard_map.106), channel_id=1, source_target_pairs={{0,508},{4,504},{8,500},{12,496},{16,492},{20,488},{24,484},{28,48... | collective-permute-start | bytes 98312 | tf_op jit(solution)/shard_map/ppermute | solution.py:284
  79.4 0.0 collective-permute-done.2.other_ref
  79.5 0.0 copy-done.3
  79.5 1.9 %shard_map.103 = (bf16[1024,1024]{1,0:T(8,128)(2,1)S(1)}, f32[136,1024]{1,0:T(8,128)S(1)}) custom-call(s32[1]{0:T(128)} %bitcast.place_ref, bf16[128,1024]{1,0:T(8,128)(2,1)S(1)} %copy-done.3, bf16[128,1024]{1,0:T(8,128)(2,1)S(1)} %collective-permute-done.1.near_ref, bf16[256,1024]{1,0:T(8,128)(2,1)S(1)} %collective-permute-done.2.other_ref, ...), custom_call_target="tpu_custom_call" | custom-call | flops 268435456 | bytes 6291456 | tf_op jit(solution)/shard_map/pallas_call | solution.py:51
  81.4 0.0 collective-permute-done.far_ref
  81.4 0.0 copy-done.2
  81.4 3.3 %shard_map.104 = (f32[128,1024]{1,0:T(8,128)S(1)}, f32[128,1024]{1,0:T(8,128)S(1)}, bf16[128,1024]{1,0:T(8,128)(2,1)S(1)}, f32[16,1024]{1,0:T(8,128)S(1)}) custom-call(bf16[128,1024]{1,0:T(8,128)(2,1)S(1)} %collective-permute-done.far_ref, bf16[1024,1024]{1,0:T(8,128)(2,1)S(1)} %get-tuple-element.28.weight_ref, ...), custom_call_target="tpu_custom_call" | custom-call | flops 268435456 | bytes 8388608 | tf_op jit(solution)/shard_map/pallas_call | solution.py:51
  84.7 16.9 %collective-permute-done.6.halo_ref = bf16[16,1024]{1,0:T(8,128)(2,1)S(1)} collective-permute-done((bf16[16,1024]{1,0:T(8,128)(2,1)S(1)}, bf16[16,1024]{1,0:T(8,128)(2,1)S(1)}, u32[]{:S(2)}, u32[]{:S(2)}) %collective-permute-start.6) | collective-permute-done | bytes 32800 | tf_op jit(solution)/shard_map/ppermute | solution.py:284
  101.6 0.0 collective-permute-done.4.slab_ref
  101.6 3.3 %shard_map.107 = (bf16[144,1024]{1,0:T(8,128)(2,1)S(1)}, bf16[128,1024]{1,0:T(8,128)(2,1)S(1)}, f32[8,1024]{1,0:T(8,128)S(1)}) custom-call(bf16[128,1024]{1,0:T(8,128)(2,1)S(1)} %collective-permute-done.4.slab_ref, bf16[16,1024]{1,0:T(8,128)(2,1)S(1)} %collective-permute-done.6.halo_ref, bf16[1024,1024]{1,0:T(8,128)(2,1)S(1)} %get-tuple-element.28.weight_ref, ...), custom_call_target="tpu_custom_call" | custom-call | flops 268435456 | bytes 8388608 | tf_op jit(solution)/shard_map/pallas_call | solution.py:51
  104.9 3.4 %collective-permute-start.7 = (bf16[144,1024]{1,0:T(8,128)(2,1)S(1)}, bf16[144,1024]{1,0:T(8,128)(2,1)S(1)}, u32[]{:S(2)}, u32[]{:S(2)}) collective-permute-start(bf16[144,1024]{1,0:T(8,128)(2,1)S(1)} %get-tuple-element.38), channel_id=1, source_target_pairs={{0,508},{4,504},{8,500},{12,496},{16,492},{20,488},{24,484},{28,48... | collective-permute-start | bytes 884744 | tf_op jit(solution)/shard_map/ppermute | solution.py:284
  108.3 1.2 shard_map.108
  109.5 12.1 %collective-permute-done.7.refs_2_ = bf16[144,1024]{1,0:T(8,128)(2,1)S(1)} collective-permute-done((bf16[144,1024]{1,0:T(8,128)(2,1)S(1)}, bf16[144,1024]{1,0:T(8,128)(2,1)S(1)}, u32[]{:S(2)}, u32[]{:S(2)}) %collective-permute-start.7) | collective-permute-done | bytes 294944 | tf_op jit(solution)/shard_map/ppermute | solution.py:284
  121.6 1.1 shard_map.109
  122.6 1.9 %collective-permute-start.8 = (bf16[272,1024]{1,0:T(8,128)(2,1)S(1)}, bf16[272,1024]{1,0:T(8,128)(2,1)S(1)}, u32[]{:S(2)}, u32[]{:S(2)}) collective-permute-start(bf16[272,1024]{1,0:T(8,128)(2,1)S(1)} %get-tuple-element.42), channel_id=1, source_target_pairs={{0,1},{1,0},{2,3},{3,2},{4,5},{5,4},{6,7},{7,6},{8,9},{9,8},{10,11... | collective-permute-start | bytes 1671176 | tf_op jit(solution)/shard_map/ppermute | solution.py:293
  124.6 1.9 %collective-permute-done.8.got_ref = bf16[272,1024]{1,0:T(8,128)(2,1)S(1)} collective-permute-done((bf16[272,1024]{1,0:T(8,128)(2,1)S(1)}, bf16[272,1024]{1,0:T(8,128)(2,1)S(1)}, u32[]{:S(2)}, u32[]{:S(2)}) %collective-permute-start.8) | collective-permute-done | bytes 557088 | tf_op jit(solution)/shard_map/ppermute | solution.py:293
  126.5 0.1 shard_map.111
  126.6 1.9 %collective-permute-start.9 = (bf16[144,1024]{1,0:T(8,128)(2,1)S(1)}, bf16[144,1024]{1,0:T(8,128)(2,1)S(1)}, u32[]{:S(2)}, u32[]{:S(2)}) collective-permute-start(bf16[144,1024]{1,0:T(8,128)(2,1)S(1)} %get-tuple-element.45), channel_id=1, source_target_pairs={{0,2},{1,3},{2,0},{3,1},{4,6},{5,7},{6,4},{7,5},{8,10},{9,11},{10,... | collective-permute-start | bytes 884744 | tf_op jit(solution)/shard_map/ppermute | solution.py:293
  128.5 2.3 %shard_map.110 = bf16[2,128,1024]{2,1,0:T(8,128)(2,1)} custom-call(bf16[2,128,1024]{2,1,0:T(8,128)(2,1)S(1)} %get-tuple-element.40.value_grad_ref, bf16[1024,1024]{1,0:T(8,128)(2,1)S(1)} %get-tuple-element.28.weight_ref), custom_call_target="tpu_custom_call" | custom-call | flops 536870912 | bytes 4194304 | tf_op jit(solution)/shard_map/pallas_call | solution.py:51
  130.8 6.7 %collective-permute-done.9.got_ref = bf16[144,1024]{1,0:T(8,128)(2,1)S(1)} collective-permute-done((bf16[144,1024]{1,0:T(8,128)(2,1)S(1)}, bf16[144,1024]{1,0:T(8,128)(2,1)S(1)}, u32[]{:S(2)}, u32[]{:S(2)}) %collective-permute-start.9) | collective-permute-done | bytes 294944 | tf_op jit(solution)/shard_map/ppermute | solution.py:293
  137.5 0.8 shard_map.112
  (2 shorter events, 0.0 us)
Async XLA Ops:
  0.6 78.8 %copy-start.3 = (bf16[128,1024]{1,0:T(8,128)(2,1)S(1)}, bf16[128,1024]{1,0:T(8,128)(2,1)}, u32[]{:S(2)}) copy-start(bf16[128,1024]{1,0:T(8,128)(2,1)} %own_ref.1) | copy-start | bytes 786436
  0.6 28.2 %copy-start = (bf16[2,1,128,1024]{3,2,1,0:T(8,128)(2,1)S(1)}, bf16[2,1,128,1024]{3,2,1,0:T(8,128)(2,1)}, u32[]{:S(2)}) copy-start(bf16[2,1,128,1024]{3,2,1,0:T(8,128)(2,1)} %param.7) | copy-start | bytes 1572868
  0.7 28.2 %copy-start.6 = (s32[2,1,128]{2,1,0:T(1,128)S(1)}, s32[2,1,128]{2,1,0:T(1,128)}, u32[]{:S(2)}) copy-start(s32[2,1,128]{2,1,0:T(1,128)} %mask_ref.5) | copy-start | bytes 3076
  0.7 28.2 %copy-start.5 = (s32[2,1,128]{2,1,0:T(1,128)S(1)}, s32[2,1,128]{2,1,0:T(1,128)}, u32[]{:S(2)}) copy-start(s32[2,1,128]{2,1,0:T(1,128)} %ids_ref.5) | copy-start | bytes 3076
  0.7 35.7 %copy-start.7 = (f32[6,1024]{1,0:T(8,128)S(1)}, f32[6,1024]{1,0:T(8,128)}, u32[]{:S(2)}) copy-start(f32[6,1024]{1,0:T(8,128)} %param.13) | copy-start | bytes 73732
  0.7 36.3 %copy-start.4 = (f32[7,1024]{1,0:T(8,128)S(1)}, f32[7,1024]{1,0:T(8,128)}, u32[]{:S(2)}) copy-start(f32[7,1024]{1,0:T(8,128)} %filter_ref.3) | copy-start | bytes 86020
  0.7 10.3 %collective-permute-start.1 = (bf16[128,1024]{1,0:T(8,128)(2,1)}, bf16[128,1024]{1,0:T(8,128)(2,1)S(1)}, u32[]{:S(2)}, u32[]{:S(2)}) collective-permute-start(bf16[128,1024]{1,0:T(8,128)(2,1)} %own_ref.1), channel_id=1, source_target_pairs={{0,2},{1,3},{2,0},{3,1},{4,6},{5,7},{6,4},{7,5},{8,10},{9,11},{10,... | collective-permute-start | bytes 786440 | tf_op jit(solution)/shard_map/ppermute | solution.py:293
  12.8 68.6 %copy-start.2 = (bf16[2,1,128,1024]{3,2,1,0:T(8,128)(2,1)S(1)}, bf16[2,1,128,1024]{3,2,1,0:T(8,128)(2,1)}, u32[]{:S(2)}) copy-start(bf16[2,1,128,1024]{3,2,1,0:T(8,128)(2,1)} %param.8) | copy-start | bytes 1572868
  12.8 66.7 %collective-permute-start.2 = (bf16[256,1024]{1,0:T(8,128)(2,1)}, bf16[256,1024]{1,0:T(8,128)(2,1)S(1)}, u32[]{:S(2)}, u32[]{:S(2)}) collective-permute-start(bf16[256,1024]{1,0:T(8,128)(2,1)} %pad_maximum_fusion), channel_id=1, source_target_pairs={{0,1},{1,0},{2,3},{3,2},{4,5},{5,4},{6,7},{7,6},{8,9},{9,8},{10,11... | collective-permute-start | bytes 1572872 | tf_op jit(solution)/shard_map/ppermute | solution.py:293
  15.8 65.6 %collective-permute-start = (bf16[128,1024]{1,0:T(8,128)(2,1)S(1)}, bf16[128,1024]{1,0:T(8,128)(2,1)S(1)}, u32[]{:S(2)}, u32[]{:S(2)}) collective-permute-start(bf16[128,1024]{1,0:T(8,128)(2,1)S(1)} %slice_bitcast_fusion), channel_id=1, source_target_pairs={{0,508},{4,504},{8,500},{12,496},{16,492},{20,488},{24,484},{28,48... | collective-permute-start | bytes 786440 | tf_op jit(solution)/shard_map/ppermute | solution.py:284
  21.3 1.0 copy-start.1
  22.8 78.8 %collective-permute-start.4 = (bf16[128,1024]{1,0:T(8,128)(2,1)S(1)}, bf16[128,1024]{1,0:T(8,128)(2,1)S(1)}, u32[]{:S(2)}, u32[]{:S(2)}) collective-permute-start(bf16[128,1024]{1,0:T(8,128)(2,1)S(1)} %shard_map.105), channel_id=1, source_target_pairs={{0,508},{4,504},{8,500},{12,496},{16,492},{20,488},{24,484},{28,48... | collective-permute-start | bytes 786440 | tf_op jit(solution)/shard_map/ppermute | solution.py:284
  28.9 40.1 %collective-permute-start.3 = (bf16[2,8,1024]{2,1,0:T(8,128)(2,1)S(1)}, bf16[2,8,1024]{2,1,0:T(8,128)(2,1)S(1)}, u32[]{:S(2)}, u32[]{:S(2)}) collective-permute-start(bf16[2,8,1024]{2,1,0:T(8,128)(2,1)S(1)} %get-tuple-element.27), channel_id=1, source_target_pairs={{0,4},{4,8},{8,12},{12,16},{16,20},{20,24},{24,28},{28,32},{32,36}... | collective-permute-start | bytes 98312 | tf_op jit(solution)/shard_map/ppermute | solution.py:289
  34.4 39.1 %collective-permute-start.5 = (bf16[2,8,1024]{2,1,0:T(8,128)(2,1)S(1)}, bf16[2,8,1024]{2,1,0:T(8,128)(2,1)S(1)}, u32[]{:S(2)}, u32[]{:S(2)}) collective-permute-start(bf16[2,8,1024]{2,1,0:T(8,128)(2,1)S(1)} %get-tuple-element.31), channel_id=1, source_target_pairs={{4,0},{8,4},{12,8},{16,12},{20,16},{24,20},{28,24},{32,28},{36,32}... | collective-permute-start | bytes 98312 | tf_op jit(solution)/shard_map/ppermute | solution.py:289
  73.9 27.7 %collective-permute-start.6 = (bf16[16,1024]{1,0:T(8,128)(2,1)S(1)}, bf16[16,1024]{1,0:T(8,128)(2,1)S(1)}, u32[]{:S(2)}, u32[]{:S(2)}) collective-permute-start(bf16[16,1024]{1,0:T(8,128)(2,1)S(1)} %shard_map.106), channel_id=1, source_target_pairs={{0,508},{4,504},{8,500},{12,496},{16,492},{20,488},{24,484},{28,48... | collective-permute-start | bytes 98312 | tf_op jit(solution)/shard_map/ppermute | solution.py:284
  104.9 16.6 %collective-permute-start.7 = (bf16[144,1024]{1,0:T(8,128)(2,1)S(1)}, bf16[144,1024]{1,0:T(8,128)(2,1)S(1)}, u32[]{:S(2)}, u32[]{:S(2)}) collective-permute-start(bf16[144,1024]{1,0:T(8,128)(2,1)S(1)} %get-tuple-element.38), channel_id=1, source_target_pairs={{0,508},{4,504},{8,500},{12,496},{16,492},{20,488},{24,484},{28,48... | collective-permute-start | bytes 884744 | tf_op jit(solution)/shard_map/ppermute | solution.py:284
  122.6 3.9 %collective-permute-start.8 = (bf16[272,1024]{1,0:T(8,128)(2,1)S(1)}, bf16[272,1024]{1,0:T(8,128)(2,1)S(1)}, u32[]{:S(2)}, u32[]{:S(2)}) collective-permute-start(bf16[272,1024]{1,0:T(8,128)(2,1)S(1)} %get-tuple-element.42), channel_id=1, source_target_pairs={{0,1},{1,0},{2,3},{3,2},{4,5},{5,4},{6,7},{7,6},{8,9},{9,8},{10,11... | collective-permute-start | bytes 1671176 | tf_op jit(solution)/shard_map/ppermute | solution.py:293
  126.6 10.9 %collective-permute-start.9 = (bf16[144,1024]{1,0:T(8,128)(2,1)S(1)}, bf16[144,1024]{1,0:T(8,128)(2,1)S(1)}, u32[]{:S(2)}, u32[]{:S(2)}) collective-permute-start(bf16[144,1024]{1,0:T(8,128)(2,1)S(1)} %get-tuple-element.45), channel_id=1, source_target_pairs={{0,2},{1,3},{2,0},{3,1},{4,6},{5,7},{6,4},{7,5},{8,10},{9,11},{10,... | collective-permute-start | bytes 884744 | tf_op jit(solution)/shard_map/ppermute | solution.py:293

commit v4 on v3

--- a/solution.py
+++ b/solution.py
@@ -63,22 +63,37 @@
     return jnp.where(mask_ref[strand] == 1, 5, ids_ref[strand]).astype(F32)
 
 
-def halo_kernel(normed_ref, grad_ref, ids_ref, mask_ref, tails_ref, heads_ref):
-    rows = normed_ref.shape[1]
-    tails_ref[...] = normed_ref[:, rows - HALO :, :]
-    width = grad_ref.shape[2]
+def lead_kernel(
+    normed_ref, grad_ref, ids_ref, mask_ref, send_ref, tails_ref, heads_ref, far_ref,
+    head, ids, mask, arrived,
+):
+    rows, width = send_ref.shape
+    copies = [
+        pltpu.make_async_copy(source, target, arrived.at[place])
+        for place, (source, target) in enumerate(
+            (
+                (normed_ref.at[1], send_ref),
+                (normed_ref.at[:, rows - HALO : rows, :], tails_ref),
+                (grad_ref.at[:, 0:HALO, :], head),
+                (grad_ref.at[1], far_ref),
+                (ids_ref, ids),
+                (mask_ref, mask),
+            )
+        )
+    ]
+    for copy in copies:
+        copy.start()
+    for copy in copies:
+        copy.wait()
     at_row = lax.broadcasted_iota(jnp.int32, (HALO, width), 0) == HALO - 1
     for strand in range(2):
-        tokens = token_row(ids_ref, mask_ref, strand)
+        tokens = token_row(ids, mask, strand)
         tokens = jnp.concatenate([tokens, jnp.zeros((1, width - LANES), F32)], axis=1)
-        heads_ref[strand] = jnp.where(at_row, tokens, grad_ref[strand, 0:HALO, :].astype(F32)).astype(BF16)
-
-
-def flip_kernel(grad_ref, out_ref, block, arrived):
-    copy = pltpu.make_async_copy(grad_ref.at[1], block, arrived)
-    copy.start()
-    copy.wait()
-    out_ref[...] = reverse_both(block[...])
+        heads_ref[strand] = jnp.where(at_row, tokens, head[strand].astype(F32)).astype(BF16)
+
+
+def flip_kernel(grad_ref, out_ref):
+    out_ref[...] = reverse_both(grad_ref[...])
 
 
 def edge_kernel(ids_ref, mask_ref, tails_ref, heads_ref, slab_ref):
@@ -297,19 +312,6 @@
     return jax.ShapeDtypeStruct(dims, dtype)
 
 
-def flipped_strand(out_grad):
-    rows, width = out_grad.shape[1:]
-    return pl.pallas_call(
-        flip_kernel,
-        out_shape=shape((rows, width), BF16),
-        in_specs=[pl.BlockSpec(memory_space=pl.ANY)],
-        out_specs=pl.BlockSpec(memory_space=pltpu.VMEM),
-        scratch_shapes=[pltpu.VMEM((rows, width), BF16), pltpu.SemaphoreType.DMA],
-        cost_estimate=pl.CostEstimate(flops=600 * rows * width, bytes_accessed=4 * rows * width, transcendentals=0),
-        compiler_params=pltpu.CompilerParams(vmem_limit_bytes=48 * 1024 * 1024),
-    )(out_grad)
-
-
 def step(normed, out_grad, ids, mask, proj_half, conv_filter, gate_bias):
     rows, width = normed.shape[2], normed.shape[3]
     taps = conv_filter.shape[0]
@@ -318,15 +320,31 @@
     normed, out_grad = normed[:, 0], out_grad[:, 0]
     place = lax.axis_index("fsdp").astype(jnp.int32).reshape(1)
 
-    normed_far = mirrored(normed[1])
-    slab = mirrored(flipped_strand(out_grad))
-    tails, heads = call(
-        halo_kernel, (shape((2, HALO, width), BF16), shape((2, HALO, width), BF16)),
-        normed, out_grad, ids, mask,
-        moved=16 * HALO * width,
-    )
+    send, tails, heads, far_grad = pl.pallas_call(
+        lead_kernel,
+        out_shape=(
+            shape((rows, width), BF16),
+            shape((2, HALO, width), BF16),
+            shape((2, HALO, width), BF16),
+            shape((rows, width), BF16),
+        ),
+        in_specs=[pl.BlockSpec(memory_space=pltpu.HBM)] * 4,
+        out_specs=[pl.BlockSpec(memory_space=pltpu.VMEM)] * 4,
+        scratch_shapes=[
+            pltpu.VMEM((2, HALO, width), BF16),
+            pltpu.VMEM((2, 1, rows), jnp.int32),
+            pltpu.VMEM((2, 1, rows), jnp.int32),
+            pltpu.SemaphoreType.DMA((6,)),
+        ],
+        cost_estimate=pl.CostEstimate(flops=0, bytes_accessed=4 * rows * width, transcendentals=0),
+    )(normed, out_grad, ids, mask)
+    normed_far = mirrored(send)
     heads = shifted(heads, -1)
     tails = shifted(tails, 1)
+    far_grad, = call(
+        flip_kernel, (shape((rows, width), BF16),), far_grad, flops=600 * rows * width, moved=4 * rows * width,
+    )
+    slab = mirrored(far_grad)
     near = partner(proj_half, 2)
     halo, = call(
         edge_kernel, (shape((2 * HALO, width), BF16),), ids, mask, tails, heads,

time: 139 us -> 140 us (level)
  Pallas kernels: 14.8 us -> 16.7 us
    pallas_call x1, Pallas kernels: 0.44 us -> 1.93 us  [step(): pl.pallas_call(lead_kernel, out_shape=(shape((rows, width), BF16), shape(...]
  transfers between devices with their start and end apart: 10 -> 10, of which waited for: 7 -> 7; matrix products, arithmetic and copies ran while one was open for 2% -> 1% of each run, Pallas kernels for 7% -> 8%
where the time goes in v4:
time: 140 us; the launch traced here: 139 us
  waiting for transfers between devices  81.1 us (58%)
  starting transfers between devices  36.6 us (26%)
  Pallas kernels  16.7 us (12%)
  local copies, waits for them, and re-layouts  2.13 us (2%)
  other arithmetic  1.78 us (1%)
    ppermute x2, waiting for transfers between devices, shifted(): lax.ppermute(value, 'ctx', [(i, i + distance) for i in devices if i + dis...  36.4 us
    ppermute x4, waiting for transfers between devices, mirrored(): return lax.ppermute(value, 'ctx', [(i, size - 1 - i) for i in range(size)])  28.7 us
    ppermute x4, starting transfers between devices, mirrored(): return lax.ppermute(value, 'ctx', [(i, size - 1 - i) for i in range(size)])  20.5 us
    ppermute x4, waiting for transfers between devices, partner(): lax.ppermute(value, 'fsdp', [(i, i ^ bit) for i in range(lax.axis_size('f...  16.1 us
    pallas_call x10, Pallas kernels, call(): pl.pallas_call(kernel, out_shape=out_shapes, in_specs=specs, out_specs=[p...  14.8 us
    ppermute x4, starting transfers between devices, partner(): lax.ppermute(value, 'fsdp', [(i, i ^ bit) for i in range(lax.axis_size('f...  8.62 us
    ppermute x2, starting transfers between devices, shifted(): lax.ppermute(value, 'ctx', [(i, i + distance) for i in devices if i + dis...  7.46 us
  transfers between devices with their start and end apart: 10, of which 7 were waited for; matrix products, arithmetic and copies ran while one was open for 1% of the time, Pallas kernels for 8%

profile of v4, /device:TPU:254, one launch (start us, length us, event | category | flops | bytes accessed | tf_op | source)
XLA Modules:
  0.0 139.1 jit_solution(4625582714258765908)
XLA Ops:
  0.6 0.0 copy-start.2
  0.6 0.0 copy-start.6
  0.7 0.0 copy-start.5
  0.7 0.0 copy-start.1
  0.7 0.0 copy-start
  0.7 0.0 copy-start.7
  0.7 0.0 copy-start.3
  0.7 2.9 %collective-permute-start.1 = (bf16[128,1024]{1,0:T(8,128)(2,1)}, bf16[128,1024]{1,0:T(8,128)(2,1)S(1)}, u32[]{:S(2)}, u32[]{:S(2)}) collective-permute-start(bf16[128,1024]{1,0:T(8,128)(2,1)} %own_ref.1), channel_id=1, source_target_pairs={{0,2},{1,3},{2,0},{3,1},{4,6},{5,7},{6,4},{7,5},{8,10},{9,11},{10,... | collective-permute-start | bytes 786440 | tf_op jit(solution)/shard_map/ppermute | solution.py:308
  3.6 7.4 %collective-permute-done.1.near_ref = bf16[128,1024]{1,0:T(8,128)(2,1)S(1)} collective-permute-done((bf16[128,1024]{1,0:T(8,128)(2,1)}, bf16[128,1024]{1,0:T(8,128)(2,1)S(1)}, u32[]{:S(2)}, u32[]{:S(2)}) %collective-permute-start.1) | collective-permute-done | bytes 262176 | tf_op jit(solution)/shard_map/ppermute | solution.py:308
  11.0 1.8 %pad_maximum_fusion = bf16[256,1024]{1,0:T(8,128)(2,1)} fusion(bf16[128,1024]{1,0:T(8,128)(2,1)S(1)} %collective-permute-done.1.near_ref, bf16[128,1024]{1,0:T(8,128)(2,1)} %own_ref.1), kind=kLoop, calls=%fused_computation | loop fusion | flops 1048576 | bytes 1048576 | tf_op jit(solution)/shard_map/concatenate | solution.py:354
  12.8 1.9 %collective-permute-start.2 = (bf16[256,1024]{1,0:T(8,128)(2,1)}, bf16[256,1024]{1,0:T(8,128)(2,1)S(1)}, u32[]{:S(2)}, u32[]{:S(2)}) collective-permute-start(bf16[256,1024]{1,0:T(8,128)(2,1)} %pad_maximum_fusion), channel_id=1, source_target_pairs={{0,1},{1,0},{2,3},{3,2},{4,5},{5,4},{6,7},{7,6},{8,9},{9,8},{10,11... | collective-permute-start | bytes 1572872 | tf_op jit(solution)/shard_map/ppermute | solution.py:308
  14.7 1.9 %shard_map.102 = (bf16[128,1024]{1,0:T(8,128)(2,1)}, bf16[2,8,1024]{2,1,0:T(8,128)(2,1)}, bf16[2,8,1024]{2,1,0:T(8,128)(2,1)}, bf16[128,1024]{1,0:T(8,128)(2,1)}) custom-call(bf16[2,128,1024]{2,1,0:T(8,128)(2,1)} %bitcast.9, bf16[2,128,1024]{2,1,0:T(8,128)(2,1)} %bitcast.12, s32[2,1,128]{2,1,0:T(1,128)} %ids_ref.5, s32[2,1,128]{2,1,0:T(1,128)} %mask_ref.5), custom_call_target="tpu_custom_call" | custom-call | bytes 524288 | tf_op jit(solution)/shard_map/pallas_call | solution.py:323
  16.6 5.5 %collective-permute-start = (bf16[128,1024]{1,0:T(8,128)(2,1)}, bf16[128,1024]{1,0:T(8,128)(2,1)S(1)}, u32[]{:S(2)}, u32[]{:S(2)}) collective-permute-start(bf16[128,1024]{1,0:T(8,128)(2,1)} %get-tuple-element.29), channel_id=1, source_target_pairs={{0,508},{4,504},{8,500},{12,496},{16,492},{20,488},{24,484},{28,48... | collective-permute-start | bytes 786440 | tf_op jit(solution)/shard_map/ppermute | solution.py:299
  22.2 0.0 copy-start.4
  22.2 0.9 copy-done.4
  23.1 0.4 shard_map.105
  23.5 6.0 %collective-permute-start.4 = (bf16[128,1024]{1,0:T(8,128)(2,1)S(1)}, bf16[128,1024]{1,0:T(8,128)(2,1)S(1)}, u32[]{:S(2)}, u32[]{:S(2)}) collective-permute-start(bf16[128,1024]{1,0:T(8,128)(2,1)S(1)} %shard_map.105), channel_id=1, source_target_pairs={{0,508},{4,504},{8,500},{12,496},{16,492},{20,488},{24,484},{28,48... | collective-permute-start | bytes 786440 | tf_op jit(solution)/shard_map/ppermute | solution.py:299
  29.6 5.5 %collective-permute-start.3 = (bf16[2,8,1024]{2,1,0:T(8,128)(2,1)}, bf16[2,8,1024]{2,1,0:T(8,128)(2,1)S(1)}, u32[]{:S(2)}, u32[]{:S(2)}) collective-permute-start(bf16[2,8,1024]{2,1,0:T(8,128)(2,1)} %get-tuple-element.30), channel_id=1, source_target_pairs={{0,4},{4,8},{8,12},{12,16},{16,20},{20,24},{24,28},{28,32},{32,36}... | collective-permute-start | bytes 98312 | tf_op jit(solution)/shard_map/ppermute | solution.py:304
  35.1 1.9 %collective-permute-start.5 = (bf16[2,8,1024]{2,1,0:T(8,128)(2,1)}, bf16[2,8,1024]{2,1,0:T(8,128)(2,1)S(1)}, u32[]{:S(2)}, u32[]{:S(2)}) collective-permute-start(bf16[2,8,1024]{2,1,0:T(8,128)(2,1)} %get-tuple-element.35), channel_id=1, source_target_pairs={{4,0},{8,4},{12,8},{16,12},{20,16},{24,20},{28,24},{32,28},{36,32}... | collective-permute-start | bytes 98312 | tf_op jit(solution)/shard_map/ppermute | solution.py:304
  37.0 0.0 copy-done.7
  37.1 0.6 rev.7.bias_rev_ref
  37.7 0.0 copy-done.3
  37.7 0.6 rev.6.filter_rev_ref
  38.2 31.9 %collective-permute-done.3.tails_ref = bf16[2,8,1024]{2,1,0:T(8,128)(2,1)S(1)} collective-permute-done((bf16[2,8,1024]{2,1,0:T(8,128)(2,1)}, bf16[2,8,1024]{2,1,0:T(8,128)(2,1)S(1)}, u32[]{:S(2)}, u32[]{:S(2)}) %collective-permute-start.3) | collective-permute-done | bytes 32800 | tf_op jit(solution)/shard_map/ppermute | solution.py:304
  70.1 4.5 %collective-permute-done.5.heads_ref = bf16[2,8,1024]{2,1,0:T(8,128)(2,1)S(1)} collective-permute-done((bf16[2,8,1024]{2,1,0:T(8,128)(2,1)}, bf16[2,8,1024]{2,1,0:T(8,128)(2,1)S(1)}, u32[]{:S(2)}, u32[]{:S(2)}) %collective-permute-start.5) | collective-permute-done | bytes 32800 | tf_op jit(solution)/shard_map/ppermute | solution.py:304
  74.6 0.0 copy-done.6
  74.6 0.0 copy-done.5
  74.6 0.4 shard_map.106
  74.9 5.5 %collective-permute-start.6 = (bf16[16,1024]{1,0:T(8,128)(2,1)S(1)}, bf16[16,1024]{1,0:T(8,128)(2,1)S(1)}, u32[]{:S(2)}, u32[]{:S(2)}) collective-permute-start(bf16[16,1024]{1,0:T(8,128)(2,1)S(1)} %shard_map.106), channel_id=1, source_target_pairs={{0,508},{4,504},{8,500},{12,496},{16,492},{20,488},{24,484},{28,48... | collective-permute-start | bytes 98312 | tf_op jit(solution)/shard_map/ppermute | solution.py:299
  80.5 0.0 collective-permute-done.2.other_ref
  80.5 0.0 copy-done.2
  80.5 0.0 copy-done
  80.5 1.9 %shard_map.103 = (bf16[1024,1024]{1,0:T(8,128)(2,1)S(1)}, f32[136,1024]{1,0:T(8,128)S(1)}) custom-call(s32[1]{0:T(128)} %bitcast.place_ref, bf16[128,1024]{1,0:T(8,128)(2,1)S(1)} %copy-done.2, bf16[128,1024]{1,0:T(8,128)(2,1)S(1)} %collective-permute-done.1.near_ref, bf16[256,1024]{1,0:T(8,128)(2,1)S(1)} %collective-permute-done.2.other_ref, ...), custom_call_target="tpu_custom_call" | custom-call | flops 268435456 | bytes 6291456 | tf_op jit(solution)/shard_map/pallas_call | solution.py:51
  82.5 0.0 collective-permute-done.far_ref
  82.5 0.0 copy-done.1
  82.5 3.3 %shard_map.104 = (f32[128,1024]{1,0:T(8,128)S(1)}, f32[128,1024]{1,0:T(8,128)S(1)}, bf16[128,1024]{1,0:T(8,128)(2,1)S(1)}, f32[16,1024]{1,0:T(8,128)S(1)}) custom-call(bf16[128,1024]{1,0:T(8,128)(2,1)S(1)} %collective-permute-done.far_ref, bf16[1024,1024]{1,0:T(8,128)(2,1)S(1)} %get-tuple-element.31.weight_ref, ...), custom_call_target="tpu_custom_call" | custom-call | flops 268435456 | bytes 8388608 | tf_op jit(solution)/shard_map/pallas_call | solution.py:51
  85.8 16.6 %collective-permute-done.6.halo_ref = bf16[16,1024]{1,0:T(8,128)(2,1)S(1)} collective-permute-done((bf16[16,1024]{1,0:T(8,128)(2,1)S(1)}, bf16[16,1024]{1,0:T(8,128)(2,1)S(1)}, u32[]{:S(2)}, u32[]{:S(2)}) %collective-permute-start.6) | collective-permute-done | bytes 32800 | tf_op jit(solution)/shard_map/ppermute | solution.py:299
  102.4 0.0 collective-permute-done.4.slab_ref
  102.4 3.3 %shard_map.107 = (bf16[144,1024]{1,0:T(8,128)(2,1)S(1)}, bf16[128,1024]{1,0:T(8,128)(2,1)S(1)}, f32[8,1024]{1,0:T(8,128)S(1)}) custom-call(bf16[128,1024]{1,0:T(8,128)(2,1)S(1)} %collective-permute-done.4.slab_ref, bf16[16,1024]{1,0:T(8,128)(2,1)S(1)} %collective-permute-done.6.halo_ref, bf16[1024,1024]{1,0:T(8,128)(2,1)S(1)} %get-tuple-element.31.weight_ref, ...), custom_call_target="tpu_custom_call" | custom-call | flops 268435456 | bytes 8388608 | tf_op jit(solution)/shard_map/pallas_call | solution.py:51
  105.7 3.4 %collective-permute-start.7 = (bf16[144,1024]{1,0:T(8,128)(2,1)S(1)}, bf16[144,1024]{1,0:T(8,128)(2,1)S(1)}, u32[]{:S(2)}, u32[]{:S(2)}) collective-permute-start(bf16[144,1024]{1,0:T(8,128)(2,1)S(1)} %get-tuple-element.42), channel_id=1, source_target_pairs={{0,508},{4,504},{8,500},{12,496},{16,492},{20,488},{24,484},{28,48... | collective-permute-start | bytes 884744 | tf_op jit(solution)/shard_map/ppermute | solution.py:299
  109.1 1.2 shard_map.108
  110.2 12.1 %collective-permute-done.7.refs_2_ = bf16[144,1024]{1,0:T(8,128)(2,1)S(1)} collective-permute-done((bf16[144,1024]{1,0:T(8,128)(2,1)S(1)}, bf16[144,1024]{1,0:T(8,128)(2,1)S(1)}, u32[]{:S(2)}, u32[]{:S(2)}) %collective-permute-start.7) | collective-permute-done | bytes 294944 | tf_op jit(solution)/shard_map/ppermute | solution.py:299
  122.3 1.1 shard_map.109
  123.4 1.9 %collective-permute-start.8 = (bf16[272,1024]{1,0:T(8,128)(2,1)S(1)}, bf16[272,1024]{1,0:T(8,128)(2,1)S(1)}, u32[]{:S(2)}, u32[]{:S(2)}) collective-permute-start(bf16[272,1024]{1,0:T(8,128)(2,1)S(1)} %get-tuple-element.46), channel_id=1, source_target_pairs={{0,1},{1,0},{2,3},{3,2},{4,5},{5,4},{6,7},{7,6},{8,9},{9,8},{10,11... | collective-permute-start | bytes 1671176 | tf_op jit(solution)/shard_map/ppermute | solution.py:308
  125.3 1.9 %collective-permute-done.8.got_ref = bf16[272,1024]{1,0:T(8,128)(2,1)S(1)} collective-permute-done((bf16[272,1024]{1,0:T(8,128)(2,1)S(1)}, bf16[272,1024]{1,0:T(8,128)(2,1)S(1)}, u32[]{:S(2)}, u32[]{:S(2)}) %collective-permute-start.8) | collective-permute-done | bytes 557088 | tf_op jit(solution)/shard_map/ppermute | solution.py:308
  127.2 0.1 shard_map.111
  127.3 1.9 %collective-permute-start.9 = (bf16[144,1024]{1,0:T(8,128)(2,1)S(1)}, bf16[144,1024]{1,0:T(8,128)(2,1)S(1)}, u32[]{:S(2)}, u32[]{:S(2)}) collective-permute-start(bf16[144,1024]{1,0:T(8,128)(2,1)S(1)} %get-tuple-element.49), channel_id=1, source_target_pairs={{0,2},{1,3},{2,0},{3,1},{4,6},{5,7},{6,4},{7,5},{8,10},{9,11},{10,... | collective-permute-start | bytes 884744 | tf_op jit(solution)/shard_map/ppermute | solution.py:308
  129.3 2.3 %shard_map.110 = bf16[2,128,1024]{2,1,0:T(8,128)(2,1)} custom-call(bf16[2,128,1024]{2,1,0:T(8,128)(2,1)S(1)} %get-tuple-element.44.value_grad_ref, bf16[1024,1024]{1,0:T(8,128)(2,1)S(1)} %get-tuple-element.31.weight_ref), custom_call_target="tpu_custom_call" | custom-call | flops 536870912 | bytes 4194304 | tf_op jit(solution)/shard_map/pallas_call | solution.py:51
  131.6 6.7 %collective-permute-done.9.got_ref = bf16[144,1024]{1,0:T(8,128)(2,1)S(1)} collective-permute-done((bf16[144,1024]{1,0:T(8,128)(2,1)S(1)}, bf16[144,1024]{1,0:T(8,128)(2,1)S(1)}, u32[]{:S(2)}, u32[]{:S(2)}) %collective-permute-start.9) | collective-permute-done | bytes 294944 | tf_op jit(solution)/shard_map/ppermute | solution.py:308
  138.3 0.8 shard_map.112
  (1 shorter events, 0.0 us)
Async XLA Ops:
  0.6 79.9 %copy-start.2 = (bf16[128,1024]{1,0:T(8,128)(2,1)S(1)}, bf16[128,1024]{1,0:T(8,128)(2,1)}, u32[]{:S(2)}) copy-start(bf16[128,1024]{1,0:T(8,128)(2,1)} %own_ref.1) | copy-start | bytes 786436
  0.6 73.9 %copy-start.6 = (s32[2,1,128]{2,1,0:T(1,128)S(1)}, s32[2,1,128]{2,1,0:T(1,128)}, u32[]{:S(2)}) copy-start(s32[2,1,128]{2,1,0:T(1,128)} %mask_ref.5) | copy-start | bytes 3076
  0.7 73.9 %copy-start.5 = (s32[2,1,128]{2,1,0:T(1,128)S(1)}, s32[2,1,128]{2,1,0:T(1,128)}, u32[]{:S(2)}) copy-start(s32[2,1,128]{2,1,0:T(1,128)} %ids_ref.5) | copy-start | bytes 3076
  0.7 81.8 %copy-start.1 = (bf16[2,1,128,1024]{3,2,1,0:T(8,128)(2,1)S(1)}, bf16[2,1,128,1024]{3,2,1,0:T(8,128)(2,1)}, u32[]{:S(2)}) copy-start(bf16[2,1,128,1024]{3,2,1,0:T(8,128)(2,1)} %param.8) | copy-start | bytes 1572868
  0.7 79.8 %copy-start = (bf16[2,1,128,1024]{3,2,1,0:T(8,128)(2,1)S(1)}, bf16[2,1,128,1024]{3,2,1,0:T(8,128)(2,1)}, u32[]{:S(2)}) copy-start(bf16[2,1,128,1024]{3,2,1,0:T(8,128)(2,1)} %param.7) | copy-start | bytes 1572868
  0.7 36.4 %copy-start.7 = (f32[6,1024]{1,0:T(8,128)S(1)}, f32[6,1024]{1,0:T(8,128)}, u32[]{:S(2)}) copy-start(f32[6,1024]{1,0:T(8,128)} %param.13) | copy-start | bytes 73732
  0.7 37.0 %copy-start.3 = (f32[7,1024]{1,0:T(8,128)S(1)}, f32[7,1024]{1,0:T(8,128)}, u32[]{:S(2)}) copy-start(f32[7,1024]{1,0:T(8,128)} %filter_ref.3) | copy-start | bytes 86020
  0.7 10.3 %collective-permute-start.1 = (bf16[128,1024]{1,0:T(8,128)(2,1)}, bf16[128,1024]{1,0:T(8,128)(2,1)S(1)}, u32[]{:S(2)}, u32[]{:S(2)}) collective-permute-start(bf16[128,1024]{1,0:T(8,128)(2,1)} %own_ref.1), channel_id=1, source_target_pairs={{0,2},{1,3},{2,0},{3,1},{4,6},{5,7},{6,4},{7,5},{8,10},{9,11},{10,... | collective-permute-start | bytes 786440 | tf_op jit(solution)/shard_map/ppermute | solution.py:308
  12.8 67.7 %collective-permute-start.2 = (bf16[256,1024]{1,0:T(8,128)(2,1)}, bf16[256,1024]{1,0:T(8,128)(2,1)S(1)}, u32[]{:S(2)}, u32[]{:S(2)}) collective-permute-start(bf16[256,1024]{1,0:T(8,128)(2,1)} %pad_maximum_fusion), channel_id=1, source_target_pairs={{0,1},{1,0},{2,3},{3,2},{4,5},{5,4},{6,7},{7,6},{8,9},{9,8},{10,11... | collective-permute-start | bytes 1572872 | tf_op jit(solution)/shard_map/ppermute | solution.py:308
  16.6 65.8 %collective-permute-start = (bf16[128,1024]{1,0:T(8,128)(2,1)}, bf16[128,1024]{1,0:T(8,128)(2,1)S(1)}, u32[]{:S(2)}, u32[]{:S(2)}) collective-permute-start(bf16[128,1024]{1,0:T(8,128)(2,1)} %get-tuple-element.29), channel_id=1, source_target_pairs={{0,508},{4,504},{8,500},{12,496},{16,492},{20,488},{24,484},{28,48... | collective-permute-start | bytes 786440 | tf_op jit(solution)/shard_map/ppermute | solution.py:299
  22.2 1.0 copy-start.4
  23.5 78.8 %collective-permute-start.4 = (bf16[128,1024]{1,0:T(8,128)(2,1)S(1)}, bf16[128,1024]{1,0:T(8,128)(2,1)S(1)}, u32[]{:S(2)}, u32[]{:S(2)}) collective-permute-start(bf16[128,1024]{1,0:T(8,128)(2,1)S(1)} %shard_map.105), channel_id=1, source_target_pairs={{0,508},{4,504},{8,500},{12,496},{16,492},{20,488},{24,484},{28,48... | collective-permute-start | bytes 786440 | tf_op jit(solution)/shard_map/ppermute | solution.py:299
  29.6 40.5 %collective-permute-start.3 = (bf16[2,8,1024]{2,1,0:T(8,128)(2,1)}, bf16[2,8,1024]{2,1,0:T(8,128)(2,1)S(1)}, u32[]{:S(2)}, u32[]{:S(2)}) collective-permute-start(bf16[2,8,1024]{2,1,0:T(8,128)(2,1)} %get-tuple-element.30), channel_id=1, source_target_pairs={{0,4},{4,8},{8,12},{12,16},{16,20},{20,24},{24,28},{28,32},{32,36}... | collective-permute-start | bytes 98312 | tf_op jit(solution)/shard_map/ppermute | solution.py:304
  35.1 39.5 %collective-permute-start.5 = (bf16[2,8,1024]{2,1,0:T(8,128)(2,1)}, bf16[2,8,1024]{2,1,0:T(8,128)(2,1)S(1)}, u32[]{:S(2)}, u32[]{:S(2)}) collective-permute-start(bf16[2,8,1024]{2,1,0:T(8,128)(2,1)} %get-tuple-element.35), channel_id=1, source_target_pairs={{4,0},{8,4},{12,8},{16,12},{20,16},{24,20},{28,24},{32,28},{36,32}... | collective-permute-start | bytes 98312 | tf_op jit(solution)/shard_map/ppermute | solution.py:304
  74.9 27.4 %collective-permute-start.6 = (bf16[16,1024]{1,0:T(8,128)(2,1)S(1)}, bf16[16,1024]{1,0:T(8,128)(2,1)S(1)}, u32[]{:S(2)}, u32[]{:S(2)}) collective-permute-start(bf16[16,1024]{1,0:T(8,128)(2,1)S(1)} %shard_map.106), channel_id=1, source_target_pairs={{0,508},{4,504},{8,500},{12,496},{16,492},{20,488},{24,484},{28,48... | collective-permute-start | bytes 98312 | tf_op jit(solution)/shard_map/ppermute | solution.py:299
  105.7 16.6 %collective-permute-start.7 = (bf16[144,1024]{1,0:T(8,128)(2,1)S(1)}, bf16[144,1024]{1,0:T(8,128)(2,1)S(1)}, u32[]{:S(2)}, u32[]{:S(2)}) collective-permute-start(bf16[144,1024]{1,0:T(8,128)(2,1)S(1)} %get-tuple-element.42), channel_id=1, source_target_pairs={{0,508},{4,504},{8,500},{12,496},{16,492},{20,488},{24,484},{28,48... | collective-permute-start | bytes 884744 | tf_op jit(solution)/shard_map/ppermute | solution.py:299
  123.4 3.9 %collective-permute-start.8 = (bf16[272,1024]{1,0:T(8,128)(2,1)S(1)}, bf16[272,1024]{1,0:T(8,128)(2,1)S(1)}, u32[]{:S(2)}, u32[]{:S(2)}) collective-permute-start(bf16[272,1024]{1,0:T(8,128)(2,1)S(1)} %get-tuple-element.46), channel_id=1, source_target_pairs={{0,1},{1,0},{2,3},{3,2},{4,5},{5,4},{6,7},{7,6},{8,9},{9,8},{10,11... | collective-permute-start | bytes 1671176 | tf_op jit(solution)/shard_map/ppermute | solution.py:308
  127.3 10.9 %collective-permute-start.9 = (bf16[144,1024]{1,0:T(8,128)(2,1)S(1)}, bf16[144,1024]{1,0:T(8,128)(2,1)S(1)}, u32[]{:S(2)}, u32[]{:S(2)}) collective-permute-start(bf16[144,1024]{1,0:T(8,128)(2,1)S(1)} %get-tuple-element.49), channel_id=1, source_target_pairs={{0,2},{1,3},{2,0},{3,1},{4,6},{5,7},{6,4},{7,5},{8,10},{9,11},{10,... | collective-permute-start | bytes 884744 | tf_op jit(solution)/shard_map/ppermute | solution.py:308

commit v5 on v4

--- a/solution.py
+++ b/solution.py
@@ -1,3 +1,4 @@
+import functools
 import math
 
 import jax
@@ -92,8 +93,20 @@
         heads_ref[strand] = jnp.where(at_row, tokens, head[strand].astype(F32)).astype(BF16)
 
 
-def flip_kernel(grad_ref, out_ref):
-    out_ref[...] = reverse_both(grad_ref[...])
+def spans_of(chunk, width):
+    part = width // 4
+    starts = (0, 3 * part) if chunk == 0 else (part, 2 * part)
+    return [
+        (slice(start, start + part), slice(place * part, (place + 1) * part))
+        for place, start in enumerate(starts)
+    ]
+
+
+def flip_kernel(grad_ref, *out_refs):
+    whole = reverse_both(grad_ref[...])
+    for chunk, out_ref in enumerate(out_refs):
+        for cols, own in spans_of(chunk, whole.shape[1]):
+            out_ref[:, own] = whole[:, cols]
 
 
 def edge_kernel(ids_ref, mask_ref, tails_ref, heads_ref, slab_ref):
@@ -171,7 +184,7 @@
 
 
 def far_strand_kernel(
-    slab_ref, halo_ref, weight_ref, values0_ref, values1_ref, mirror_ref, heads_ref,
+    chunk, slab_ref, halo_ref, weight_ref, values0_ref, values1_ref, mirror_ref, heads_ref,
     filter_rev_ref, bias_ref, bias_rev_ref,
     send_ref, mirror_out_ref, edge_ref,
     wide1, pull1, sums,
@@ -182,17 +195,15 @@
     hot_own = one_hot(tokens[:, :LANES], LANES)
     hot_far = one_hot(tokens[:, LANES : 2 * LANES], LANES)
     hot_edge = one_hot(heads_ref[0].astype(F32)[HALO - 1 : HALO, :LANES], LANES)
-    edge = dot(halo_ref[HALO:, :], weight_ref[...]).astype(BF16).astype(F32)
-    edge_gate = jax.nn.sigmoid(edge + rows_of(hot_edge, bias_ref[...])[0:HALO])
-    edge_ref[...] = heads_ref[0].astype(F32) * edge_gate
     sums[...] = jnp.zeros_like(sums)
-    wide = 2 * LANES
-    for index in range(width // wide):
-        cols = slice(index * wide, (index + 1) * wide)
+    for cols, local in spans_of(chunk, width):
+        edge = dot(halo_ref[HALO:, :], weight_ref[:, cols]).astype(BF16).astype(F32)
+        edge_gate = jax.nn.sigmoid(edge + rows_of(hot_edge, bias_ref[:, cols])[0:HALO])
+        edge_ref[:, local] = heads_ref[0, :, cols].astype(F32) * edge_gate
         weights = filter_rev_ref[:, cols]
         wide1[0:rows, :] = values1_ref[:, cols]
-        wide1[rows:, :] = edge[:, cols]
-        own = slab_ref[:, cols].astype(F32)
+        wide1[rows:, :] = edge
+        own = slab_ref[:, local].astype(F32)
         gate = jax.nn.sigmoid(values0_ref[HALO:, cols] + rows_of(hot_own, bias_rev_ref[:, cols]))
         far_gate = jax.nn.sigmoid(
             values0_ref[0:HALO, cols] + rows_of(hot_far, bias_rev_ref[:, cols])[LANES - HALO :]
@@ -200,44 +211,44 @@
         conv_grad = own * gate
         pull1[HALO:, :] = conv_grad
         pull1[0:HALO, :] = halo_ref[0:HALO, cols].astype(F32) * far_gate
-        conv = jnp.zeros((rows, wide), F32)
+        conv = jnp.zeros_like(own)
         for tap in range(taps):
             shifted = wide1[tap : tap + rows, :]
             conv = conv + weights[tap : tap + 1] * shifted
-            sums[tap : tap + 1, cols] = jnp.sum(conv_grad * shifted, axis=0, keepdims=True)
+            sums[tap : tap + 1, local] = jnp.sum(conv_grad * shifted, axis=0, keepdims=True)
         pre = own * conv * gate * (1.0 - gate)
-        mirror_out_ref[:, cols] = pre.astype(BF16)
-        sums[8:16, cols] = jnp.dot(hot_own, pre, preferred_element_type=F32, precision=HIGHEST)
+        mirror_out_ref[:, local] = pre.astype(BF16)
+        sums[8:16, local] = jnp.dot(hot_own, pre, preferred_element_type=F32, precision=HIGHEST)
         total = mirror_ref[:, cols].astype(F32)
         for tap in range(taps):
             total = total + weights[tap : tap + 1] * pull1[HALO - tap : HALO - tap + rows, :]
-        send_ref[0:rows, cols] = total.astype(BF16)
+        send_ref[0:rows, local] = total.astype(BF16)
     send_ref[rows:, :] = sums[...].astype(BF16)
 
 
-def operands_kernel(
-    normed_ref, conv_grad_ref, edge_ref, mirror_ref, filter_ref, left_ref, right_ref, pull0,
-):
-    rows, width = conv_grad_ref.shape
-    half = width // 2
-    pull0[0:rows, :] = conv_grad_ref[...]
-    pull0[rows:, :] = edge_ref[...]
+def left_kernel(normed_ref, left_ref):
+    rows = normed_ref.shape[1]
+    half = normed_ref.shape[2] // 2
     for strand in range(2):
         value = normed_ref[strand]
         left_ref[strand * rows : (strand + 1) * rows, :] = value[:, :half]
         left_ref[(2 + strand) * rows : (3 + strand) * rows, :] = reverse_both(value)[:, :half]
-    wide = 2 * LANES
-    for index in range(width // wide):
-        cols = slice(index * wide, (index + 1) * wide)
-        total = mirror_ref[:, cols].astype(F32)
+
+
+def near_grad_kernel(chunk, conv_grad_ref, edge_ref, mirror_ref, filter_ref, right_ref, pull0):
+    rows, width = conv_grad_ref.shape
+    for cols, local in spans_of(chunk, width):
+        pull0[0:rows, :] = conv_grad_ref[:, cols]
+        pull0[rows:, :] = edge_ref[:, local]
+        total = mirror_ref[:, local].astype(F32)
         for tap in range(filter_ref.shape[0]):
-            total = total + filter_ref[tap : tap + 1, cols] * pull0[tap : tap + rows, cols]
-        right_ref[0:rows, cols] = total.astype(BF16)
+            total = total + filter_ref[tap : tap + 1, cols] * pull0[tap : tap + rows, :]
+        right_ref[0:rows, local] = total.astype(BF16)
     right_ref[rows:, :] = reverse_both(right_ref[0:rows, :])
 
 
 def project_kernel(
-    place_ref, scale, left_ref, right_ref, back_ref, terms_ref,
+    chunk, scale, place_ref, left_ref, right_ref, back_ref, terms_ref,
     send_ref, keep_ref, sums_ref, final_ref,
 ):
     rows = right_ref.shape[0] // 2
@@ -246,7 +257,8 @@
     final_ref[0] = right_ref[0:rows, :]
     final_ref[1] = home
     right = jnp.concatenate([right_ref[0:rows, :], home, right_ref[rows:, :], back], axis=0)
-    sums = (terms_ref[...] + reverse_lanes(back_ref[rows:, :]).astype(F32)) * scale
+    terms = jnp.concatenate([terms_ref[:, cols] for cols, _ in spans_of(chunk, terms_ref.shape[1])], axis=1)
+    sums = (terms + reverse_lanes(back_ref[rows:, :]).astype(F32)) * scale
     sums_ref[...] = sums
     core = place_ref[0] % 2
     shard = left_ref.shape[1] // 4
@@ -262,11 +274,14 @@
     send_ref[2 * shard :, :] = sums.astype(BF16)
 
 
-def input_grad_kernel(value_grad_ref, weight_ref, out_ref):
+def input_grad_kernel(outer_ref, inner_ref, weight_ref, out_ref):
     weight = weight_ref[...]
+    part = weight.shape[1] // 4
     for strand in range(2):
+        outer = outer_ref[strand]
+        value = jnp.concatenate([outer[:, :part], inner_ref[strand], outer[:, part:]], axis=1)
         out_ref[strand] = lax.dot_general(
-            value_grad_ref[strand], weight, (((1,), (1,)), ((), ())), preferred_element_type=F32
+            value, weight, (((1,), (1,)), ((), ())), preferred_element_type=F32
         ).astype(BF16)
 
 
@@ -282,12 +297,23 @@
     send_ref[shard:, :] = sums.astype(BF16)
 
 
-def last_sum_kernel(place_ref, keep_ref, got_ref, sums_ref, proj_ref, filter_ref, bias_ref):
-    shard = keep_ref.shape[0]
+def last_sum_kernel(
+    place_ref, keep0_ref, got0_ref, sums0_ref, keep1_ref, got1_ref, sums1_ref,
+    proj_ref, filter_ref, bias_ref,
+):
+    shard, width = proj_ref.shape
     part = filter_ref.shape[2]
-    proj_ref[...] = keep_ref[...] + got_ref[0:shard, :].astype(F32)
-    cols = pl.ds(pl.multiple_of(place_ref[0] * part, part), part)
-    sums = sums_ref[:, cols] + got_ref[shard:, cols].astype(F32)
+    place = place_ref[0]
+    picked = []
+    for chunk, (keep_ref, got_ref, sums_ref) in enumerate(
+        ((keep0_ref, got0_ref, sums0_ref), (keep1_ref, got1_ref, sums1_ref))
+    ):
+        for cols, local in spans_of(chunk, width):
+            proj_ref[:, cols] = keep_ref[:, local] + got_ref[0:shard, local].astype(F32)
+        mine = pl.ds(pl.multiple_of((place // 2) * part, part), part)
+        picked.append(sums_ref[:, mine] + got_ref[shard:, mine].astype(F32))
+    inner = jnp.logical_or(place == 1, place == 2)
+    sums = jnp.where(inner, picked[1], picked[0])
     for tap in range(filter_ref.shape[0]):
         filter_ref[tap] = sums[tap : tap + 1, :]
     for token in range(bias_ref.shape[0]):
@@ -341,10 +367,11 @@
     normed_far = mirrored(send)
     heads = shifted(heads, -1)
     tails = shifted(tails, 1)
-    far_grad, = call(
-        flip_kernel, (shape((rows, width), BF16),), far_grad, flops=600 * rows * width, moved=4 * rows * width,
-    )
-    slab = mirrored(far_grad)
+    half = width // 2
+    far_grads = call(
+        flip_kernel, (shape((rows, half), BF16),) * 2, far_grad, flops=600 * rows * width, moved=4 * rows * width,
+    )
+    slabs = [mirrored(far) for far in far_grads]
     near = partner(proj_half, 2)
     halo, = call(
         edge_kernel, (shape((2 * HALO, width), BF16),), ids, mask, tails, heads,
@@ -373,49 +400,57 @@
         normed_far, weight, values0, out_grad, ids, mask, conv_filter, bias,
         flops=2 * rows * width * width, moved=8 * width * width,
     )
-    wide = 2 * LANES
-    send, mirror1, edge = call(
-        far_strand_kernel,
-        (shape((rows + 16, width), BF16), shape((rows, width), BF16), shape((HALO, width), F32)),
-        slab, halo, weight, values0, values1, mirror0, heads, filter_rev, bias, bias_rev,
-        scratch=[pltpu.VMEM((rows + HALO, wide), F32)] * 2 + [pltpu.VMEM((16, width), F32)],
-        flops=2 * rows * width * width, moved=8 * width * width,
-    )
-    back = mirrored(send)
-    left, right = call(
-        operands_kernel, (shape((4 * rows, width // 2), BF16), shape((2 * rows, width), BF16)),
-        normed, conv_grad, edge, mirror1, conv_filter,
-        scratch=[pltpu.VMEM((rows + HALO, width), F32)],
-        flops=rows * width * width, moved=16 * rows * width,
-    )
+    left, = call(left_kernel, (shape((4 * rows, half), BF16),), normed, flops=rows * width * width)
     grad_scale = 1.0 / math.sqrt(2.0 * lax.axis_size("fsdp") * rows)
-    send1, keep1, sums1, final = call(
-        lambda place_ref, *refs: project_kernel(place_ref, grad_scale, *refs),
-        (
-            shape((2 * shard + 16, width), BF16),
-            shape((2 * shard, width), F32),
-            shape((16, width), F32),
-            shape((2, rows, width), BF16),
-        ),
-        place, left, right, back, terms, scalars=1,
+    part = width // lax.axis_size("fsdp")
+    chunks = []
+    for chunk in range(2):
+        window = pltpu.VMEM((rows + HALO, part), F32)
+        send, mirror1, edge = call(
+            functools.partial(far_strand_kernel, chunk),
+            (shape((rows + 16, half), BF16), shape((rows, half), BF16), shape((HALO, half), F32)),
+            slabs[chunk], halo, weight, values0, values1, mirror0, heads, filter_rev, bias, bias_rev,
+            scratch=[window, window, pltpu.VMEM((16, half), F32)],
+            flops=rows * width * width, moved=4 * width * width,
+        )
+        back = mirrored(send)
+        right, = call(
+            functools.partial(near_grad_kernel, chunk), (shape((2 * rows, half), BF16),),
+            conv_grad, edge, mirror1, conv_filter,
+            scratch=[window], flops=rows * width * width // 2, moved=8 * rows * width,
+        )
+        chunks.append((back, right))
+    sums = []
+    finals = []
+    for chunk, (back, right) in enumerate(chunks):
+        send1, keep1, sums1, final = call(
+            functools.partial(project_kernel, chunk, grad_scale),
+            (
+                shape((2 * shard + 16, half), BF16),
+                shape((2 * shard, half), F32),
+                shape((16, half), F32),
+                shape((2, rows, half), BF16),
+            ),
+            place, left, right, back, terms, scalars=1,
+            flops=2 * rows * width * width, moved=2 * width * width,
+        )
+        finals.append(final)
+        got1 = partner(send1, 1)
+        send2, keep2, sums2 = call(
+            first_sum_kernel,
+            (shape((shard + 16, half), BF16), shape((shard, half), F32), shape((16, half), F32)),
+            place, keep1, got1, sums1, scalars=1, moved=8 * shard * width,
+        )
+        got2 = partner(send2, 2)
+        sums += [keep2, got2, sums2]
+    in_grad, = call(
+        input_grad_kernel, (shape((2, rows, width), BF16),), *finals, weight,
         flops=4 * rows * width * width, moved=4 * width * width,
     )
-    got1 = partner(send1, 1)
-    send2, keep2, sums2 = call(
-        first_sum_kernel,
-        (shape((shard + 16, width), BF16), shape((shard, width), F32), shape((16, width), F32)),
-        place, keep1, got1, sums1, scalars=1, moved=16 * shard * width,
-    )
-    got2 = partner(send2, 2)
-    in_grad, = call(
-        input_grad_kernel, (shape((2, rows, width), BF16),), final, weight,
-        flops=4 * rows * width * width, moved=4 * width * width,
-    )
-    part = width // lax.axis_size("fsdp")
     proj_grad, filter_grad, bias_grad = call(
         last_sum_kernel,
         (shape((shard, width), F32), shape((taps, 1, part), F32), shape((classes, 1, part), F32)),
-        place, keep2, got2, sums2, scalars=1, moved=12 * shard * width,
+        place, *sums, scalars=1, moved=12 * shard * width,
     )
     return (
         in_grad[:, None],

time: 140 us -> 142 us (1.014)
  the two profiles are of different devices: /device:TPU:254 before, /device:TPU:256 now
where the time goes in v5:
time: 142 us; the launch traced here: 141 us
  starting transfers between devices  60 us (42%)
  waiting for transfers between devices  58.4 us (41%)
  Pallas kernels  17.8 us (13%)
  local copies, waits for them, and re-layouts  2.13 us (2%)
  other arithmetic  1.78 us (1%)
    ppermute x6, starting transfers between devices, mirrored(): return lax.ppermute(value, 'ctx', [(i, size - 1 - i) for i in range(size)])  40.7 us
    ppermute x2, waiting for transfers between devices, shifted(): lax.ppermute(value, 'ctx', [(i, i + distance) for i in devices if i + dis...  34 us
    pallas_call x15, Pallas kernels, call(): pl.pallas_call(kernel, out_shape=out_shapes, in_specs=specs, out_specs=[p...  15.9 us
    ppermute x6, starting transfers between devices, partner(): lax.ppermute(value, 'fsdp', [(i, i ^ bit) for i in range(lax.axis_size('f...  15.1 us
    ppermute x6, waiting for transfers between devices, mirrored(): return lax.ppermute(value, 'ctx', [(i, size - 1 - i) for i in range(size)])  14.5 us
    ppermute x6, waiting for transfers between devices, partner(): lax.ppermute(value, 'fsdp', [(i, i ^ bit) for i in range(lax.axis_size('f...  9.88 us
    ppermute x2, starting transfers between devices, shifted(): lax.ppermute(value, 'ctx', [(i, i + distance) for i in devices if i + dis...  4.18 us
  transfers between devices with their start and end apart: 14, of which 6 were waited for; matrix products, arithmetic and copies ran while one was open for 1% of the time, Pallas kernels for 12%

profile of v5, /device:TPU:256, one launch (start us, length us, event | category | flops | bytes accessed | tf_op | source)
XLA Modules:
  0.0 141.1 jit_solution(844781989519632960)
XLA Ops:
  0.6 0.0 copy-start.2
  0.6 0.0 copy-start.5
  0.7 0.0 copy-start.4
  0.7 0.0 copy-start.1
  0.7 0.0 copy-start
  0.7 0.0 copy-start.7
  0.7 0.0 copy-start.3
  0.7 3.5 %collective-permute-start.1 = (bf16[128,1024]{1,0:T(8,128)(2,1)}, bf16[128,1024]{1,0:T(8,128)(2,1)S(1)}, u32[]{:S(2)}, u32[]{:S(2)}) collective-permute-start(bf16[128,1024]{1,0:T(8,128)(2,1)} %own_ref.1), channel_id=1, source_target_pairs={{0,2},{1,3},{2,0},{3,1},{4,6},{5,7},{6,4},{7,5},{8,10},{9,11},{10,... | collective-permute-start | bytes 786440 | tf_op jit(solution)/shard_map/ppermute | solution.py:334
  4.2 6.7 %collective-permute-done.1.near_ref = bf16[128,1024]{1,0:T(8,128)(2,1)S(1)} collective-permute-done((bf16[128,1024]{1,0:T(8,128)(2,1)}, bf16[128,1024]{1,0:T(8,128)(2,1)S(1)}, u32[]{:S(2)}, u32[]{:S(2)}) %collective-permute-start.1) | collective-permute-done | bytes 262176 | tf_op jit(solution)/shard_map/ppermute | solution.py:334
  11.0 1.8 %pad_maximum_fusion = bf16[256,1024]{1,0:T(8,128)(2,1)} fusion(bf16[128,1024]{1,0:T(8,128)(2,1)S(1)} %collective-permute-done.1.near_ref, bf16[128,1024]{1,0:T(8,128)(2,1)} %own_ref.1), kind=kLoop, calls=%fused_computation | loop fusion | flops 1048576 | bytes 1048576 | tf_op jit(solution)/shard_map/concatenate | solution.py:381
  12.8 1.9 %collective-permute-start.2 = (bf16[256,1024]{1,0:T(8,128)(2,1)}, bf16[256,1024]{1,0:T(8,128)(2,1)S(1)}, u32[]{:S(2)}, u32[]{:S(2)}) collective-permute-start(bf16[256,1024]{1,0:T(8,128)(2,1)} %pad_maximum_fusion), channel_id=1, source_target_pairs={{0,1},{1,0},{2,3},{3,2},{4,5},{5,4},{6,7},{7,6},{8,9},{9,8},{10,11... | collective-permute-start | bytes 1572872 | tf_op jit(solution)/shard_map/ppermute | solution.py:334
  14.7 1.9 %shard_map.103 = (bf16[128,1024]{1,0:T(8,128)(2,1)}, bf16[2,8,1024]{2,1,0:T(8,128)(2,1)}, bf16[2,8,1024]{2,1,0:T(8,128)(2,1)}, bf16[128,1024]{1,0:T(8,128)(2,1)}) custom-call(bf16[2,128,1024]{2,1,0:T(8,128)(2,1)} %bitcast.9, bf16[2,128,1024]{2,1,0:T(8,128)(2,1)} %bitcast.12, s32[2,1,128]{2,1,0:T(1,128)} %ids_ref.5, s32[2,1,128]{2,1,0:T(1,128)} %mask_ref.5), custom_call_target="tpu_custom_call" | custom-call | bytes 524288 | tf_op jit(solution)/shard_map/pallas_call | solution.py:349
  16.6 6.9 %collective-permute-start = (bf16[128,1024]{1,0:T(8,128)(2,1)}, bf16[128,1024]{1,0:T(8,128)(2,1)S(1)}, u32[]{:S(2)}, u32[]{:S(2)}) collective-permute-start(bf16[128,1024]{1,0:T(8,128)(2,1)} %get-tuple-element.39), channel_id=1, source_target_pairs={{0,508},{4,504},{8,500},{12,496},{16,492},{20,488},{24,484},{28,48... | collective-permute-start | bytes 786440 | tf_op jit(solution)/shard_map/ppermute | solution.py:325
  23.6 0.0 copy-start.6
  23.6 0.9 copy-done.6
  24.5 0.4 shard_map.106
  24.9 4.6 %collective-permute-start.8 = (bf16[128,512]{1,0:T(8,128)(2,1)S(1)}, bf16[128,512]{1,0:T(8,128)(2,1)S(1)}, u32[]{:S(2)}, u32[]{:S(2)}) collective-permute-start(bf16[128,512]{1,0:T(8,128)(2,1)S(1)} %get-tuple-element.54), channel_id=1, source_target_pairs={{0,508},{4,504},{8,500},{12,496},{16,492},{20,488},{24,484},{28,48... | collective-permute-start | bytes 393224 | tf_op jit(solution)/shard_map/ppermute | solution.py:325
  29.6 2.3 %collective-permute-start.3 = (bf16[2,8,1024]{2,1,0:T(8,128)(2,1)}, bf16[2,8,1024]{2,1,0:T(8,128)(2,1)S(1)}, u32[]{:S(2)}, u32[]{:S(2)}) collective-permute-start(bf16[2,8,1024]{2,1,0:T(8,128)(2,1)} %get-tuple-element.40), channel_id=1, source_target_pairs={{0,4},{4,8},{8,12},{12,16},{16,20},{20,24},{24,28},{28,32},{32,36}... | collective-permute-start | bytes 98312 | tf_op jit(solution)/shard_map/ppermute | solution.py:330
  31.8 9.3 %collective-permute-start.4 = (bf16[128,512]{1,0:T(8,128)(2,1)S(1)}, bf16[128,512]{1,0:T(8,128)(2,1)S(1)}, u32[]{:S(2)}, u32[]{:S(2)}) collective-permute-start(bf16[128,512]{1,0:T(8,128)(2,1)S(1)} %get-tuple-element.45), channel_id=1, source_target_pairs={{0,508},{4,504},{8,500},{12,496},{16,492},{20,488},{24,484},{28,48... | collective-permute-start | bytes 393224 | tf_op jit(solution)/shard_map/ppermute | solution.py:325
  41.1 31.1 %collective-permute-done.3.tails_ref = bf16[2,8,1024]{2,1,0:T(8,128)(2,1)S(1)} collective-permute-done((bf16[2,8,1024]{2,1,0:T(8,128)(2,1)}, bf16[2,8,1024]{2,1,0:T(8,128)(2,1)S(1)}, u32[]{:S(2)}, u32[]{:S(2)}) %collective-permute-start.3) | collective-permute-done | bytes 32800 | tf_op jit(solution)/shard_map/ppermute | solution.py:330
  72.2 1.9 %collective-permute-start.5 = (bf16[2,8,1024]{2,1,0:T(8,128)(2,1)}, bf16[2,8,1024]{2,1,0:T(8,128)(2,1)S(1)}, u32[]{:S(2)}, u32[]{:S(2)}) collective-permute-start(bf16[2,8,1024]{2,1,0:T(8,128)(2,1)} %get-tuple-element.46), channel_id=1, source_target_pairs={{4,0},{8,4},{12,8},{16,12},{20,16},{24,20},{28,24},{32,28},{36,32}... | collective-permute-start | bytes 98312 | tf_op jit(solution)/shard_map/ppermute | solution.py:330
  74.2 0.0 copy-done.7
  74.2 0.6 rev.7.bias_rev_ref
  74.8 0.0 copy-done.3
  74.8 0.6 rev.6.filter_rev_ref
  75.3 2.9 %collective-permute-done.5.heads_ref = bf16[2,8,1024]{2,1,0:T(8,128)(2,1)S(1)} collective-permute-done((bf16[2,8,1024]{2,1,0:T(8,128)(2,1)}, bf16[2,8,1024]{2,1,0:T(8,128)(2,1)S(1)}, u32[]{:S(2)}, u32[]{:S(2)}) %collective-permute-start.5) | collective-permute-done | bytes 32800 | tf_op jit(solution)/shard_map/ppermute | solution.py:330
  78.3 0.0 copy-done.5
  78.3 0.0 copy-done.4
  78.3 0.4 shard_map.107
  78.6 7.6 %collective-permute-start.6 = (bf16[16,1024]{1,0:T(8,128)(2,1)S(1)}, bf16[16,1024]{1,0:T(8,128)(2,1)S(1)}, u32[]{:S(2)}, u32[]{:S(2)}) collective-permute-start(bf16[16,1024]{1,0:T(8,128)(2,1)S(1)} %shard_map.107), channel_id=1, source_target_pairs={{0,508},{4,504},{8,500},{12,496},{16,492},{20,488},{24,484},{28,48... | collective-permute-start | bytes 98312 | tf_op jit(solution)/shard_map/ppermute | solution.py:325
  86.3 0.0 collective-permute-done.2.other_ref
  86.3 0.0 copy-done.2
  86.3 0.0 copy-done
  86.3 1.9 %shard_map.104 = (bf16[1024,1024]{1,0:T(8,128)(2,1)S(1)}, f32[136,1024]{1,0:T(8,128)S(1)}) custom-call(s32[1]{0:T(128)} %bitcast.place_ref, bf16[128,1024]{1,0:T(8,128)(2,1)S(1)} %copy-done.2, bf16[128,1024]{1,0:T(8,128)(2,1)S(1)} %collective-permute-done.1.near_ref, bf16[256,1024]{1,0:T(8,128)(2,1)S(1)} %collective-permute-done.2.other_ref, ...), custom_call_target="tpu_custom_call" | custom-call | flops 268435456 | bytes 6291456 | tf_op jit(solution)/shard_map/pallas_call | solution.py:52
  88.2 0.0 collective-permute-done.far_ref
  88.2 0.0 copy-done.1
  88.2 3.3 %shard_map.105 = (f32[128,1024]{1,0:T(8,128)S(1)}, f32[128,1024]{1,0:T(8,128)S(1)}, bf16[128,1024]{1,0:T(8,128)(2,1)S(1)}, f32[16,1024]{1,0:T(8,128)S(1)}) custom-call(bf16[128,1024]{1,0:T(8,128)(2,1)S(1)} %collective-permute-done.far_ref, bf16[1024,1024]{1,0:T(8,128)(2,1)S(1)} %get-tuple-element.41.weight_ref, ...), custom_call_target="tpu_custom_call" | custom-call | flops 268435456 | bytes 8388608 | tf_op jit(solution)/shard_map/pallas_call | solution.py:52
  91.6 7.9 %collective-permute-done.6.halo_ref = bf16[16,1024]{1,0:T(8,128)(2,1)S(1)} collective-permute-done((bf16[16,1024]{1,0:T(8,128)(2,1)S(1)}, bf16[16,1024]{1,0:T(8,128)(2,1)S(1)}, u32[]{:S(2)}, u32[]{:S(2)}) %collective-permute-start.6) | collective-permute-done | bytes 32800 | tf_op jit(solution)/shard_map/ppermute | solution.py:325
  99.5 0.0 collective-permute-done.8.slab_ref
  99.5 1.8 %shard_map.111 = (bf16[144,512]{1,0:T(8,128)(2,1)S(1)}, bf16[128,512]{1,0:T(8,128)(2,1)S(1)}, f32[8,512]{1,0:T(8,128)S(1)}) custom-call(bf16[128,512]{1,0:T(8,128)(2,1)S(1)} %collective-permute-done.8.slab_ref, bf16[16,1024]{1,0:T(8,128)(2,1)S(1)} %collective-permute-done.6.halo_ref, bf16[1024,1024]{1,0:T(8,128)(2,1)S(1)} %get-tuple-element.41.weight_ref, ...), custom_call_target="tpu_custom_call" | custom-call | flops 134217728 | bytes 4194304 | tf_op jit(solution)/shard_map/pallas_call | solution.py:52
  101.3 10.3 %collective-permute-start.9 = (bf16[144,512]{1,0:T(8,128)(2,1)S(1)}, bf16[144,512]{1,0:T(8,128)(2,1)S(1)}, u32[]{:S(2)}, u32[]{:S(2)}) collective-permute-start(bf16[144,512]{1,0:T(8,128)(2,1)S(1)} %get-tuple-element.57), channel_id=1, source_target_pairs={{0,508},{4,504},{8,500},{12,496},{16,492},{20,488},{24,484},{28,48... | collective-permute-start | bytes 442376 | tf_op jit(solution)/shard_map/ppermute | solution.py:325
  111.5 0.0 collective-permute-done.4.slab_ref
  111.6 1.8 %shard_map.108 = (bf16[144,512]{1,0:T(8,128)(2,1)S(1)}, bf16[128,512]{1,0:T(8,128)(2,1)S(1)}, f32[8,512]{1,0:T(8,128)S(1)}) custom-call(bf16[128,512]{1,0:T(8,128)(2,1)S(1)} %collective-permute-done.4.slab_ref, bf16[16,1024]{1,0:T(8,128)(2,1)S(1)} %collective-permute-done.6.halo_ref, bf16[1024,1024]{1,0:T(8,128)(2,1)S(1)} %get-tuple-element.41.weight_ref, ...), custom_call_target="tpu_custom_call" | custom-call | flops 134217728 | bytes 4194304 | tf_op jit(solution)/shard_map/pallas_call | solution.py:52
  113.4 1.9 %collective-permute-start.7 = (bf16[144,512]{1,0:T(8,128)(2,1)S(1)}, bf16[144,512]{1,0:T(8,128)(2,1)S(1)}, u32[]{:S(2)}, u32[]{:S(2)}) collective-permute-start(bf16[144,512]{1,0:T(8,128)(2,1)S(1)} %get-tuple-element.51), channel_id=1, source_target_pairs={{0,508},{4,504},{8,500},{12,496},{16,492},{20,488},{24,484},{28,48... | collective-permute-start | bytes 442376 | tf_op jit(solution)/shard_map/ppermute | solution.py:325
  115.3 0.5 shard_map.102.left_ref
  115.8 0.6 shard_map.112.right_ref
  116.3 0.5 shard_map.109.right_ref
  116.9 0.0 collective-permute-done.9.back_ref
  116.9 0.7 shard_map.113
  117.6 1.9 %collective-permute-start.12 = (bf16[272,512]{1,0:T(8,128)(2,1)S(1)}, bf16[272,512]{1,0:T(8,128)(2,1)S(1)}, u32[]{:S(2)}, u32[]{:S(2)}) collective-permute-start(bf16[272,512]{1,0:T(8,128)(2,1)S(1)} %get-tuple-element.66), channel_id=1, source_target_pairs={{0,1},{1,0},{2,3},{3,2},{4,5},{5,4},{6,7},{7,6},{8,9},{9,8},{10,11... | collective-permute-start | bytes 835592 | tf_op jit(solution)/shard_map/ppermute | solution.py:334
  119.5 6.6 %collective-permute-done.7.back_ref = bf16[144,512]{1,0:T(8,128)(2,1)S(1)} collective-permute-done((bf16[144,512]{1,0:T(8,128)(2,1)S(1)}, bf16[144,512]{1,0:T(8,128)(2,1)S(1)}, u32[]{:S(2)}, u32[]{:S(2)}) %collective-permute-start.7) | collective-permute-done | bytes 147488 | tf_op jit(solution)/shard_map/ppermute | solution.py:325
  126.1 0.7 shard_map.110
  126.8 1.9 %collective-permute-start.10 = (bf16[272,512]{1,0:T(8,128)(2,1)S(1)}, bf16[272,512]{1,0:T(8,128)(2,1)S(1)}, u32[]{:S(2)}, u32[]{:S(2)}) collective-permute-start(bf16[272,512]{1,0:T(8,128)(2,1)S(1)} %get-tuple-element.60), channel_id=1, source_target_pairs={{0,1},{1,0},{2,3},{3,2},{4,5},{5,4},{6,7},{7,6},{8,9},{9,8},{10,11... | collective-permute-start | bytes 835592 | tf_op jit(solution)/shard_map/ppermute | solution.py:334
  128.8 0.0 collective-permute-done.12.got_ref
  128.8 0.1 shard_map.116
  128.8 3.4 %collective-permute-start.13 = (bf16[144,512]{1,0:T(8,128)(2,1)S(1)}, bf16[144,512]{1,0:T(8,128)(2,1)S(1)}, u32[]{:S(2)}, u32[]{:S(2)}) collective-permute-start(bf16[144,512]{1,0:T(8,128)(2,1)S(1)} %get-tuple-element.69), channel_id=1, source_target_pairs={{0,2},{1,3},{2,0},{3,1},{4,6},{5,7},{6,4},{7,5},{8,10},{9,11},{10,... | collective-permute-start | bytes 442376 | tf_op jit(solution)/shard_map/ppermute | solution.py:334
  132.2 0.0 collective-permute-done.10.got_ref
  132.3 0.1 shard_map.115
  132.3 2.4 %collective-permute-start.11 = (bf16[144,512]{1,0:T(8,128)(2,1)S(1)}, bf16[144,512]{1,0:T(8,128)(2,1)S(1)}, u32[]{:S(2)}, u32[]{:S(2)}) collective-permute-start(bf16[144,512]{1,0:T(8,128)(2,1)S(1)} %get-tuple-element.63), channel_id=1, source_target_pairs={{0,2},{1,3},{2,0},{3,1},{4,6},{5,7},{6,4},{7,5},{8,10},{9,11},{10,... | collective-permute-start | bytes 442376 | tf_op jit(solution)/shard_map/ppermute | solution.py:334
  134.8 2.3 %shard_map.114 = bf16[2,128,1024]{2,1,0:T(8,128)(2,1)} custom-call(bf16[2,128,512]{2,1,0:T(8,128)(2,1)S(1)} %get-tuple-element.53.outer_ref, bf16[2,128,512]{2,1,0:T(8,128)(2,1)S(1)} %get-tuple-element.58.inner_ref, bf16[1024,1024]{1,0:T(8,128)(2,1)S(1)} %get-tuple-element.41.weight_ref), custom_call_target="tpu_custom_call" | custom-call | flops 536870912 | bytes 4194304 | tf_op jit(solution)/shard_map/pallas_call | solution.py:52
  137.1 0.0 collective-permute-done.13.got1_ref
  137.1 3.1 %collective-permute-done.11.got0_ref = bf16[144,512]{1,0:T(8,128)(2,1)S(1)} collective-permute-done((bf16[144,512]{1,0:T(8,128)(2,1)S(1)}, bf16[144,512]{1,0:T(8,128)(2,1)S(1)}, u32[]{:S(2)}, u32[]{:S(2)}) %collective-permute-start.11) | collective-permute-done | bytes 147488 | tf_op jit(solution)/shard_map/ppermute | solution.py:334
  140.2 0.9 shard_map.117
  (1 shorter events, 0.0 us)
Async XLA Ops:
  0.6 85.7 %copy-start.2 = (bf16[128,1024]{1,0:T(8,128)(2,1)S(1)}, bf16[128,1024]{1,0:T(8,128)(2,1)}, u32[]{:S(2)}) copy-start(bf16[128,1024]{1,0:T(8,128)(2,1)} %own_ref.1) | copy-start | bytes 786436
  0.6 77.6 %copy-start.5 = (s32[2,1,128]{2,1,0:T(1,128)S(1)}, s32[2,1,128]{2,1,0:T(1,128)}, u32[]{:S(2)}) copy-start(s32[2,1,128]{2,1,0:T(1,128)} %mask_ref.5) | copy-start | bytes 3076
  0.7 77.6 %copy-start.4 = (s32[2,1,128]{2,1,0:T(1,128)S(1)}, s32[2,1,128]{2,1,0:T(1,128)}, u32[]{:S(2)}) copy-start(s32[2,1,128]{2,1,0:T(1,128)} %ids_ref.5) | copy-start | bytes 3076
  0.7 87.6 %copy-start.1 = (bf16[2,1,128,1024]{3,2,1,0:T(8,128)(2,1)S(1)}, bf16[2,1,128,1024]{3,2,1,0:T(8,128)(2,1)}, u32[]{:S(2)}) copy-start(bf16[2,1,128,1024]{3,2,1,0:T(8,128)(2,1)} %param.8) | copy-start | bytes 1572868
  0.7 85.6 %copy-start = (bf16[2,1,128,1024]{3,2,1,0:T(8,128)(2,1)S(1)}, bf16[2,1,128,1024]{3,2,1,0:T(8,128)(2,1)}, u32[]{:S(2)}) copy-start(bf16[2,1,128,1024]{3,2,1,0:T(8,128)(2,1)} %param.7) | copy-start | bytes 1572868
  0.7 73.5 %copy-start.7 = (f32[6,1024]{1,0:T(8,128)S(1)}, f32[6,1024]{1,0:T(8,128)}, u32[]{:S(2)}) copy-start(f32[6,1024]{1,0:T(8,128)} %param.13) | copy-start | bytes 73732
  0.7 74.1 %copy-start.3 = (f32[7,1024]{1,0:T(8,128)S(1)}, f32[7,1024]{1,0:T(8,128)}, u32[]{:S(2)}) copy-start(f32[7,1024]{1,0:T(8,128)} %filter_ref.5) | copy-start | bytes 86020
  0.7 10.3 %collective-permute-start.1 = (bf16[128,1024]{1,0:T(8,128)(2,1)}, bf16[128,1024]{1,0:T(8,128)(2,1)S(1)}, u32[]{:S(2)}, u32[]{:S(2)}) collective-permute-start(bf16[128,1024]{1,0:T(8,128)(2,1)} %own_ref.1), channel_id=1, source_target_pairs={{0,2},{1,3},{2,0},{3,1},{4,6},{5,7},{6,4},{7,5},{8,10},{9,11},{10,... | collective-permute-start | bytes 786440 | tf_op jit(solution)/shard_map/ppermute | solution.py:334
  12.8 73.5 %collective-permute-start.2 = (bf16[256,1024]{1,0:T(8,128)(2,1)}, bf16[256,1024]{1,0:T(8,128)(2,1)S(1)}, u32[]{:S(2)}, u32[]{:S(2)}) collective-permute-start(bf16[256,1024]{1,0:T(8,128)(2,1)} %pad_maximum_fusion), channel_id=1, source_target_pairs={{0,1},{1,0},{2,3},{3,2},{4,5},{5,4},{6,7},{7,6},{8,9},{9,8},{10,11... | collective-permute-start | bytes 1572872 | tf_op jit(solution)/shard_map/ppermute | solution.py:334
  16.6 71.6 %collective-permute-start = (bf16[128,1024]{1,0:T(8,128)(2,1)}, bf16[128,1024]{1,0:T(8,128)(2,1)S(1)}, u32[]{:S(2)}, u32[]{:S(2)}) collective-permute-start(bf16[128,1024]{1,0:T(8,128)(2,1)} %get-tuple-element.39), channel_id=1, source_target_pairs={{0,508},{4,504},{8,500},{12,496},{16,492},{20,488},{24,484},{28,48... | collective-permute-start | bytes 786440 | tf_op jit(solution)/shard_map/ppermute | solution.py:325
  23.6 1.0 copy-start.6
  24.9 74.6 %collective-permute-start.8 = (bf16[128,512]{1,0:T(8,128)(2,1)S(1)}, bf16[128,512]{1,0:T(8,128)(2,1)S(1)}, u32[]{:S(2)}, u32[]{:S(2)}) collective-permute-start(bf16[128,512]{1,0:T(8,128)(2,1)S(1)} %get-tuple-element.54), channel_id=1, source_target_pairs={{0,508},{4,504},{8,500},{12,496},{16,492},{20,488},{24,484},{28,48... | collective-permute-start | bytes 393224 | tf_op jit(solution)/shard_map/ppermute | solution.py:325
  29.6 42.7 %collective-permute-start.3 = (bf16[2,8,1024]{2,1,0:T(8,128)(2,1)}, bf16[2,8,1024]{2,1,0:T(8,128)(2,1)S(1)}, u32[]{:S(2)}, u32[]{:S(2)}) collective-permute-start(bf16[2,8,1024]{2,1,0:T(8,128)(2,1)} %get-tuple-element.40), channel_id=1, source_target_pairs={{0,4},{4,8},{8,12},{12,16},{16,20},{20,24},{24,28},{28,32},{32,36}... | collective-permute-start | bytes 98312 | tf_op jit(solution)/shard_map/ppermute | solution.py:330
  31.8 79.7 %collective-permute-start.4 = (bf16[128,512]{1,0:T(8,128)(2,1)S(1)}, bf16[128,512]{1,0:T(8,128)(2,1)S(1)}, u32[]{:S(2)}, u32[]{:S(2)}) collective-permute-start(bf16[128,512]{1,0:T(8,128)(2,1)S(1)} %get-tuple-element.45), channel_id=1, source_target_pairs={{0,508},{4,504},{8,500},{12,496},{16,492},{20,488},{24,484},{28,48... | collective-permute-start | bytes 393224 | tf_op jit(solution)/shard_map/ppermute | solution.py:325
  72.2 6.0 %collective-permute-start.5 = (bf16[2,8,1024]{2,1,0:T(8,128)(2,1)}, bf16[2,8,1024]{2,1,0:T(8,128)(2,1)S(1)}, u32[]{:S(2)}, u32[]{:S(2)}) collective-permute-start(bf16[2,8,1024]{2,1,0:T(8,128)(2,1)} %get-tuple-element.46), channel_id=1, source_target_pairs={{4,0},{8,4},{12,8},{16,12},{20,16},{24,20},{28,24},{32,28},{36,32}... | collective-permute-start | bytes 98312 | tf_op jit(solution)/shard_map/ppermute | solution.py:330
  78.6 20.9 %collective-permute-start.6 = (bf16[16,1024]{1,0:T(8,128)(2,1)S(1)}, bf16[16,1024]{1,0:T(8,128)(2,1)S(1)}, u32[]{:S(2)}, u32[]{:S(2)}) collective-permute-start(bf16[16,1024]{1,0:T(8,128)(2,1)S(1)} %shard_map.107), channel_id=1, source_target_pairs={{0,508},{4,504},{8,500},{12,496},{16,492},{20,488},{24,484},{28,48... | collective-permute-start | bytes 98312 | tf_op jit(solution)/shard_map/ppermute | solution.py:325
  101.3 15.6 %collective-permute-start.9 = (bf16[144,512]{1,0:T(8,128)(2,1)S(1)}, bf16[144,512]{1,0:T(8,128)(2,1)S(1)}, u32[]{:S(2)}, u32[]{:S(2)}) collective-permute-start(bf16[144,512]{1,0:T(8,128)(2,1)S(1)} %get-tuple-element.57), channel_id=1, source_target_pairs={{0,508},{4,504},{8,500},{12,496},{16,492},{20,488},{24,484},{28,48... | collective-permute-start | bytes 442376 | tf_op jit(solution)/shard_map/ppermute | solution.py:325
  113.4 12.8 %collective-permute-start.7 = (bf16[144,512]{1,0:T(8,128)(2,1)S(1)}, bf16[144,512]{1,0:T(8,128)(2,1)S(1)}, u32[]{:S(2)}, u32[]{:S(2)}) collective-permute-start(bf16[144,512]{1,0:T(8,128)(2,1)S(1)} %get-tuple-element.51), channel_id=1, source_target_pairs={{0,508},{4,504},{8,500},{12,496},{16,492},{20,488},{24,484},{28,48... | collective-permute-start | bytes 442376 | tf_op jit(solution)/shard_map/ppermute | solution.py:325
  117.6 11.1 %collective-permute-start.12 = (bf16[272,512]{1,0:T(8,128)(2,1)S(1)}, bf16[272,512]{1,0:T(8,128)(2,1)S(1)}, u32[]{:S(2)}, u32[]{:S(2)}) collective-permute-start(bf16[272,512]{1,0:T(8,128)(2,1)S(1)} %get-tuple-element.66), channel_id=1, source_target_pairs={{0,1},{1,0},{2,3},{3,2},{4,5},{5,4},{6,7},{7,6},{8,9},{9,8},{10,11... | collective-permute-start | bytes 835592 | tf_op jit(solution)/shard_map/ppermute | solution.py:334
  126.8 5.4 %collective-permute-start.10 = (bf16[272,512]{1,0:T(8,128)(2,1)S(1)}, bf16[272,512]{1,0:T(8,128)(2,1)S(1)}, u32[]{:S(2)}, u32[]{:S(2)}) collective-permute-start(bf16[272,512]{1,0:T(8,128)(2,1)S(1)} %get-tuple-element.60), channel_id=1, source_target_pairs={{0,1},{1,0},{2,3},{3,2},{4,5},{5,4},{6,7},{7,6},{8,9},{9,8},{10,11... | collective-permute-start | bytes 835592 | tf_op jit(solution)/shard_map/ppermute | solution.py:334
  128.8 8.2 %collective-permute-start.13 = (bf16[144,512]{1,0:T(8,128)(2,1)S(1)}, bf16[144,512]{1,0:T(8,128)(2,1)S(1)}, u32[]{:S(2)}, u32[]{:S(2)}) collective-permute-start(bf16[144,512]{1,0:T(8,128)(2,1)S(1)} %get-tuple-element.69), channel_id=1, source_target_pairs={{0,2},{1,3},{2,0},{3,1},{4,6},{5,7},{6,4},{7,5},{8,10},{9,11},{10,... | collective-permute-start | bytes 442376 | tf_op jit(solution)/shard_map/ppermute | solution.py:334
  132.3 7.9 %collective-permute-start.11 = (bf16[144,512]{1,0:T(8,128)(2,1)S(1)}, bf16[144,512]{1,0:T(8,128)(2,1)S(1)}, u32[]{:S(2)}, u32[]{:S(2)}) collective-permute-start(bf16[144,512]{1,0:T(8,128)(2,1)S(1)} %get-tuple-element.63), channel_id=1, source_target_pairs={{0,2},{1,3},{2,0},{3,1},{4,6},{5,7},{6,4},{7,5},{8,10},{9,11},{10,... | collective-permute-start | bytes 442376 | tf_op jit(solution)/shard_map/ppermute | solution.py:334

commit v6 on v4

--- a/solution.py
+++ b/solution.py
@@ -1,3 +1,4 @@
+import functools
 import math
 
 import jax
@@ -10,6 +11,7 @@
 
 LANES = 128
 HALO = 8
+VMEM_BYTES = 20 * 1024 * 1024
 F32 = jnp.float32
 BF16 = jnp.bfloat16
 HIGHEST = lax.Precision.HIGHEST
@@ -55,7 +57,7 @@
         out_specs=[pl.BlockSpec(memory_space=pltpu.VMEM)] * len(out_shapes),
         scratch_shapes=list(scratch),
         cost_estimate=pl.CostEstimate(flops=flops, bytes_accessed=moved, transcendentals=0),
-        compiler_params=pltpu.CompilerParams(vmem_limit_bytes=48 * 1024 * 1024),
+        compiler_params=pltpu.CompilerParams(vmem_limit_bytes=VMEM_BYTES),
     )(*operands)
 
 
@@ -64,7 +66,7 @@
 
 
 def lead_kernel(
-    normed_ref, grad_ref, ids_ref, mask_ref, send_ref, tails_ref, heads_ref, far_ref,
+    normed_ref, grad_ref, ids_ref, mask_ref, send_ref, tails_ref, heads_ref, far_ref, tokens_ref,
     head, ids, mask, arrived,
 ):
     rows, width = send_ref.shape
@@ -88,30 +90,31 @@
     at_row = lax.broadcasted_iota(jnp.int32, (HALO, width), 0) == HALO - 1
     for strand in range(2):
         tokens = token_row(ids, mask, strand)
+        tokens_ref[strand] = tokens
         tokens = jnp.concatenate([tokens, jnp.zeros((1, width - LANES), F32)], axis=1)
         heads_ref[strand] = jnp.where(at_row, tokens, head[strand].astype(F32)).astype(BF16)
 
 
-def flip_kernel(grad_ref, out_ref):
-    out_ref[...] = reverse_both(grad_ref[...])
-
-
-def edge_kernel(ids_ref, mask_ref, tails_ref, heads_ref, slab_ref):
-    width = slab_ref.shape[1]
+def pack_kernel(grad_ref, tokens_ref, tails_ref, heads_ref, slab_ref):
+    rows, width = grad_ref.shape
     head = heads_ref[1].astype(F32)
     swap = reversal(HALO, F32)
     tail_rev = jnp.dot(swap, tails_ref[1].astype(F32), preferred_element_type=F32).astype(BF16)
     head_rev = jnp.dot(swap, head, preferred_element_type=F32).astype(BF16)
-    own = token_row(ids_ref, mask_ref, 1)
+    own = tokens_ref[1]
     both = jnp.concatenate([own, head[HALO - 1 : HALO, :LANES], jnp.zeros((6, LANES), F32)], axis=0)
     flipped = dot(both.astype(BF16), reversal(LANES))
     tokens = jnp.concatenate([flipped[0:1], flipped[1:2], jnp.zeros((1, width - 2 * LANES), F32)], axis=1)
     at_row = lax.broadcasted_iota(jnp.int32, (HALO, width), 0) == HALO - 1
     slab_ref[0:HALO, :] = reverse_lanes(head_rev)
-    slab_ref[HALO:, :] = jnp.where(at_row, tokens, reverse_lanes(tail_rev).astype(F32)).astype(BF16)
-
-
-def forward_kernel(place_ref, own_ref, near_ref, other_ref, normed_ref, tails_ref, weight_ref, values_ref):
+    slab_ref[HALO : HALO + rows, :] = reverse_both(grad_ref[...])
+    slab_ref[HALO + rows :, :] = jnp.where(at_row, tokens, reverse_lanes(tail_rev).astype(F32)).astype(BF16)
+
+
+def forward_kernel(
+    place_ref, own_ref, near_ref, other_ref, normed_ref, tails_ref, filter_ref, bias_ref,
+    weight_ref, values_ref, filter_rev_ref, bias_out_ref, bias_rev_ref,
+):
     shard = own_ref.shape[0]
     half = 4 * shard
     x_lo = place_ref[0] // 2
@@ -127,11 +130,24 @@
         weight_ref[pl.ds(pl.multiple_of(index * shard, shard), shard), :] = block
         back = half + (3 - index) * shard
         weight_ref[pl.ds(pl.multiple_of(back, shard), shard), :] = reverse_both(block)
+    width = weight_ref.shape[1]
+    table = jnp.concatenate([bias_ref[...], jnp.zeros((HALO - bias_ref.shape[0], width), F32)], axis=0)
+    bias_out_ref[...] = table
+    bias_rev_ref[...] = reverse_lanes(table, HIGHEST)
+    taps = filter_ref.shape[0]
+    table = jnp.concatenate([filter_ref[...], jnp.zeros((HALO - taps, width), F32)], axis=0)
+    filter_rev_ref[...] = reverse_lanes(table, HIGHEST)
     weight = weight_ref[...]
     values_ref[HALO:, :] = dot(normed_ref[0], weight).astype(BF16).astype(F32)
     values_ref[0:HALO, :] = dot(tails_ref[0], weight).astype(BF16).astype(F32)
 
 
+def join_kernel(first_ref, second_ref, out_ref):
+    shard = first_ref.shape[0]
+    out_ref[0:shard, :] = first_ref[...]
+    out_ref[shard:, :] = second_ref[...]
+
+
 def one_hot(row, count):
     classes = lax.broadcasted_iota(jnp.int32, (HALO, count), 0)
     return (row.astype(jnp.int32) == classes).astype(F32)
@@ -144,13 +160,13 @@
 
 
 def near_strand_kernel(
-    far_ref, weight_ref, values0_ref, grad_ref, ids_ref, mask_ref, filter_ref, bias_ref,
+    far_ref, weight_ref, values0_ref, grad_ref, tokens_ref, filter_ref, bias_ref,
     values1_ref, conv_grad_ref, mirror_ref, terms_ref,
 ):
     rows, width = grad_ref.shape[1], grad_ref.shape[2]
     taps = filter_ref.shape[0]
     values1_ref[...] = dot(reverse_both(far_ref[...]), weight_ref[...]).astype(BF16).astype(F32)
-    hot = one_hot(token_row(ids_ref, mask_ref, 0), LANES)
+    hot = one_hot(tokens_ref[0], LANES)
     wide = 2 * LANES
     for index in range(width // wide):
         cols = slice(index * wide, (index + 1) * wide)
@@ -171,18 +187,17 @@
 
 
 def far_strand_kernel(
-    slab_ref, halo_ref, weight_ref, values0_ref, values1_ref, mirror_ref, heads_ref,
+    taps, slab_ref, weight_ref, values0_ref, values1_ref, mirror_ref, heads_ref,
     filter_rev_ref, bias_ref, bias_rev_ref,
     send_ref, mirror_out_ref, edge_ref,
     wide1, pull1, sums,
 ):
     rows, width = mirror_ref.shape
-    taps = filter_rev_ref.shape[0]
-    tokens = halo_ref[HALO:, :].astype(F32)[HALO - 1 : HALO, :]
+    tokens = slab_ref[HALO + rows :, :].astype(F32)[HALO - 1 : HALO, :]
     hot_own = one_hot(tokens[:, :LANES], LANES)
     hot_far = one_hot(tokens[:, LANES : 2 * LANES], LANES)
     hot_edge = one_hot(heads_ref[0].astype(F32)[HALO - 1 : HALO, :LANES], LANES)
-    edge = dot(halo_ref[HALO:, :], weight_ref[...]).astype(BF16).astype(F32)
+    edge = dot(slab_ref[HALO + rows :, :], weight_ref[...]).astype(BF16).astype(F32)
     edge_gate = jax.nn.sigmoid(edge + rows_of(hot_edge, bias_ref[...])[0:HALO])
     edge_ref[...] = heads_ref[0].astype(F32) * edge_gate
     sums[...] = jnp.zeros_like(sums)
@@ -192,14 +207,14 @@
         weights = filter_rev_ref[:, cols]
         wide1[0:rows, :] = values1_ref[:, cols]
         wide1[rows:, :] = edge[:, cols]
-        own = slab_ref[:, cols].astype(F32)
+        own = slab_ref[HALO : HALO + rows, cols].astype(F32)
         gate = jax.nn.sigmoid(values0_ref[HALO:, cols] + rows_of(hot_own, bias_rev_ref[:, cols]))
         far_gate = jax.nn.sigmoid(
             values0_ref[0:HALO, cols] + rows_of(hot_far, bias_rev_ref[:, cols])[LANES - HALO :]
         )
         conv_grad = own * gate
         pull1[HALO:, :] = conv_grad
-        pull1[0:HALO, :] = halo_ref[0:HALO, cols].astype(F32) * far_gate
+        pull1[0:HALO, :] = slab_ref[0:HALO, cols].astype(F32) * far_gate
         conv = jnp.zeros((rows, wide), F32)
         for tap in range(taps):
             shifted = wide1[tap : tap + rows, :]
@@ -320,16 +335,17 @@
     normed, out_grad = normed[:, 0], out_grad[:, 0]
     place = lax.axis_index("fsdp").astype(jnp.int32).reshape(1)
 
-    send, tails, heads, far_grad = pl.pallas_call(
+    send, tails, heads, far_grad, tokens = pl.pallas_call(
         lead_kernel,
         out_shape=(
             shape((rows, width), BF16),
             shape((2, HALO, width), BF16),
             shape((2, HALO, width), BF16),
             shape((rows, width), BF16),
+            shape((2, 1, rows), F32),
         ),
         in_specs=[pl.BlockSpec(memory_space=pltpu.HBM)] * 4,
-        out_specs=[pl.BlockSpec(memory_space=pltpu.VMEM)] * 4,
+        out_specs=[pl.BlockSpec(memory_space=pltpu.VMEM)] * 5,
         scratch_shapes=[
             pltpu.VMEM((2, HALO, width), BF16),
             pltpu.VMEM((2, 1, rows), jnp.int32),
@@ -341,25 +357,18 @@
     normed_far = mirrored(send)
     heads = shifted(heads, -1)
     tails = shifted(tails, 1)
-    far_grad, = call(
-        flip_kernel, (shape((rows, width), BF16),), far_grad, flops=600 * rows * width, moved=4 * rows * width,
-    )
-    slab = mirrored(far_grad)
     near = partner(proj_half, 2)
-    halo, = call(
-        edge_kernel, (shape((2 * HALO, width), BF16),), ids, mask, tails, heads,
-        flops=600 * HALO * width, moved=8 * HALO * width,
-    )
-    halo = mirrored(halo)
-    other = partner(jnp.concatenate([proj_half, near], axis=0), 1)
-    filter_rev = conv_filter[:, ::-1]
-    bias = jnp.pad(gate_bias, ((0, HALO - classes), (0, 0)))
-    bias_rev = bias[:, ::-1]
-
-    weight, values0 = call(
+    slab, = call(
+        pack_kernel, (shape((rows + 2 * HALO, width), BF16),), far_grad, tokens, tails, heads,
+        flops=600 * rows * width, moved=4 * rows * width,
+    )
+    slab = mirrored(slab)
+    pair, = call(join_kernel, (shape((2 * shard, width), BF16),), proj_half, near, moved=8 * shard * width)
+    other = partner(pair, 1)
+    weight, values0, filter_rev, bias, bias_rev = call(
         forward_kernel,
-        (shape((width, width), BF16), shape((rows + HALO, width), F32)),
-        place, proj_half, near, other, normed, tails, scalars=1,
+        (shape((width, width), BF16), shape((rows + HALO, width), F32)) + (shape((HALO, width), F32),) * 3,
+        place, proj_half, near, other, normed, tails, conv_filter, gate_bias, scalars=1,
         flops=2 * rows * width * width, moved=6 * width * width,
     )
     values1, conv_grad, mirror0, terms = call(
@@ -370,14 +379,14 @@
             shape((rows, width), BF16),
             shape((16, width), F32),
         ),
-        normed_far, weight, values0, out_grad, ids, mask, conv_filter, bias,
+        normed_far, weight, values0, out_grad, tokens, conv_filter, bias,
         flops=2 * rows * width * width, moved=8 * width * width,
     )
     wide = 2 * LANES
     send, mirror1, edge = call(
-        far_strand_kernel,
+        functools.partial(far_strand_kernel, taps),
         (shape((rows + 16, width), BF16), shape((rows, width), BF16), shape((HALO, width), F32)),
-        slab, halo, weight, values0, values1, mirror0, heads, filter_rev, bias, bias_rev,
+        slab, weight, values0, values1, mirror0, heads, filter_rev, bias, bias_rev,
         scratch=[pltpu.VMEM((rows + HALO, wide), F32)] * 2 + [pltpu.VMEM((16, width), F32)],
         flops=2 * rows * width * width, moved=8 * width * width,
     )

time: 140 us -> 154 us (1.10)
  the two profiles are of different devices: /device:TPU:254 before, /device:TPU:4 now
where the time goes in v6:
time: 154 us; the launch traced here: 153 us
  waiting for transfers between devices  82.5 us (54%)
  starting transfers between devices  47.7 us (31%)
  Pallas kernels  17.4 us (11%)
  local copies, waits for them, and re-layouts  4.73 us (3%)
    ppermute x3, waiting for transfers between devices, mirrored(): return lax.ppermute(value, 'ctx', [(i, size - 1 - i) for i in range(size)])  66.1 us
    ppermute x3, starting transfers between devices, mirrored(): return lax.ppermute(value, 'ctx', [(i, size - 1 - i) for i in range(size)])  27.9 us
    pallas_call x10, Pallas kernels, call(): pl.pallas_call(kernel, out_shape=out_shapes, in_specs=specs, out_specs=[p...  15.4 us
    ppermute x4, waiting for transfers between devices, partner(): lax.ppermute(value, 'fsdp', [(i, i ^ bit) for i in range(lax.axis_size('f...  14.5 us
    ppermute x4, starting transfers between devices, partner(): lax.ppermute(value, 'fsdp', [(i, i ^ bit) for i in range(lax.axis_size('f...  10.3 us
    ppermute x2, starting transfers between devices, shifted(): lax.ppermute(value, 'ctx', [(i, i + distance) for i in devices if i + dis...  9.46 us
    unnamed x22, local copies, waits for them, and re-layouts  4.73 us
  transfers between devices with their start and end apart: 9, of which 7 were waited for; matrix products, arithmetic and copies ran while one was open for 0% of the time, Pallas kernels for 8%

profile of v6, /device:TPU:4, one launch (start us, length us, event | category | flops | bytes accessed | tf_op | source)
XLA Modules:
  0.0 153.1 jit_solution(5929179955649358575)
XLA Ops:
  0.6 0.0 copy-start.1
  0.6 0.0 copy-start
  0.7 3.2 %collective-permute-start.1 = (bf16[128,1024]{1,0:T(8,128)(2,1)}, bf16[128,1024]{1,0:T(8,128)(2,1)S(1)}, u32[]{:S(2)}, u32[]{:S(2)}) collective-permute-start(bf16[128,1024]{1,0:T(8,128)(2,1)} %own_ref.1), channel_id=1, source_target_pairs={{0,2},{1,3},{2,0},{3,1},{4,6},{5,7},{6,4},{7,5},{8,10},{9,11},{10,... | collective-permute-start | bytes 786440 | tf_op jit(solution)/shard_map/ppermute | solution.py:323
  3.9 7.0 %collective-permute-done.1.second_ref.near_ref = bf16[128,1024]{1,0:T(8,128)(2,1)S(1)} collective-permute-done((bf16[128,1024]{1,0:T(8,128)(2,1)}, bf16[128,1024]{1,0:T(8,128)(2,1)S(1)}, u32[]{:S(2)}, u32[]{:S(2)}) %collective-permute-start.1) | collective-permute-done | bytes 262176 | tf_op jit(solution)/shard_map/ppermute | solution.py:323
  10.9 0.0 copy-start.2
  10.9 0.9 copy-done.2
  11.9 0.0 copy-start.3
  11.9 0.0 copy-start.4
  11.9 2.1 %collective-permute-start.2 = (bf16[256,1024]{1,0:T(8,128)(2,1)S(1)}, bf16[256,1024]{1,0:T(8,128)(2,1)S(1)}, u32[]{:S(2)}, u32[]{:S(2)}) collective-permute-start(bf16[256,1024]{1,0:T(8,128)(2,1)S(1)} %shard_map.103), channel_id=1, source_target_pairs={{0,1},{1,0},{2,3},{3,2},{4,5},{5,4},{6,7},{7,6},{8,9},{9,8},{10,11... | collective-permute-start | bytes 1572872 | tf_op jit(solution)/shard_map/ppermute | solution.py:323
  14.0 1.9 %shard_map.102 = (bf16[128,1024]{1,0:T(8,128)(2,1)}, bf16[2,8,1024]{2,1,0:T(8,128)(2,1)}, bf16[2,8,1024]{2,1,0:T(8,128)(2,1)}, bf16[128,1024]{1,0:T(8,128)(2,1)}, f32[2,1,128]{2,1,0:T(1,128)}) custom-call(bf16[2,128,1024]{2,1,0:T(8,128)(2,1)} %bitcast.9, bf16[2,128,1024]{2,1,0:T(8,128)(2,1)} %bitcast.12, s32[2,1,128]{2,1,0:T(1,128)} %ids_ref.1, ...), custom_call_target="tpu_custom_call" | custom-call | bytes 524288 | tf_op jit(solution)/shard_map/pallas_call | solution.py:338
  15.9 0.0 copy-start.10
  15.9 3.5 %collective-permute-start.3 = (bf16[2,8,1024]{2,1,0:T(8,128)(2,1)}, bf16[2,8,1024]{2,1,0:T(8,128)(2,1)S(1)}, u32[]{:S(2)}, u32[]{:S(2)}) collective-permute-start(bf16[2,8,1024]{2,1,0:T(8,128)(2,1)} %get-tuple-element.34), channel_id=1, source_target_pairs={{0,4},{4,8},{8,12},{12,16},{16,20},{20,24},{24,28},{28,32},{32,36}... | collective-permute-start | bytes 98312 | tf_op jit(solution)/shard_map/ppermute | solution.py:319
  19.4 6.0 %collective-permute-start.4 = (bf16[2,8,1024]{2,1,0:T(8,128)(2,1)}, bf16[2,8,1024]{2,1,0:T(8,128)(2,1)S(1)}, u32[]{:S(2)}, u32[]{:S(2)}) collective-permute-start(bf16[2,8,1024]{2,1,0:T(8,128)(2,1)} %get-tuple-element.41), channel_id=1, source_target_pairs={{4,0},{8,4},{12,8},{16,12},{20,16},{24,20},{28,24},{32,28},{36,32}... | collective-permute-start | bytes 98312 | tf_op jit(solution)/shard_map/ppermute | solution.py:319
  25.4 0.2 collective-permute-done.3.tails_ref
  25.6 1.7 %collective-permute-done.4.heads_ref = bf16[2,8,1024]{2,1,0:T(8,128)(2,1)S(1)} collective-permute-done((bf16[2,8,1024]{2,1,0:T(8,128)(2,1)}, bf16[2,8,1024]{2,1,0:T(8,128)(2,1)S(1)}, u32[]{:S(2)}, u32[]{:S(2)}) %collective-permute-start.4) | collective-permute-done | bytes 32800 | tf_op jit(solution)/shard_map/ppermute | solution.py:319
  27.3 0.0 copy-start.5
  27.3 0.9 copy-done.5
  28.3 0.0 copy-start.9
  28.3 0.7 copy-done.9
  28.9 0.6 shard_map.106
  29.6 0.0 copy-start.6
  29.6 0.6 copy-done.6
  30.2 16.7 %collective-permute-start.5 = (bf16[144,1024]{1,0:T(8,128)(2,1)S(1)}, bf16[144,1024]{1,0:T(8,128)(2,1)S(1)}, u32[]{:S(2)}, u32[]{:S(2)}) collective-permute-start(bf16[144,1024]{1,0:T(8,128)(2,1)S(1)} %shard_map.106), channel_id=1, source_target_pairs={{0,508},{4,504},{8,500},{12,496},{16,492},{20,488},{24,484},{28,48... | collective-permute-start | bytes 884744 | tf_op jit(solution)/shard_map/ppermute | solution.py:314
  46.9 1.9 %collective-permute-start = (bf16[128,1024]{1,0:T(8,128)(2,1)}, bf16[128,1024]{1,0:T(8,128)(2,1)S(1)}, u32[]{:S(2)}, u32[]{:S(2)}) collective-permute-start(bf16[128,1024]{1,0:T(8,128)(2,1)} %get-tuple-element.33), channel_id=1, source_target_pairs={{0,508},{4,504},{8,500},{12,496},{16,492},{20,488},{24,484},{28,48... | collective-permute-start | bytes 786440 | tf_op jit(solution)/shard_map/ppermute | solution.py:314
  48.8 0.0 collective-permute-done.2.other_ref
  48.8 0.0 copy-done
  48.8 0.0 copy-done.3
  48.8 0.0 copy-done.4
  48.8 0.0 copy-start.7
  48.8 0.7 copy-done.7
  49.6 0.0 copy-start.8
  49.6 0.8 copy-done.8
  50.4 2.6 %shard_map.104 = (bf16[1024,1024]{1,0:T(8,128)(2,1)S(1)}, f32[136,1024]{1,0:T(8,128)S(1)}, f32[8,1024]{1,0:T(8,128)S(1)}, f32[8,1024]{1,0:T(8,128)S(1)}, f32[8,1024]{1,0:T(8,128)S(1)}) custom-call(s32[1]{0:T(128)} %bitcast.place_ref, bf16[128,1024]{1,0:T(8,128)(2,1)S(1)} %copy-done.3, bf16[128,1024]{1,0:T(8,128)(2,1)S(1)} %collective-permute-done.1.second_ref.near_ref, ...), custom_call_target="tpu_custom_call" | custom-call | flops 268435456 | bytes 6291456 | tf_op jit(solution)/shard_map/pallas_call | solution.py:53
  52.9 60.5 %collective-permute-done.far_ref = bf16[128,1024]{1,0:T(8,128)(2,1)S(1)} collective-permute-done((bf16[128,1024]{1,0:T(8,128)(2,1)}, bf16[128,1024]{1,0:T(8,128)(2,1)S(1)}, u32[]{:S(2)}, u32[]{:S(2)}) %collective-permute-start) | collective-permute-done | bytes 262176 | tf_op jit(solution)/shard_map/ppermute | solution.py:314
  113.5 0.0 copy-done.1
  113.5 0.0 copy-done.10
  113.5 3.3 %shard_map.105 = (f32[128,1024]{1,0:T(8,128)S(1)}, f32[128,1024]{1,0:T(8,128)S(1)}, bf16[128,1024]{1,0:T(8,128)(2,1)S(1)}, f32[16,1024]{1,0:T(8,128)S(1)}) custom-call(bf16[128,1024]{1,0:T(8,128)(2,1)S(1)} %collective-permute-done.far_ref, bf16[1024,1024]{1,0:T(8,128)(2,1)S(1)} %get-tuple-element.35.weight_ref, ...), custom_call_target="tpu_custom_call" | custom-call | flops 268435456 | bytes 8388608 | tf_op jit(solution)/shard_map/pallas_call | solution.py:53
  116.8 0.0 collective-permute-done.5.slab_ref
  116.8 3.4 %shard_map.107 = (bf16[144,1024]{1,0:T(8,128)(2,1)S(1)}, bf16[128,1024]{1,0:T(8,128)(2,1)S(1)}, f32[8,1024]{1,0:T(8,128)S(1)}) custom-call(bf16[144,1024]{1,0:T(8,128)(2,1)S(1)} %collective-permute-done.5.slab_ref, bf16[1024,1024]{1,0:T(8,128)(2,1)S(1)} %get-tuple-element.35.weight_ref, f32[136,1024]{1,0:T(8,128)S(1)} %get-tuple-element.36.values0_ref, ...), custom_call_target="tpu_custom_call" | custom-call | flops 268435456 | bytes 8388608 | tf_op jit(solution)/shard_map/pallas_call | solution.py:53
  120.2 9.4 %collective-permute-start.6 = (bf16[144,1024]{1,0:T(8,128)(2,1)S(1)}, bf16[144,1024]{1,0:T(8,128)(2,1)S(1)}, u32[]{:S(2)}, u32[]{:S(2)}) collective-permute-start(bf16[144,1024]{1,0:T(8,128)(2,1)S(1)} %get-tuple-element.50), channel_id=1, source_target_pairs={{0,508},{4,504},{8,500},{12,496},{16,492},{20,488},{24,484},{28,48... | collective-permute-start | bytes 884744 | tf_op jit(solution)/shard_map/ppermute | solution.py:314
  129.5 1.2 shard_map.108
  130.7 5.6 %collective-permute-done.6.refs_2_ = bf16[144,1024]{1,0:T(8,128)(2,1)S(1)} collective-permute-done((bf16[144,1024]{1,0:T(8,128)(2,1)S(1)}, bf16[144,1024]{1,0:T(8,128)(2,1)S(1)}, u32[]{:S(2)}, u32[]{:S(2)}) %collective-permute-start.6) | collective-permute-done | bytes 294944 | tf_op jit(solution)/shard_map/ppermute | solution.py:314
  136.3 1.1 shard_map.109
  137.4 1.9 %collective-permute-start.7 = (bf16[272,1024]{1,0:T(8,128)(2,1)S(1)}, bf16[272,1024]{1,0:T(8,128)(2,1)S(1)}, u32[]{:S(2)}, u32[]{:S(2)}) collective-permute-start(bf16[272,1024]{1,0:T(8,128)(2,1)S(1)} %get-tuple-element.54), channel_id=1, source_target_pairs={{0,1},{1,0},{2,3},{3,2},{4,5},{5,4},{6,7},{7,6},{8,9},{9,8},{10,11... | collective-permute-start | bytes 1671176 | tf_op jit(solution)/shard_map/ppermute | solution.py:323
  139.3 1.9 %collective-permute-done.7.got_ref = bf16[272,1024]{1,0:T(8,128)(2,1)S(1)} collective-permute-done((bf16[272,1024]{1,0:T(8,128)(2,1)S(1)}, bf16[272,1024]{1,0:T(8,128)(2,1)S(1)}, u32[]{:S(2)}, u32[]{:S(2)}) %collective-permute-start.7) | collective-permute-done | bytes 557088 | tf_op jit(solution)/shard_map/ppermute | solution.py:323
  141.2 0.1 shard_map.111
  141.3 3.1 %collective-permute-start.8 = (bf16[144,1024]{1,0:T(8,128)(2,1)S(1)}, bf16[144,1024]{1,0:T(8,128)(2,1)S(1)}, u32[]{:S(2)}, u32[]{:S(2)}) collective-permute-start(bf16[144,1024]{1,0:T(8,128)(2,1)S(1)} %get-tuple-element.57), channel_id=1, source_target_pairs={{0,2},{1,3},{2,0},{3,1},{4,6},{5,7},{6,4},{7,5},{8,10},{9,11},{10,... | collective-permute-start | bytes 884744 | tf_op jit(solution)/shard_map/ppermute | solution.py:323
  144.4 2.3 %shard_map.110 = bf16[2,128,1024]{2,1,0:T(8,128)(2,1)} custom-call(bf16[2,128,1024]{2,1,0:T(8,128)(2,1)S(1)} %get-tuple-element.52.value_grad_ref, bf16[1024,1024]{1,0:T(8,128)(2,1)S(1)} %get-tuple-element.35.weight_ref), custom_call_target="tpu_custom_call" | custom-call | flops 536870912 | bytes 4194304 | tf_op jit(solution)/shard_map/pallas_call | solution.py:53
  146.7 5.6 %collective-permute-done.8.got_ref = bf16[144,1024]{1,0:T(8,128)(2,1)S(1)} collective-permute-done((bf16[144,1024]{1,0:T(8,128)(2,1)S(1)}, bf16[144,1024]{1,0:T(8,128)(2,1)S(1)}, u32[]{:S(2)}, u32[]{:S(2)}) %collective-permute-start.8) | collective-permute-done | bytes 294944 | tf_op jit(solution)/shard_map/ppermute | solution.py:323
  152.3 0.8 shard_map.112
  (1 shorter events, 0.0 us)
Async XLA Ops:
  0.6 112.9 %copy-start.1 = (bf16[2,1,128,1024]{3,2,1,0:T(8,128)(2,1)S(1)}, bf16[2,1,128,1024]{3,2,1,0:T(8,128)(2,1)}, u32[]{:S(2)}) copy-start(bf16[2,1,128,1024]{3,2,1,0:T(8,128)(2,1)} %param.8) | copy-start | bytes 1572868
  0.6 48.2 %copy-start = (bf16[2,1,128,1024]{3,2,1,0:T(8,128)(2,1)S(1)}, bf16[2,1,128,1024]{3,2,1,0:T(8,128)(2,1)}, u32[]{:S(2)}) copy-start(bf16[2,1,128,1024]{3,2,1,0:T(8,128)(2,1)} %param.7) | copy-start | bytes 1572868
  0.7 10.3 %collective-permute-start.1 = (bf16[128,1024]{1,0:T(8,128)(2,1)}, bf16[128,1024]{1,0:T(8,128)(2,1)S(1)}, u32[]{:S(2)}, u32[]{:S(2)}) collective-permute-start(bf16[128,1024]{1,0:T(8,128)(2,1)} %own_ref.1), channel_id=1, source_target_pairs={{0,2},{1,3},{2,0},{3,1},{4,6},{5,7},{6,4},{7,5},{8,10},{9,11},{10,... | collective-permute-start | bytes 786440 | tf_op jit(solution)/shard_map/ppermute | solution.py:323
  10.9 1.0 copy-start.2
  11.9 36.9 %copy-start.3 = (bf16[128,1024]{1,0:T(8,128)(2,1)S(1)}, bf16[128,1024]{1,0:T(8,128)(2,1)}, u32[]{:S(2)}) copy-start(bf16[128,1024]{1,0:T(8,128)(2,1)} %own_ref.1) | copy-start | bytes 786436
  11.9 36.9 %copy-start.4 = (f32[7,1024]{1,0:T(8,128)S(1)}, f32[7,1024]{1,0:T(8,128)}, u32[]{:S(2)}) copy-start(f32[7,1024]{1,0:T(8,128)} %filter_ref.5) | copy-start | bytes 86020
  11.9 36.9 %collective-permute-start.2 = (bf16[256,1024]{1,0:T(8,128)(2,1)S(1)}, bf16[256,1024]{1,0:T(8,128)(2,1)S(1)}, u32[]{:S(2)}, u32[]{:S(2)}) collective-permute-start(bf16[256,1024]{1,0:T(8,128)(2,1)S(1)} %shard_map.103), channel_id=1, source_target_pairs={{0,1},{1,0},{2,3},{3,2},{4,5},{5,4},{6,7},{7,6},{8,9},{9,8},{10,11... | collective-permute-start | bytes 1572872 | tf_op jit(solution)/shard_map/ppermute | solution.py:323
  15.9 97.6 %copy-start.10 = (f32[2,1,128]{2,1,0:T(1,128)S(1)}, f32[2,1,128]{2,1,0:T(1,128)}, u32[]{:S(2)}) copy-start(f32[2,1,128]{2,1,0:T(1,128)} %get-tuple-element.37.tokens_ref) | copy-start | bytes 3076
  15.9 9.6 %collective-permute-start.3 = (bf16[2,8,1024]{2,1,0:T(8,128)(2,1)}, bf16[2,8,1024]{2,1,0:T(8,128)(2,1)S(1)}, u32[]{:S(2)}, u32[]{:S(2)}) collective-permute-start(bf16[2,8,1024]{2,1,0:T(8,128)(2,1)} %get-tuple-element.34), channel_id=1, source_target_pairs={{0,4},{4,8},{8,12},{12,16},{16,20},{20,24},{24,28},{28,32},{32,36}... | collective-permute-start | bytes 98312 | tf_op jit(solution)/shard_map/ppermute | solution.py:319
  19.4 7.9 %collective-permute-start.4 = (bf16[2,8,1024]{2,1,0:T(8,128)(2,1)}, bf16[2,8,1024]{2,1,0:T(8,128)(2,1)S(1)}, u32[]{:S(2)}, u32[]{:S(2)}) collective-permute-start(bf16[2,8,1024]{2,1,0:T(8,128)(2,1)} %get-tuple-element.41), channel_id=1, source_target_pairs={{4,0},{8,4},{12,8},{16,12},{20,16},{24,20},{28,24},{32,28},{36,32}... | collective-permute-start | bytes 98312 | tf_op jit(solution)/shard_map/ppermute | solution.py:319
  27.3 0.9 copy-start.5
  28.3 0.7 copy-start.9
  29.6 0.6 copy-start.6
  30.2 86.6 %collective-permute-start.5 = (bf16[144,1024]{1,0:T(8,128)(2,1)S(1)}, bf16[144,1024]{1,0:T(8,128)(2,1)S(1)}, u32[]{:S(2)}, u32[]{:S(2)}) collective-permute-start(bf16[144,1024]{1,0:T(8,128)(2,1)S(1)} %shard_map.106), channel_id=1, source_target_pairs={{0,508},{4,504},{8,500},{12,496},{16,492},{20,488},{24,484},{28,48... | collective-permute-start | bytes 884744 | tf_op jit(solution)/shard_map/ppermute | solution.py:314
  46.9 66.6 %collective-permute-start = (bf16[128,1024]{1,0:T(8,128)(2,1)}, bf16[128,1024]{1,0:T(8,128)(2,1)S(1)}, u32[]{:S(2)}, u32[]{:S(2)}) collective-permute-start(bf16[128,1024]{1,0:T(8,128)(2,1)} %get-tuple-element.33), channel_id=1, source_target_pairs={{0,508},{4,504},{8,500},{12,496},{16,492},{20,488},{24,484},{28,48... | collective-permute-start | bytes 786440 | tf_op jit(solution)/shard_map/ppermute | solution.py:314
  48.8 0.8 copy-start.7
  49.6 0.8 copy-start.8
  120.2 16.1 %collective-permute-start.6 = (bf16[144,1024]{1,0:T(8,128)(2,1)S(1)}, bf16[144,1024]{1,0:T(8,128)(2,1)S(1)}, u32[]{:S(2)}, u32[]{:S(2)}) collective-permute-start(bf16[144,1024]{1,0:T(8,128)(2,1)S(1)} %get-tuple-element.50), channel_id=1, source_target_pairs={{0,508},{4,504},{8,500},{12,496},{16,492},{20,488},{24,484},{28,48... | collective-permute-start | bytes 884744 | tf_op jit(solution)/shard_map/ppermute | solution.py:314
  137.4 3.9 %collective-permute-start.7 = (bf16[272,1024]{1,0:T(8,128)(2,1)S(1)}, bf16[272,1024]{1,0:T(8,128)(2,1)S(1)}, u32[]{:S(2)}, u32[]{:S(2)}) collective-permute-start(bf16[272,1024]{1,0:T(8,128)(2,1)S(1)} %get-tuple-element.54), channel_id=1, source_target_pairs={{0,1},{1,0},{2,3},{3,2},{4,5},{5,4},{6,7},{7,6},{8,9},{9,8},{10,11... | collective-permute-start | bytes 1671176 | tf_op jit(solution)/shard_map/ppermute | solution.py:323
  141.3 10.9 %collective-permute-start.8 = (bf16[144,1024]{1,0:T(8,128)(2,1)S(1)}, bf16[144,1024]{1,0:T(8,128)(2,1)S(1)}, u32[]{:S(2)}, u32[]{:S(2)}) collective-permute-start(bf16[144,1024]{1,0:T(8,128)(2,1)S(1)} %get-tuple-element.57), channel_id=1, source_target_pairs={{0,2},{1,3},{2,0},{3,1},{4,6},{5,7},{6,4},{7,5},{8,10},{9,11},{10,... | collective-permute-start | bytes 884744 | tf_op jit(solution)/shard_map/ppermute | solution.py:323

commit v7 on v6

--- a/solution.py
+++ b/solution.py
@@ -66,7 +66,7 @@
 
 
 def lead_kernel(
-    normed_ref, grad_ref, ids_ref, mask_ref, send_ref, tails_ref, heads_ref, far_ref, tokens_ref,
+    normed_ref, grad_ref, ids_ref, mask_ref, send_ref, tails_ref, heads_ref, far_ref, tokens_ref, rims_ref,
     head, ids, mask, arrived,
 ):
     rows, width = send_ref.shape
@@ -92,11 +92,19 @@
         tokens = token_row(ids, mask, strand)
         tokens_ref[strand] = tokens
         tokens = jnp.concatenate([tokens, jnp.zeros((1, width - LANES), F32)], axis=1)
-        heads_ref[strand] = jnp.where(at_row, tokens, head[strand].astype(F32)).astype(BF16)
-
-
-def pack_kernel(grad_ref, tokens_ref, tails_ref, heads_ref, slab_ref):
+        head_rows = jnp.where(at_row, tokens, head[strand].astype(F32)).astype(BF16)
+        heads_ref[strand] = head_rows
+        rims_ref[strand] = tails_ref[strand]
+        rims_ref[2 + strand] = head_rows
+
+
+def pack_kernel(
+    middle, shard_ref, grad_ref, tokens_ref, near_tails_ref, near_heads_ref, rims_ref, slab_ref, tails_ref, heads_ref,
+):
     rows, width = grad_ref.shape
+    for strand in range(2):
+        tails_ref[strand] = jnp.where(shard_ref[0] == middle, rims_ref[strand], near_tails_ref[strand])
+        heads_ref[strand] = jnp.where(shard_ref[0] == middle - 1, rims_ref[2 + strand], near_heads_ref[strand])
     head = heads_ref[1].astype(F32)
     swap = reversal(HALO, F32)
     tail_rev = jnp.dot(swap, tails_ref[1].astype(F32), preferred_element_type=F32).astype(BF16)
@@ -315,8 +323,10 @@
 
 
 def shifted(value, distance):
-    devices = range(lax.axis_size("ctx"))
-    return lax.ppermute(value, "ctx", [(i, i + distance) for i in devices if i + distance in devices])
+    size = lax.axis_size("ctx")
+    middle = {size // 2 - 1, size // 2}
+    pairs = [(i, i + distance) for i in range(size) if 0 <= i + distance < size and {i, i + distance} != middle]
+    return lax.ppermute(value, "ctx", pairs)
 
 
 def partner(value, bit):
@@ -335,7 +345,7 @@
     normed, out_grad = normed[:, 0], out_grad[:, 0]
     place = lax.axis_index("fsdp").astype(jnp.int32).reshape(1)
 
-    send, tails, heads, far_grad, tokens = pl.pallas_call(
+    send, tails, heads, far_grad, tokens, rims = pl.pallas_call(
         lead_kernel,
         out_shape=(
             shape((rows, width), BF16),
@@ -343,9 +353,10 @@
             shape((2, HALO, width), BF16),
             shape((rows, width), BF16),
             shape((2, 1, rows), F32),
+            shape((4, HALO, width), BF16),
         ),
         in_specs=[pl.BlockSpec(memory_space=pltpu.HBM)] * 4,
-        out_specs=[pl.BlockSpec(memory_space=pltpu.VMEM)] * 5,
+        out_specs=[pl.BlockSpec(memory_space=pltpu.VMEM)] * 6,
         scratch_shapes=[
             pltpu.VMEM((2, HALO, width), BF16),
             pltpu.VMEM((2, 1, rows), jnp.int32),
@@ -354,12 +365,17 @@
         ],
         cost_estimate=pl.CostEstimate(flops=0, bytes_accessed=4 * rows * width, transcendentals=0),
     )(normed, out_grad, ids, mask)
+    middle = lax.axis_size("ctx") // 2
+    shard_index = lax.axis_index("ctx").astype(jnp.int32).reshape(1)
+    rims = lax.ppermute(rims, "ctx", [(middle - 1, middle), (middle, middle - 1)])
     normed_far = mirrored(send)
     heads = shifted(heads, -1)
     tails = shifted(tails, 1)
     near = partner(proj_half, 2)
-    slab, = call(
-        pack_kernel, (shape((rows + 2 * HALO, width), BF16),), far_grad, tokens, tails, heads,
+    slab, tails, heads = call(
+        functools.partial(pack_kernel, middle),
+        (shape((rows + 2 * HALO, width), BF16), shape((2, HALO, width), BF16), shape((2, HALO, width), BF16)),
+        shard_index, far_grad, tokens, tails, heads, rims, scalars=1,
         flops=600 * rows * width, moved=4 * rows * width,
     )
     slab = mirrored(slab)

time: 154 us -> 155 us (level)
  the two profiles are of different devices: /device:TPU:4 before, /device:TPU:6 now
where the time goes in v7:
time: 155 us; the launch traced here: 154 us
  waiting for transfers between devices  85 us (55%)
  starting transfers between devices  47.6 us (31%)
  Pallas kernels  18.1 us (12%)
  local copies, waits for them, and re-layouts  2.61 us (2%)
    ppermute x3, waiting for transfers between devices, mirrored(): return lax.ppermute(value, 'ctx', [(i, size - 1 - i) for i in range(size)])  67.8 us
    ppermute x3, starting transfers between devices, mirrored(): return lax.ppermute(value, 'ctx', [(i, size - 1 - i) for i in range(size)])  27.9 us
    pallas_call x10, Pallas kernels, call(): pl.pallas_call(kernel, out_shape=out_shapes, in_specs=specs, out_specs=[p...  16.1 us
    ppermute x4, waiting for transfers between devices, partner(): lax.ppermute(value, 'fsdp', [(i, i ^ bit) for i in range(lax.axis_size('f...  15.3 us
    ppermute x4, starting transfers between devices, partner(): lax.ppermute(value, 'fsdp', [(i, i ^ bit) for i in range(lax.axis_size('f...  9.55 us
    ppermute x2, starting transfers between devices, shifted(): return lax.ppermute(value, 'ctx', pairs)  9.46 us
  transfers between devices with their start and end apart: 10, of which 7 were waited for; matrix products, arithmetic and copies ran while one was open for 0% of the time, Pallas kernels for 8%

profile of v7, /device:TPU:6, one launch (start us, length us, event | category | flops | bytes accessed | tf_op | source)
XLA Modules:
  0.0 154.1 jit_solution(11873259520186927480)
XLA Ops:
  0.6 0.0 copy-start.1
  0.6 0.0 copy-start
  0.7 2.9 %collective-permute-start.1 = (bf16[128,1024]{1,0:T(8,128)(2,1)}, bf16[128,1024]{1,0:T(8,128)(2,1)S(1)}, u32[]{:S(2)}, u32[]{:S(2)}) collective-permute-start(bf16[128,1024]{1,0:T(8,128)(2,1)} %own_ref.1), channel_id=1, source_target_pairs={{0,2},{1,3},{2,0},{3,1},{4,6},{5,7},{6,4},{7,5},{8,10},{9,11},{10,... | collective-permute-start | bytes 786440 | tf_op jit(solution)/shard_map/ppermute | solution.py:333
  3.5 7.4 %collective-permute-done.1.second_ref.near_ref = bf16[128,1024]{1,0:T(8,128)(2,1)S(1)} collective-permute-done((bf16[128,1024]{1,0:T(8,128)(2,1)}, bf16[128,1024]{1,0:T(8,128)(2,1)S(1)}, u32[]{:S(2)}, u32[]{:S(2)}) %collective-permute-start.1) | collective-permute-done | bytes 262176 | tf_op jit(solution)/shard_map/ppermute | solution.py:333
  10.9 0.0 copy-start.2
  10.9 0.9 copy-done.2
  11.9 0.0 copy-start.3
  11.9 0.0 copy-start.4
  11.9 0.0 copy-start.6
  11.9 2.1 %collective-permute-start.2 = (bf16[256,1024]{1,0:T(8,128)(2,1)S(1)}, bf16[256,1024]{1,0:T(8,128)(2,1)S(1)}, u32[]{:S(2)}, u32[]{:S(2)}) collective-permute-start(bf16[256,1024]{1,0:T(8,128)(2,1)S(1)} %shard_map.103), channel_id=1, source_target_pairs={{0,1},{1,0},{2,3},{3,2},{4,5},{5,4},{6,7},{7,6},{8,9},{9,8},{10,11... | collective-permute-start | bytes 1572872 | tf_op jit(solution)/shard_map/ppermute | solution.py:333
  14.0 1.9 %shard_map.102 = (bf16[128,1024]{1,0:T(8,128)(2,1)}, bf16[2,8,1024]{2,1,0:T(8,128)(2,1)}, bf16[2,8,1024]{2,1,0:T(8,128)(2,1)}, bf16[128,1024]{1,0:T(8,128)(2,1)}...) custom-call(bf16[2,128,1024]{2,1,0:T(8,128)(2,1)} %bitcast.10, bf16[2,128,1024]{2,1,0:T(8,128)(2,1)} %bitcast.13, ...), custom_call_target="tpu_custom_call" | custom-call | bytes 524288 | tf_op jit(solution)/shard_map/pallas_call | solution.py:348
  15.9 0.0 copy-start.8
  16.0 0.7 collective-permute-start.5
  16.6 3.5 %collective-permute-start.3 = (bf16[2,8,1024]{2,1,0:T(8,128)(2,1)}, bf16[2,8,1024]{2,1,0:T(8,128)(2,1)S(1)}, u32[]{:S(2)}, u32[]{:S(2)}) collective-permute-start(bf16[2,8,1024]{2,1,0:T(8,128)(2,1)} %get-tuple-element.40), channel_id=1, source_target_pairs={{0,4},{4,8},{8,12},{12,16},{16,20},{20,24},{24,28},{28,32},{32,36}... | collective-permute-start | bytes 98312 | tf_op jit(solution)/shard_map/ppermute | solution.py:329
  20.1 6.0 %collective-permute-start.4 = (bf16[2,8,1024]{2,1,0:T(8,128)(2,1)}, bf16[2,8,1024]{2,1,0:T(8,128)(2,1)S(1)}, u32[]{:S(2)}, u32[]{:S(2)}) collective-permute-start(bf16[2,8,1024]{2,1,0:T(8,128)(2,1)} %get-tuple-element.41), channel_id=1, source_target_pairs={{4,0},{8,4},{12,8},{16,12},{20,16},{24,20},{28,24},{32,28},{36,32}... | collective-permute-start | bytes 98312 | tf_op jit(solution)/shard_map/ppermute | solution.py:329
  26.1 0.2 collective-permute-done.3.near_tails_ref
  26.3 1.7 %collective-permute-done.4.near_heads_ref = bf16[2,8,1024]{2,1,0:T(8,128)(2,1)S(1)} collective-permute-done((bf16[2,8,1024]{2,1,0:T(8,128)(2,1)}, bf16[2,8,1024]{2,1,0:T(8,128)(2,1)S(1)}, u32[]{:S(2)}, u32[]{:S(2)}) %collective-permute-start.4) | collective-permute-done | bytes 32800 | tf_op jit(solution)/shard_map/ppermute | solution.py:329
  28.0 0.0 collective-permute-done.5.rims_ref
  28.0 0.0 copy-start.5
  28.0 0.9 copy-done.5
  28.9 0.0 copy-start.7
  28.9 0.7 copy-done.7
  29.6 1.4 shard_map.104
  31.0 16.6 %collective-permute-start.6 = (bf16[144,1024]{1,0:T(8,128)(2,1)}, bf16[144,1024]{1,0:T(8,128)(2,1)S(1)}, u32[]{:S(2)}, u32[]{:S(2)}) collective-permute-start(bf16[144,1024]{1,0:T(8,128)(2,1)} %get-tuple-element.48), channel_id=1, source_target_pairs={{0,508},{4,504},{8,500},{12,496},{16,492},{20,488},{24,484},{28,48... | collective-permute-start | bytes 884744 | tf_op jit(solution)/shard_map/ppermute | solution.py:322
  47.7 1.9 %collective-permute-start = (bf16[128,1024]{1,0:T(8,128)(2,1)}, bf16[128,1024]{1,0:T(8,128)(2,1)S(1)}, u32[]{:S(2)}, u32[]{:S(2)}) collective-permute-start(bf16[128,1024]{1,0:T(8,128)(2,1)} %get-tuple-element.37), channel_id=1, source_target_pairs={{0,508},{4,504},{8,500},{12,496},{16,492},{20,488},{24,484},{28,48... | collective-permute-start | bytes 786440 | tf_op jit(solution)/shard_map/ppermute | solution.py:322
  49.6 0.0 collective-permute-done.2.other_ref
  49.6 0.0 copy-done
  49.6 0.0 copy-done.3
  49.6 0.0 copy-done.4
  49.6 0.0 copy-done.6
  49.6 2.6 %shard_map.105 = (bf16[1024,1024]{1,0:T(8,128)(2,1)S(1)}, f32[136,1024]{1,0:T(8,128)S(1)}, f32[8,1024]{1,0:T(8,128)S(1)}, f32[8,1024]{1,0:T(8,128)S(1)}, f32[8,1024]{1,0:T(8,128)S(1)}) custom-call(s32[1]{0:T(128)} %bitcast.place_ref, bf16[128,1024]{1,0:T(8,128)(2,1)S(1)} %copy-done.3, bf16[128,1024]{1,0:T(8,128)(2,1)S(1)} %collective-permute-done.1.second_ref.near_ref, ...), custom_call_target="tpu_custom_call" | custom-call | flops 268435456 | bytes 6291456 | tf_op jit(solution)/shard_map/pallas_call | solution.py:53
  52.2 62.2 %collective-permute-done.far_ref = bf16[128,1024]{1,0:T(8,128)(2,1)S(1)} collective-permute-done((bf16[128,1024]{1,0:T(8,128)(2,1)}, bf16[128,1024]{1,0:T(8,128)(2,1)S(1)}, u32[]{:S(2)}, u32[]{:S(2)}) %collective-permute-start) | collective-permute-done | bytes 262176 | tf_op jit(solution)/shard_map/ppermute | solution.py:322
  114.5 0.0 copy-done.1
  114.5 0.0 copy-done.8
  114.5 3.3 %shard_map.106 = (f32[128,1024]{1,0:T(8,128)S(1)}, f32[128,1024]{1,0:T(8,128)S(1)}, bf16[128,1024]{1,0:T(8,128)(2,1)S(1)}, f32[16,1024]{1,0:T(8,128)S(1)}) custom-call(bf16[128,1024]{1,0:T(8,128)(2,1)S(1)} %collective-permute-done.far_ref, bf16[1024,1024]{1,0:T(8,128)(2,1)S(1)} %get-tuple-element.44.weight_ref, ...), custom_call_target="tpu_custom_call" | custom-call | flops 268435456 | bytes 8388608 | tf_op jit(solution)/shard_map/pallas_call | solution.py:53
  117.8 0.0 collective-permute-done.6.slab_ref
  117.8 3.3 %shard_map.107 = (bf16[144,1024]{1,0:T(8,128)(2,1)S(1)}, bf16[128,1024]{1,0:T(8,128)(2,1)S(1)}, f32[8,1024]{1,0:T(8,128)S(1)}) custom-call(bf16[144,1024]{1,0:T(8,128)(2,1)S(1)} %collective-permute-done.6.slab_ref, bf16[1024,1024]{1,0:T(8,128)(2,1)S(1)} %get-tuple-element.44.weight_ref, f32[136,1024]{1,0:T(8,128)S(1)} %get-tuple-element.45.values0_ref, ...), custom_call_target="tpu_custom_call" | custom-call | flops 268435456 | bytes 8388608 | tf_op jit(solution)/shard_map/pallas_call | solution.py:53
  121.1 9.4 %collective-permute-start.7 = (bf16[144,1024]{1,0:T(8,128)(2,1)S(1)}, bf16[144,1024]{1,0:T(8,128)(2,1)S(1)}, u32[]{:S(2)}, u32[]{:S(2)}) collective-permute-start(bf16[144,1024]{1,0:T(8,128)(2,1)S(1)} %get-tuple-element.58), channel_id=1, source_target_pairs={{0,508},{4,504},{8,500},{12,496},{16,492},{20,488},{24,484},{28,48... | collective-permute-start | bytes 884744 | tf_op jit(solution)/shard_map/ppermute | solution.py:322
  130.5 1.2 shard_map.108
  131.7 5.6 %collective-permute-done.7.refs_2_ = bf16[144,1024]{1,0:T(8,128)(2,1)S(1)} collective-permute-done((bf16[144,1024]{1,0:T(8,128)(2,1)S(1)}, bf16[144,1024]{1,0:T(8,128)(2,1)S(1)}, u32[]{:S(2)}, u32[]{:S(2)}) %collective-permute-start.7) | collective-permute-done | bytes 294944 | tf_op jit(solution)/shard_map/ppermute | solution.py:322
  137.2 1.1 shard_map.109
  138.3 1.9 %collective-permute-start.8 = (bf16[272,1024]{1,0:T(8,128)(2,1)S(1)}, bf16[272,1024]{1,0:T(8,128)(2,1)S(1)}, u32[]{:S(2)}, u32[]{:S(2)}) collective-permute-start(bf16[272,1024]{1,0:T(8,128)(2,1)S(1)} %get-tuple-element.62), channel_id=1, source_target_pairs={{0,1},{1,0},{2,3},{3,2},{4,5},{5,4},{6,7},{7,6},{8,9},{9,8},{10,11... | collective-permute-start | bytes 1671176 | tf_op jit(solution)/shard_map/ppermute | solution.py:333
  140.3 1.9 %collective-permute-done.8.got_ref = bf16[272,1024]{1,0:T(8,128)(2,1)S(1)} collective-permute-done((bf16[272,1024]{1,0:T(8,128)(2,1)S(1)}, bf16[272,1024]{1,0:T(8,128)(2,1)S(1)}, u32[]{:S(2)}, u32[]{:S(2)}) %collective-permute-start.8) | collective-permute-done | bytes 557088 | tf_op jit(solution)/shard_map/ppermute | solution.py:333
  142.2 0.1 shard_map.111
  142.3 2.7 %collective-permute-start.9 = (bf16[144,1024]{1,0:T(8,128)(2,1)S(1)}, bf16[144,1024]{1,0:T(8,128)(2,1)S(1)}, u32[]{:S(2)}, u32[]{:S(2)}) collective-permute-start(bf16[144,1024]{1,0:T(8,128)(2,1)S(1)} %get-tuple-element.65), channel_id=1, source_target_pairs={{0,2},{1,3},{2,0},{3,1},{4,6},{5,7},{6,4},{7,5},{8,10},{9,11},{10,... | collective-permute-start | bytes 884744 | tf_op jit(solution)/shard_map/ppermute | solution.py:333
  145.0 2.3 %shard_map.110 = bf16[2,128,1024]{2,1,0:T(8,128)(2,1)} custom-call(bf16[2,128,1024]{2,1,0:T(8,128)(2,1)S(1)} %get-tuple-element.60.value_grad_ref, bf16[1024,1024]{1,0:T(8,128)(2,1)S(1)} %get-tuple-element.44.weight_ref), custom_call_target="tpu_custom_call" | custom-call | flops 536870912 | bytes 4194304 | tf_op jit(solution)/shard_map/pallas_call | solution.py:53
  147.3 5.9 %collective-permute-done.9.got_ref = bf16[144,1024]{1,0:T(8,128)(2,1)S(1)} collective-permute-done((bf16[144,1024]{1,0:T(8,128)(2,1)S(1)}, bf16[144,1024]{1,0:T(8,128)(2,1)S(1)}, u32[]{:S(2)}, u32[]{:S(2)}) %collective-permute-start.9) | collective-permute-done | bytes 294944 | tf_op jit(solution)/shard_map/ppermute | solution.py:333
  153.2 0.8 shard_map.112
  (1 shorter events, 0.0 us)
Async XLA Ops:
  0.6 113.9 %copy-start.1 = (bf16[2,1,128,1024]{3,2,1,0:T(8,128)(2,1)S(1)}, bf16[2,1,128,1024]{3,2,1,0:T(8,128)(2,1)}, u32[]{:S(2)}) copy-start(bf16[2,1,128,1024]{3,2,1,0:T(8,128)(2,1)} %param.8) | copy-start | bytes 1572868
  0.6 49.0 %copy-start = (bf16[2,1,128,1024]{3,2,1,0:T(8,128)(2,1)S(1)}, bf16[2,1,128,1024]{3,2,1,0:T(8,128)(2,1)}, u32[]{:S(2)}) copy-start(bf16[2,1,128,1024]{3,2,1,0:T(8,128)(2,1)} %param.7) | copy-start | bytes 1572868
  0.7 10.3 %collective-permute-start.1 = (bf16[128,1024]{1,0:T(8,128)(2,1)}, bf16[128,1024]{1,0:T(8,128)(2,1)S(1)}, u32[]{:S(2)}, u32[]{:S(2)}) collective-permute-start(bf16[128,1024]{1,0:T(8,128)(2,1)} %own_ref.1), channel_id=1, source_target_pairs={{0,2},{1,3},{2,0},{3,1},{4,6},{5,7},{6,4},{7,5},{8,10},{9,11},{10,... | collective-permute-start | bytes 786440 | tf_op jit(solution)/shard_map/ppermute | solution.py:333
  10.9 1.0 copy-start.2
  11.9 37.7 %copy-start.3 = (bf16[128,1024]{1,0:T(8,128)(2,1)S(1)}, bf16[128,1024]{1,0:T(8,128)(2,1)}, u32[]{:S(2)}) copy-start(bf16[128,1024]{1,0:T(8,128)(2,1)} %own_ref.1) | copy-start | bytes 786436
  11.9 37.7 %copy-start.4 = (f32[7,1024]{1,0:T(8,128)S(1)}, f32[7,1024]{1,0:T(8,128)}, u32[]{:S(2)}) copy-start(f32[7,1024]{1,0:T(8,128)} %filter_ref.5) | copy-start | bytes 86020
  11.9 37.7 %copy-start.6 = (f32[6,1024]{1,0:T(8,128)S(1)}, f32[6,1024]{1,0:T(8,128)}, u32[]{:S(2)}) copy-start(f32[6,1024]{1,0:T(8,128)} %bias_ref.1) | copy-start | bytes 73732
  11.9 37.7 %collective-permute-start.2 = (bf16[256,1024]{1,0:T(8,128)(2,1)S(1)}, bf16[256,1024]{1,0:T(8,128)(2,1)S(1)}, u32[]{:S(2)}, u32[]{:S(2)}) collective-permute-start(bf16[256,1024]{1,0:T(8,128)(2,1)S(1)} %shard_map.103), channel_id=1, source_target_pairs={{0,1},{1,0},{2,3},{3,2},{4,5},{5,4},{6,7},{7,6},{8,9},{9,8},{10,11... | collective-permute-start | bytes 1572872 | tf_op jit(solution)/shard_map/ppermute | solution.py:333
  15.9 98.5 %copy-start.8 = (f32[2,1,128]{2,1,0:T(1,128)S(1)}, f32[2,1,128]{2,1,0:T(1,128)}, u32[]{:S(2)}) copy-start(f32[2,1,128]{2,1,0:T(1,128)} %get-tuple-element.39.tokens_ref) | copy-start | bytes 3076
  16.0 12.0 %collective-permute-start.5 = (bf16[4,8,1024]{2,1,0:T(8,128)(2,1)}, bf16[4,8,1024]{2,1,0:T(8,128)(2,1)S(1)}, u32[]{:S(2)}, u32[]{:S(2)}) collective-permute-start(bf16[4,8,1024]{2,1,0:T(8,128)(2,1)} %get-tuple-element.42), channel_id=1, source_target_pairs={{252,256},{256,252},{253,257},{257,253},{254,258},{258,254},{255,2... | collective-permute-start | bytes 196616 | tf_op jit(solution)/shard_map/ppermute | solution.py:370
  16.6 9.6 %collective-permute-start.3 = (bf16[2,8,1024]{2,1,0:T(8,128)(2,1)}, bf16[2,8,1024]{2,1,0:T(8,128)(2,1)S(1)}, u32[]{:S(2)}, u32[]{:S(2)}) collective-permute-start(bf16[2,8,1024]{2,1,0:T(8,128)(2,1)} %get-tuple-element.40), channel_id=1, source_target_pairs={{0,4},{4,8},{8,12},{12,16},{16,20},{20,24},{24,28},{28,32},{32,36}... | collective-permute-start | bytes 98312 | tf_op jit(solution)/shard_map/ppermute | solution.py:329
  20.1 7.9 %collective-permute-start.4 = (bf16[2,8,1024]{2,1,0:T(8,128)(2,1)}, bf16[2,8,1024]{2,1,0:T(8,128)(2,1)S(1)}, u32[]{:S(2)}, u32[]{:S(2)}) collective-permute-start(bf16[2,8,1024]{2,1,0:T(8,128)(2,1)} %get-tuple-element.41), channel_id=1, source_target_pairs={{4,0},{8,4},{12,8},{16,12},{20,16},{24,20},{28,24},{32,28},{36,32}... | collective-permute-start | bytes 98312 | tf_op jit(solution)/shard_map/ppermute | solution.py:329
  28.0 1.0 copy-start.5
  28.9 0.7 copy-start.7
  31.0 86.8 %collective-permute-start.6 = (bf16[144,1024]{1,0:T(8,128)(2,1)}, bf16[144,1024]{1,0:T(8,128)(2,1)S(1)}, u32[]{:S(2)}, u32[]{:S(2)}) collective-permute-start(bf16[144,1024]{1,0:T(8,128)(2,1)} %get-tuple-element.48), channel_id=1, source_target_pairs={{0,508},{4,504},{8,500},{12,496},{16,492},{20,488},{24,484},{28,48... | collective-permute-start | bytes 884744 | tf_op jit(solution)/shard_map/ppermute | solution.py:322
  47.7 66.8 %collective-permute-start = (bf16[128,1024]{1,0:T(8,128)(2,1)}, bf16[128,1024]{1,0:T(8,128)(2,1)S(1)}, u32[]{:S(2)}, u32[]{:S(2)}) collective-permute-start(bf16[128,1024]{1,0:T(8,128)(2,1)} %get-tuple-element.37), channel_id=1, source_target_pairs={{0,508},{4,504},{8,500},{12,496},{16,492},{20,488},{24,484},{28,48... | collective-permute-start | bytes 786440 | tf_op jit(solution)/shard_map/ppermute | solution.py:322
  121.1 16.1 %collective-permute-start.7 = (bf16[144,1024]{1,0:T(8,128)(2,1)S(1)}, bf16[144,1024]{1,0:T(8,128)(2,1)S(1)}, u32[]{:S(2)}, u32[]{:S(2)}) collective-permute-start(bf16[144,1024]{1,0:T(8,128)(2,1)S(1)} %get-tuple-element.58), channel_id=1, source_target_pairs={{0,508},{4,504},{8,500},{12,496},{16,492},{20,488},{24,484},{28,48... | collective-permute-start | bytes 884744 | tf_op jit(solution)/shard_map/ppermute | solution.py:322
  138.3 3.9 %collective-permute-start.8 = (bf16[272,1024]{1,0:T(8,128)(2,1)S(1)}, bf16[272,1024]{1,0:T(8,128)(2,1)S(1)}, u32[]{:S(2)}, u32[]{:S(2)}) collective-permute-start(bf16[272,1024]{1,0:T(8,128)(2,1)S(1)} %get-tuple-element.62), channel_id=1, source_target_pairs={{0,1},{1,0},{2,3},{3,2},{4,5},{5,4},{6,7},{7,6},{8,9},{9,8},{10,11... | collective-permute-start | bytes 1671176 | tf_op jit(solution)/shard_map/ppermute | solution.py:333
  142.3 10.9 %collective-permute-start.9 = (bf16[144,1024]{1,0:T(8,128)(2,1)S(1)}, bf16[144,1024]{1,0:T(8,128)(2,1)S(1)}, u32[]{:S(2)}, u32[]{:S(2)}) collective-permute-start(bf16[144,1024]{1,0:T(8,128)(2,1)S(1)} %get-tuple-element.65), channel_id=1, source_target_pairs={{0,2},{1,3},{2,0},{3,1},{4,6},{5,7},{6,4},{7,5},{8,10},{9,11},{10,... | collective-permute-start | bytes 884744 | tf_op jit(solution)/shard_map/ppermute | solution.py:333
